TPU v7x, 256 devices: a whole 4x4x8 slice. The times are simulated.
256 devices in a mesh: patch: 64 (over z, x, core), band: 4 (over y).
Axes of the slice: x: 4, y: 4, z: 8, core: 2. Of those that a mesh axis runs over, the one named last changes fastest.
Arguments:
- exposures: bfloat16 [2048, 4, 128, 128], P('patch', 'band'), may hold values from -6 to 6
- psf_taps: bfloat16 [2048, 4, 2, 7], P('patch', 'band'), may hold values from -0.15 to 1, as said below
- warp_rows: bfloat16 [2048, 4, 128, 128], P('patch', 'band'), may hold values from -0.2 to 1, as said below
- warp_cols: bfloat16 [2048, 4, 128, 128], P('patch', 'band'), may hold values from -0.2 to 1, as said below
- routes: int32 [4, 2048, 1], P('band'), may hold values from 0 to 63; in each aligned block of 32 rows (0 to 31, 32 to 63, ..., all dimensions but the last counted through in order) at most 2 rows name the same one
- offsets: int32 [4, 2048, 2], P('band'), may hold values from 0 to 384
- weights: float32 [4, 2048], P('band'), may hold values from 0.1 to 2
- det_weight: bfloat16 [64, 100], replicated, may hold values from -0.625 to 0.625
- det_bias: float32 [64], replicated, may hold values from -3 to 3
Outputs:
- coadd: bfloat16 [64, 4, 512, 512], P('patch', 'band')
- detection: bfloat16 [64, 64, 512, 512], P('patch', None, 'band')
Inputs may be any that keep to these rules, and one draw needn't show every extreme that they name: `routes`: in each aligned block of 32 tiles of a band (the tiles of one device) no patch is named more than 2 times; over all bands together every patch is named by some tile. `psf_taps`: the centre tap (index 3) lies between 0.6 and 1.0, the others between -0.15 and 0.15. `warp_rows`: Lanczos-3 resampling matrices. `warp_cols`: Lanczos-3 resampling matrices.
All inputs are finite; a program needn't handle non-finite values.
Results may differ from a plain program's by a relative error of at most 0.007.
Values may be sent and summed in bfloat16 or wider, within the bound.
No kernel may reach another device: no remote copies, remote signals or barrier semaphores. Data moves between devices by JAX's collectives and lax.ppermute only.
A program may use at most 128 MiB of HBM per device.

v0:
```python
import math

import jax
import jax.numpy as jnp
from jax import lax
from jax.sharding import PartitionSpec as P

PS = 512


def extended(shard, sides, width):
    for axis, dim in sides:
        size, length = (lax.axis_size(axis), shard.shape[dim])
        up = [(i, (i + 1) % size) for i in range(size - 1)]
        down = [(j, i) for i, j in up]
        last = lax.slice_in_dim(shard, length - width, length, axis=dim)
        first = lax.slice_in_dim(shard, 0, width, axis=dim)
        before = lax.ppermute(last, axis, up)
        after = lax.ppermute(first, axis, down)
        shard = jnp.concatenate([before, shard, after], axis=dim)
    return shard


def band_matrix(taps, tile_side):
    across = jnp.arange(tile_side)
    offset_diag = across[None, :] - across[:, None] + taps.shape[-1] // 2
    result = jnp.zeros((taps.shape[0], tile_side, tile_side), taps.dtype)
    for tap_index in range(taps.shape[-1]):
        result = result + jnp.where(
            (offset_diag == tap_index)[None],
            taps[:, tap_index, None, None],
            jnp.zeros((), taps.dtype),
        )
    return result


def psf_match(tile_data, taps):
    tile_side = tile_data.shape[1]
    psf_rows = band_matrix(taps[:, 0], tile_side)
    psf_cols = band_matrix(taps[:, 1], tile_side)
    half_done = jnp.einsum(
        "eij,ekj->eik", tile_data, psf_cols, preferred_element_type=jnp.float32
    ).astype(jnp.bfloat16)
    return jnp.einsum(
        "eij,ejk->eik", psf_rows, half_done, preferred_element_type=jnp.float32
    ).astype(jnp.bfloat16)


def apply_warp(matched, rows_warp, cols_warp, tile_weight):
    across_cols = jnp.einsum(
        "eij,ekj->eik", matched, cols_warp, preferred_element_type=jnp.float32
    ).astype(jnp.bfloat16)
    product = jnp.einsum("eij,ejk->eik", rows_warp, across_cols, preferred_element_type=jnp.float32)
    return (tile_weight[:, None, None] * product).astype(jnp.bfloat16)


def slot_select(targets, capacity):
    counts = jnp.cumsum(targets.astype(jnp.int32), axis=1) - 1
    slot_ids = jnp.arange(capacity, dtype=jnp.int32)
    return targets[:, None, :] & (counts[:, None, :] == slot_ids[None, :, None])


def body(exposures, psf_taps, warp_rows, warp_cols, routes, offsets, weights, det_weight, det_bias):
    npatch = lax.axis_size("patch")
    nband = lax.axis_size("band")
    e_dev = exposures.shape[0]
    tile_side = exposures.shape[2]
    capacity = max(2, 2 * e_dev // npatch)
    owner = lax.axis_index("patch")
    tile_data = exposures[:, 0]
    taps = psf_taps[:, 0]
    rows_warp = warp_rows[:, 0]
    cols_warp = warp_cols[:, 0]
    dest_all = routes[0, :, 0].reshape(npatch, e_dev)
    corner_all = offsets[0].reshape(npatch, e_dev, 2)
    weight_all = weights[0].reshape(npatch, e_dev)
    own_dest = lax.dynamic_index_in_dim(dest_all, owner, 0, keepdims=False)
    own_weights = lax.dynamic_index_in_dim(weight_all, owner, 0, keepdims=False)
    outgoing = own_dest[None, :] == jnp.arange(npatch, dtype=jnp.int32)[:, None]
    chosen = slot_select(outgoing, capacity).astype(jnp.bfloat16)
    arriving = dest_all == owner
    landed = slot_select(arriving, capacity)
    landed_int = landed.astype(jnp.int32)
    slot_rows = jnp.sum(landed_int * corner_all[:, None, :, 0], axis=-1).reshape(-1)
    slot_cols = jnp.sum(landed_int * corner_all[:, None, :, 1], axis=-1).reshape(-1)
    slot_weights = jnp.sum(jnp.where(landed, weight_all[:, None, :], 0.0), axis=-1).reshape(-1)
    slots = npatch * capacity
    matched = psf_match(tile_data, taps)
    warped = apply_warp(matched, rows_warp, cols_warp, own_weights)
    received = lax.all_to_all(
        jnp.einsum("nce,eij->ncij", chosen, warped, preferred_element_type=jnp.float32).astype(
            jnp.bfloat16
        ),
        "patch",
        split_axis=0,
        concat_axis=0,
        tiled=True,
    )
    incoming = received.reshape(slots, tile_side, tile_side)
    block_slots = math.gcd(slots, 16)
    block_count = slots // block_slots
    tile_rows_b = incoming.reshape(block_count, block_slots, tile_side, tile_side)
    rows_b = slot_rows.reshape(block_count, block_slots)
    cols_b = slot_cols.reshape(block_count, block_slots)
    weights_b = slot_weights.reshape(block_count, block_slots)
    inside = jnp.arange(tile_side, dtype=jnp.int32)
    pixels = jnp.arange(PS, dtype=jnp.int32)

    def place_block(block_index, totals):
        flux_total, cover_total = totals
        block_tiles = tile_rows_b[block_index]
        row_start = rows_b[block_index]
        col_start = cols_b[block_index]
        block_weight = weights_b[block_index]
        row_table = pixels[None, None, :] == row_start[:, None, None] + inside[None, :, None]
        col_table = pixels[None, None, :] == col_start[:, None, None] + inside[None, :, None]
        placed_cols = jnp.einsum(
            "kij,kjx->kix",
            block_tiles,
            col_table.astype(jnp.bfloat16),
            preferred_element_type=jnp.float32,
        ).astype(jnp.bfloat16)
        flux_total = flux_total + jnp.einsum(
            "kiy,kix->yx",
            row_table.astype(jnp.bfloat16),
            placed_cols,
            preferred_element_type=jnp.float32,
        )
        row_cover = jnp.sum(row_table.astype(jnp.float32), axis=1) * block_weight[:, None]
        col_cover = jnp.sum(col_table.astype(jnp.float32), axis=1)
        cover_total = cover_total + jnp.einsum(
            "ky,kx->yx", row_cover, col_cover, precision=lax.Precision.HIGHEST
        )
        return (flux_total, cover_total)

    start = (jnp.zeros((PS, PS), jnp.float32), jnp.zeros((PS, PS), jnp.float32))
    flux_sum, coverage = lax.fori_loop(0, block_count, place_block, start)
    coadd = (flux_sum / jnp.maximum(coverage, 1.0)).astype(jnp.bfloat16)
    strip_rows = PS // nband
    strips = lax.all_to_all(
        coadd.reshape(nband, strip_rows, PS), "band", split_axis=0, concat_axis=0, tiled=True
    )
    framed = extended(strips, (("band", 1),), 2)
    wide = jnp.pad(framed, ((0, 0), (0, 0), (2, 2)))
    features = jnp.stack(
        [
            wide[:, row_shift : row_shift + strip_rows, col_shift : col_shift + PS]
            for row_shift in range(5)
            for col_shift in range(5)
        ],
        axis=1,
    )
    features = features.reshape(nband * 25, strip_rows * PS)
    detection = (
        jnp.dot(det_weight, features, preferred_element_type=jnp.float32) + det_bias[:, None]
    )
    detection = detection.reshape(det_weight.shape[0], strip_rows, PS).astype(jnp.bfloat16)
    return (coadd[None, None], detection[None])


def solution(mesh):
    placed = (
        P("patch", "band", None, None),
        P("patch", "band", None, None),
        P("patch", "band", None, None),
        P("patch", "band", None, None),
        P("band", None, None),
        P("band", None, None),
        P("band", None),
        P(),
        P(),
    )
    return jax.shard_map(
        body,
        mesh=mesh,
        in_specs=placed,
        out_specs=(P("patch", "band", None, None), P("patch", None, "band", None)),
        check_vma=False,
    )
```

profile of v0, /device:TPU:32, one launch (start us, length us, event | category | flops | bytes accessed | tf_op | source)
XLA Modules:
  0.0 244.3 jit_solution(6917586174469735215)
XLA Ops:
  0.8 0.8 copy.117
  1.6 0.5 broadcast.265
  2.1 1.4 reduce.7
  3.6 2.7 %convolution_convert_fusion.2 = bf16[32,128,128]{2,1,0:T(8,128)(2,1)} fusion(bf16[32,1,128,128]{3,2,1,0:T(8,128)(2,1)S(1)} %copy-done, pred[128,128]{1,0:T(8,128)(4,1)S(1)} %get-tuple-element.267, pred[128,128]{1,0:T(8,128)(4,1)S(1)} %get-tuple-element.268, pred[128,128]{1,0:T(8,128)(4,1)S(1)} %get-tuple-element.269, ...), kind=kOutput, calls=%fused_computation.36 | convolution fusion | flops 283115520 | bytes 2212736 | tf_op jit(solution)/shard_map/eij,ejk->eik/dot_general | solution.py:44
  6.3 3.1 %fusion.33 = bf16[32,128,128]{1,2,0:T(8,128)(2,1)S(1)} fusion(bf16[32,128,128]{2,1,0:T(8,128)(2,1)} %convolution_convert_fusion.2, bf16[32,1,128,128]{3,2,1,0:T(8,128)(2,1)S(1)} %copy-done.3, bf16[32,1,128,128]{3,2,1,0:T(8,128)(2,1)} %param.14, f32[32]{0:T(128)S(1)} %dynamic-slice_bitcast_fusion), kind=kOutput, calls=%fused_computation.39 | convolution fusion | flops 270008320 | bytes 4194432 | tf_op jit(solution)/shard_map/eij,ejk->eik/dot_general | solution.py:53
  9.4 1.0 copy.81
  10.4 0.5 broadcast.264
  10.9 0.7 reduce.6
  12.1 1.3 convolution_convert_fusion
  13.4 4.7 %copy.82 = bf16[64,2,128,128]{3,2,1,0:T(8,128)(2,1)} copy(bf16[64,2,128,128]{3,0,2,1:T(8,128)(2,1)S(1)} %convolution_convert_fusion) | data formatting | bytes 8388608 | tf_op jit(solution)/shard_map/convert_element_type | solution.py:91
  18.1 11.8 %all-to-all-start = ((bf16[64,2,128,128]{3,2,1,0:T(8,128)(2,1)}), bf16[64,2,128,128]{3,2,1,0:T(8,128)(2,1)}, u32[]{:S(2)}, u32[]{:S(2)}) async-start(bf16[64,2,128,128]{3,2,1,0:T(8,128)(2,1)} %copy.82), calls=%async_computation | async-start | bytes 8388608 | tf_op jit(solution)/shard_map/all_to_all | solution.py:90
  31.2 93.9 %all-to-all-done = bf16[64,2,128,128]{3,2,1,0:T(8,128)(2,1)} async-done(((bf16[64,2,128,128]{3,2,1,0:T(8,128)(2,1)}), bf16[64,2,128,128]{3,2,1,0:T(8,128)(2,1)}, u32[]{:S(2)}, u32[]{:S(2)}) %all-to-all-start) | async-done | bytes 4194336 | tf_op jit(solution)/shard_map/all_to_all | solution.py:90
  125.2 50.5 %while.17 = (s32[]{:T(128)}, f32[512,512]{1,0:T(8,128)S(1)}, f32[512,512]{1,0:T(8,128)S(1)}, s32[8,16]{1,0:T(8,128)S(1)}, bf16[8,16,128,128]{3,2,1,0:T(8,128)(2,...) while((s32[]{:T(128)}, f32[512,512]{1,0:T(8,128)S(1)}, ...), condition=%wide.region_8.9_spmd.clone.clone, body=%wide.region_5.8_spmd.clone.clone.sunk | while | flops 1402990592 | bytes 4900016 | solution.py:137
  125.2 0.7 fusion.185
  126.0 0.7 fusion.186
  126.7 1.3 convolution_add_fusion.3
  128.0 3.4 %fusion.184 = f32[512,512]{1,0:T(8,128)S(1)} fusion(s32[16,128]{1,0:T(8,128)S(1)} %iota_add_fusion.4, s32[16,128]{1,0:T(8,128)S(1)} %iota_add_fusion.5, f32[512,512]{1,0:T(8,128)S(1)} %get-tuple-element.330, bf16[8,16,128,128]{3,2,1,0:T(8,128)(2,1)} %get-tuple-element.342, s32[]{:T(128)} %get-tuple-element.329, pred[]{:T(512)S(6)} %compare.44), kind=kOutput, calls=%fused_computation.15.clone.1 | convolution fusion | flops 1345847296 | bytes 2638337 | tf_op jit(solution)/shard_map/while/body/eval_jaxpr/kiy,kix->yx/dot_general | solution.py:123
  131.6 0.7 fusion.185
  132.3 0.7 fusion.186
  133.1 1.3 convolution_add_fusion.3
  134.3 3.4 %fusion.184 = f32[512,512]{1,0:T(8,128)S(1)} fusion(s32[16,128]{1,0:T(8,128)S(1)} %iota_add_fusion.4, s32[16,128]{1,0:T(8,128)S(1)} %iota_add_fusion.5, f32[512,512]{1,0:T(8,128)S(1)} %get-tuple-element.330, bf16[8,16,128,128]{3,2,1,0:T(8,128)(2,1)} %get-tuple-element.342, s32[]{:T(128)} %get-tuple-element.329, pred[]{:T(512)S(6)} %compare.44), kind=kOutput, calls=%fused_computation.15.clone.1 | convolution fusion | flops 1345847296 | bytes 2638337 | tf_op jit(solution)/shard_map/while/body/eval_jaxpr/kiy,kix->yx/dot_general | solution.py:123
  137.9 0.7 fusion.185
  138.7 0.7 fusion.186
  139.4 1.3 convolution_add_fusion.3
  140.7 3.4 %fusion.184 = f32[512,512]{1,0:T(8,128)S(1)} fusion(s32[16,128]{1,0:T(8,128)S(1)} %iota_add_fusion.4, s32[16,128]{1,0:T(8,128)S(1)} %iota_add_fusion.5, f32[512,512]{1,0:T(8,128)S(1)} %get-tuple-element.330, bf16[8,16,128,128]{3,2,1,0:T(8,128)(2,1)} %get-tuple-element.342, s32[]{:T(128)} %get-tuple-element.329, pred[]{:T(512)S(6)} %compare.44), kind=kOutput, calls=%fused_computation.15.clone.1 | convolution fusion | flops 1345847296 | bytes 2638337 | tf_op jit(solution)/shard_map/while/body/eval_jaxpr/kiy,kix->yx/dot_general | solution.py:123
  144.2 0.7 fusion.185
  145.0 0.7 fusion.186
  145.7 1.3 convolution_add_fusion.3
  147.0 3.4 %fusion.184 = f32[512,512]{1,0:T(8,128)S(1)} fusion(s32[16,128]{1,0:T(8,128)S(1)} %iota_add_fusion.4, s32[16,128]{1,0:T(8,128)S(1)} %iota_add_fusion.5, f32[512,512]{1,0:T(8,128)S(1)} %get-tuple-element.330, bf16[8,16,128,128]{3,2,1,0:T(8,128)(2,1)} %get-tuple-element.342, s32[]{:T(128)} %get-tuple-element.329, pred[]{:T(512)S(6)} %compare.44), kind=kOutput, calls=%fused_computation.15.clone.1 | convolution fusion | flops 1345847296 | bytes 2638337 | tf_op jit(solution)/shard_map/while/body/eval_jaxpr/kiy,kix->yx/dot_general | solution.py:123
  150.5 0.7 fusion.185
  151.3 0.7 fusion.186
  152.0 1.3 convolution_add_fusion.3
  153.3 3.4 %fusion.184 = f32[512,512]{1,0:T(8,128)S(1)} fusion(s32[16,128]{1,0:T(8,128)S(1)} %iota_add_fusion.4, s32[16,128]{1,0:T(8,128)S(1)} %iota_add_fusion.5, f32[512,512]{1,0:T(8,128)S(1)} %get-tuple-element.330, bf16[8,16,128,128]{3,2,1,0:T(8,128)(2,1)} %get-tuple-element.342, s32[]{:T(128)} %get-tuple-element.329, pred[]{:T(512)S(6)} %compare.44), kind=kOutput, calls=%fused_computation.15.clone.1 | convolution fusion | flops 1345847296 | bytes 2638337 | tf_op jit(solution)/shard_map/while/body/eval_jaxpr/kiy,kix->yx/dot_general | solution.py:123
  156.8 0.7 fusion.185
  157.6 0.7 fusion.186
  158.3 1.3 convolution_add_fusion.3
  159.6 3.4 %fusion.184 = f32[512,512]{1,0:T(8,128)S(1)} fusion(s32[16,128]{1,0:T(8,128)S(1)} %iota_add_fusion.4, s32[16,128]{1,0:T(8,128)S(1)} %iota_add_fusion.5, f32[512,512]{1,0:T(8,128)S(1)} %get-tuple-element.330, bf16[8,16,128,128]{3,2,1,0:T(8,128)(2,1)} %get-tuple-element.342, s32[]{:T(128)} %get-tuple-element.329, pred[]{:T(512)S(6)} %compare.44), kind=kOutput, calls=%fused_computation.15.clone.1 | convolution fusion | flops 1345847296 | bytes 2638337 | tf_op jit(solution)/shard_map/while/body/eval_jaxpr/kiy,kix->yx/dot_general | solution.py:123
  163.1 0.7 fusion.185
  163.9 0.7 fusion.186
  164.6 1.3 convolution_add_fusion.3
  165.9 3.4 %fusion.184 = f32[512,512]{1,0:T(8,128)S(1)} fusion(s32[16,128]{1,0:T(8,128)S(1)} %iota_add_fusion.4, s32[16,128]{1,0:T(8,128)S(1)} %iota_add_fusion.5, f32[512,512]{1,0:T(8,128)S(1)} %get-tuple-element.330, bf16[8,16,128,128]{3,2,1,0:T(8,128)(2,1)} %get-tuple-element.342, s32[]{:T(128)} %get-tuple-element.329, pred[]{:T(512)S(6)} %compare.44), kind=kOutput, calls=%fused_computation.15.clone.1 | convolution fusion | flops 1345847296 | bytes 2638337 | tf_op jit(solution)/shard_map/while/body/eval_jaxpr/kiy,kix->yx/dot_general | solution.py:123
  169.5 0.7 fusion.185
  170.2 0.7 fusion.186
  171.0 1.3 convolution_add_fusion.3
  172.2 3.4 %fusion.184 = f32[512,512]{1,0:T(8,128)S(1)} fusion(s32[16,128]{1,0:T(8,128)S(1)} %iota_add_fusion.4, s32[16,128]{1,0:T(8,128)S(1)} %iota_add_fusion.5, f32[512,512]{1,0:T(8,128)S(1)} %get-tuple-element.330, bf16[8,16,128,128]{3,2,1,0:T(8,128)(2,1)} %get-tuple-element.342, s32[]{:T(128)} %get-tuple-element.329, pred[]{:T(512)S(6)} %compare.44), kind=kOutput, calls=%fused_computation.15.clone.1 | convolution fusion | flops 1345847296 | bytes 2638337 | tf_op jit(solution)/shard_map/while/body/eval_jaxpr/kiy,kix->yx/dot_general | solution.py:123
  175.9 13.6 %all_to_all.10 = bf16[4,128,512]{2,1,0:T(8,128)(2,1)S(1)} all-to-all(bf16[4,128,512]{2,1,0:T(8,128)(2,1)S(1)} %bitcast.257), channel_id=1, replica_groups=mesh['patch'=64,'band'=4] {'band'}, dimensions={0} | all-to-all | bytes 1048576 | tf_op jit(solution)/shard_map/all_to_all | solution.py:140
  189.6 2.5 %collective-permute-start = (bf16[4,2,512]{2,1,0:T(2,128)(2,1)S(1)}, bf16[4,2,512]{2,1,0:T(2,128)(2,1)S(1)}, u32[]{:S(2)}, u32[]{:S(2)}) collective-permute-start(bf16[4,2,512]{2,1,0:T(2,128)(2,1)S(1)} %get-tuple-element.238), channel_id=1, source_target_pairs={{0,1},{1,2},{2,3},{4,5},{5,6},{6,7},{8,9},{9,10},{10,11},{12,13},{... | collective-permute-start | bytes 24584 | tf_op jit(solution)/shard_map/ppermute | solution.py:18
  192.0 1.5 collective-permute-start.1
  193.6 4.0 %collective-permute-done.1 = bf16[4,2,512]{2,1,0:T(2,128)(2,1)S(1)} collective-permute-done((bf16[4,2,512]{2,1,0:T(2,128)(2,1)S(1)}, bf16[4,2,512]{2,1,0:T(2,128)(2,1)S(1)}, u32[]{:S(2)}, u32[]{:S(2)}) %collective-permute-start.1) | collective-permute-done | bytes 8224 | tf_op jit(solution)/shard_map/ppermute | solution.py:19
  197.6 0.5 fusion.97
  199.2 0.4 fusion.119
  199.7 0.4 fusion.116
  200.1 0.4 fusion.115
  200.6 0.4 fusion.113
  201.0 0.4 fusion.112
  201.4 0.4 fusion.111
  201.9 0.4 fusion.109
  202.4 0.4 fusion.107
  202.8 0.4 fusion.106
  203.8 0.4 fusion.102
  204.5 2.0 pad.15
  206.5 17.2 %copy.114 = bf16[13,8,128,512]{3,1,2,0:T(8,128)(2,1)} copy(bf16[13,8,128,512]{3,2,1,0:T(8,128)(2,1)S(1)} %bitcast.253) | data formatting | bytes 27262976
  223.7 10.5 %fusion.31 = bf16[65536,64]{0,1:T(8,128)(2,1)} fusion(bf16[100,65536]{1,0:T(8,128)(2,1)} %bitcast.252, bf16[64,100]{1,0:T(8,128)(2,1)S(1)} %copy-done.4, f32[64]{0:T(128)S(1)} %copy-done.7), kind=kOutput, calls=%fused_computation.30 | convolution fusion | flops 847249408 | bytes 21508864 | tf_op jit(solution)/shard_map/dot_general | solution.py:155
  234.3 10.1 %copy.115 = bf16[8,8,128,512]{3,2,1,0:T(8,128)(2,1)} copy(bf16[8,8,128,512]{3,1,2,0:T(8,128)(2,1)} %bitcast.254) | data formatting | bytes 16777216
  (103 shorter events, 6.2 us)
Async XLA Ops:
  0.6 3.0 %copy-start = (bf16[32,1,128,128]{3,2,1,0:T(8,128)(2,1)S(1)}, bf16[32,1,128,128]{3,2,1,0:T(8,128)(2,1)}, u32[]{:S(2)}) copy-start(bf16[32,1,128,128]{3,2,1,0:T(8,128)(2,1)} %param.11) | copy-start | bytes 3145732
  0.6 5.7 %copy-start.3 = (bf16[32,1,128,128]{3,2,1,0:T(8,128)(2,1)S(1)}, bf16[32,1,128,128]{3,2,1,0:T(8,128)(2,1)}, u32[]{:S(2)}) copy-start(bf16[32,1,128,128]{3,2,1,0:T(8,128)(2,1)} %param.13) | copy-start | bytes 3145732
  3.6 7.3 %copy-start.6 = (s32[1,2048,1]{1,2,0:T(1,128)S(1)}, s32[1,2048,1]{1,2,0:T(1,128)}, u32[]{:S(2)}) copy-start(s32[1,2048,1]{1,2,0:T(1,128)} %param.15) | copy-start | bytes 24580
  9.4 20.9 %copy-start.5 = (s32[1,2048,2]{1,2,0:T(2,128)S(1)}, s32[1,2048,2]{1,2,0:T(2,128)}, u32[]{:S(2)}) copy-start(s32[1,2048,2]{1,2,0:T(2,128)} %param.16) | copy-start | bytes 49156
  18.1 107.1 %all-to-all-start = ((bf16[64,2,128,128]{3,2,1,0:T(8,128)(2,1)}), bf16[64,2,128,128]{3,2,1,0:T(8,128)(2,1)}, u32[]{:S(2)}, u32[]{:S(2)}) async-start(bf16[64,2,128,128]{3,2,1,0:T(8,128)(2,1)} %copy.82), calls=%async_computation | async-start | bytes 8388608 | tf_op jit(solution)/shard_map/all_to_all | solution.py:90
  175.9 27.7 %copy-start.2 = (bf16[512,512]{1,0:T(8,128)(2,1)}, bf16[512,512]{1,0:T(8,128)(2,1)S(1)}, u32[]{:S(2)}) copy-start(bf16[512,512]{1,0:T(8,128)(2,1)S(1)} %divide_convert_fusion) | copy-start | bytes 1572868
  189.6 4.0 %collective-permute-start = (bf16[4,2,512]{2,1,0:T(2,128)(2,1)S(1)}, bf16[4,2,512]{2,1,0:T(2,128)(2,1)S(1)}, u32[]{:S(2)}, u32[]{:S(2)}) collective-permute-start(bf16[4,2,512]{2,1,0:T(2,128)(2,1)S(1)} %get-tuple-element.238), channel_id=1, source_target_pairs={{0,1},{1,2},{2,3},{4,5},{5,6},{6,7},{8,9},{9,10},{10,11},{12,13},{... | collective-permute-start | bytes 24584 | tf_op jit(solution)/shard_map/ppermute | solution.py:18
  192.0 5.5 %collective-permute-start.1 = (bf16[4,2,512]{2,1,0:T(2,128)(2,1)S(1)}, bf16[4,2,512]{2,1,0:T(2,128)(2,1)S(1)}, u32[]{:S(2)}, u32[]{:S(2)}) collective-permute-start(bf16[4,2,512]{2,1,0:T(2,128)(2,1)S(1)} %get-tuple-element.239), channel_id=1, source_target_pairs={{1,0},{2,1},{3,2},{5,4},{6,5},{7,6},{9,8},{10,9},{11,10},{13,12},{... | collective-permute-start | bytes 24584 | tf_op jit(solution)/shard_map/ppermute | solution.py:19
  206.5 17.2 %copy-start.4 = (bf16[64,100]{1,0:T(8,128)(2,1)S(1)}, bf16[64,100]{1,0:T(8,128)(2,1)}, u32[]{:S(2)}) copy-start(bf16[64,100]{1,0:T(8,128)(2,1)} %param.18) | copy-start | bytes 38404
  206.5 17.2 %copy-start.7 = (f32[64]{0:T(128)S(1)}, f32[64]{0:T(128)}, u32[]{:S(2)}) copy-start(f32[64]{0:T(128)} %param.19) | copy-start | bytes 772
  223.7 20.6 %copy-start.1 = (bf16[32,1,128,128]{3,2,1,0:T(8,128)(2,1)S(1)}, bf16[32,1,128,128]{3,2,1,0:T(8,128)(2,1)}, u32[]{:S(2)}) copy-start(bf16[32,1,128,128]{3,2,1,0:T(8,128)(2,1)} %param.11) | copy-start | bytes 3145732
where the time goes:
time: 245 us; the launch traced here: 244 us
  waiting for transfers between devices  97.9 us (40%)
  matrix products  55.1 us (22%)
  local copies, waits for them, and re-layouts  44.3 us (18%)
  other arithmetic  16.1 us (7%)
  starting transfers between devices  15.8 us (6%)
  blocking collectives  13.6 us (6%)
    all_to_all x1, waiting for transfers between devices, body(): lax.all_to_all(jnp.einsum('nce,eij->ncij', chosen, warped, preferred_elem...  93.9 us
    unnamed x45, local copies, waits for them, and re-layouts  36.8 us
    dot_general x8, matrix products, place_block(): jnp.einsum('kiy,kix->yx', row_table.astype(jnp.bfloat16), placed_cols, pr...  27.3 us
    all_to_all x1, blocking collectives, body(): lax.all_to_all(coadd.reshape(nband, strip_rows, PS), 'band', split_axis=0...  13.6 us
    all_to_all x1, starting transfers between devices, body(): lax.all_to_all(jnp.einsum('nce,eij->ncij', chosen, warped, preferred_elem...  11.8 us
    dot_general x1, matrix products, body(): jnp.dot(det_weight, features, preferred_element_type=jnp.float32)  10.5 us
    dot_general x8, matrix products, place_block(): jnp.einsum('ky,kx->yx', row_cover, col_cover, precision=lax.Precision.HIG...  10.2 us
    reduce_sum x8, other arithmetic, place_block(): col_cover = jnp.sum(col_table.astype(jnp.float32), axis=1)  5.69 us
  transfers between devices with their start and end apart: 3, of which 2 were waited for; matrix products, arithmetic and copies ran while one was open for 1% of the time, Pallas kernels for 0%

commit v1 on v0

v1 whole, which is shorter than its diff:
```python
import jax
import jax.numpy as jnp
from jax import lax
from jax.experimental import pallas as pl
from jax.experimental.pallas import tpu as pltpu
from jax.sharding import PartitionSpec as P

PS = 512
S = 128
TAPS = 7
HALF = TAPS // 2
KS = 5
PAD = KS // 2
LANES = 128
F32 = jnp.float32
BF16 = jnp.bfloat16


def dot_nt(a, b):
    return lax.dot_general(a, b, (((1,), (1,)), ((), ())), preferred_element_type=F32)


def dot_nn(a, b):
    return lax.dot_general(a, b, (((1,), (0,)), ((), ())), preferred_element_type=F32)


def front_kernel(
    per_step, owner_ref, routes_ref, offs_ref, wts_ref, taps_ref,
    exp_ref, rows_ref, cols_ref, buf0_ref, buf1_ref, extra_ref, stage, count, sems,
):
    step = pl.program_id(0)
    steps = pl.num_programs(0)
    tiles = stage.shape[0]
    base = owner_ref[0] * tiles

    @pl.when(step == 0)
    def _():
        @pl.loop(0, count.shape[0])
        def _(i):
            count[i] = 0

    diag = lax.broadcasted_iota(jnp.int32, (S, S), 1) - lax.broadcasted_iota(jnp.int32, (S, S), 0)
    for k in range(per_step):
        tile = step * per_step + k
        psf_rows = jnp.zeros((S, S), F32)
        psf_cols = jnp.zeros((S, S), F32)
        for tap in range(TAPS):
            on = diag == tap - HALF
            psf_rows = jnp.where(on, taps_ref[tap, tile], psf_rows)
            psf_cols = jnp.where(on, taps_ref[TAPS + tap, tile], psf_cols)
        half_done = dot_nt(exp_ref[k], psf_cols.astype(BF16)).astype(BF16)
        matched = dot_nn(psf_rows.astype(BF16), half_done).astype(BF16)
        across = dot_nt(matched, cols_ref[k]).astype(BF16)
        product = dot_nn(rows_ref[k], across)
        place = base + tile
        warped = wts_ref[0, place] * product
        warped = pltpu.roll(warped, offs_ref[1, place] & (LANES - 1), 1)
        warped = pltpu.roll(warped, offs_ref[0, place] & 7, 0)
        warped = warped.astype(BF16)
        stage[tile] = warped
        dest = routes_ref[0, place]
        rank = count[dest]
        count[dest] = rank + 1

        @pl.when(rank == 0)
        def _():
            pltpu.make_async_copy(stage.at[tile], buf0_ref.at[dest], sems.at[tile]).start()

        @pl.when(rank > 0)
        def _():
            extra_ref[...] = warped
            pltpu.make_async_copy(stage.at[tile], buf1_ref.at[dest], sems.at[tile]).start()

    @pl.when(step == steps - 1)
    def _():
        @pl.loop(0, tiles)
        def _(i):
            pltpu.make_async_copy(stage.at[i], buf0_ref.at[0], sems.at[i]).wait()


def front(owner, routes, offs, wts, taps, exposures, warp_rows, warp_cols, npatch):
    tiles = exposures.shape[0]
    per_step = 4
    spec = pl.BlockSpec((per_step, None, S, S), lambda i, *_: (i, 0, 0, 0))
    anywhere = pl.BlockSpec(memory_space=pl.ANY)
    return pl.pallas_call(
        lambda *refs: front_kernel(per_step, *refs),
        name="front",
        out_shape=(
            jax.ShapeDtypeStruct((npatch, S, S), BF16),
            jax.ShapeDtypeStruct((npatch, S, S), BF16),
            jax.ShapeDtypeStruct((S, S), BF16),
        ),
        grid_spec=pltpu.PrefetchScalarGridSpec(
            num_scalar_prefetch=5,
            grid=(tiles // per_step,),
            in_specs=[spec, spec, spec],
            out_specs=(anywhere, anywhere, pl.BlockSpec((S, S), lambda i, *_: (0, 0))),
            scratch_shapes=[
                pltpu.VMEM((tiles, S, S), BF16),
                pltpu.SMEM((npatch,), jnp.int32),
                pltpu.SemaphoreType.DMA((tiles,)),
            ],
        ),
        compiler_params=pltpu.CompilerParams(
            dimension_semantics=("arbitrary",), vmem_limit_bytes=24 << 20
        ),
    )(owner, routes, offs, wts, taps, exposures, warp_rows, warp_cols)


def place_kernel(per_step, nband, table_ref, first_ref, second_ref, cover_ref, coadd_ref, strip_ref, acc, full):
    step = pl.program_id(0)
    steps = pl.num_programs(0)
    strip_rows = PS // nband
    parts = PS // LANES

    @pl.when(step == 0)
    def _():
        acc[...] = jnp.zeros_like(acc)

    lane = lax.broadcasted_iota(jnp.int32, (8, LANES), 1)
    sub = lax.broadcasted_iota(jnp.int32, (8, LANES), 0)
    for slot, src in ((0, first_ref), (1, second_ref)):
        for k in range(per_step):
            code = table_ref[slot, step * per_step + k]

            @pl.when(code > 0)
            def _():
                corner = code - 1
                top = corner // PS
                left = corner & (PS - 1)
                base = pl.multiple_of((top // 8) * 8, 8)
                shift = top & 7
                part = left // LANES
                on = lane >= (left & (LANES - 1))
                tile = src[k].astype(F32)
                for g in range(S // 8):
                    rows = tile[8 * g : 8 * g + 8]
                    if g == 0:
                        low = jnp.where(sub < shift, rows, 0.0)
                        rows = rows - low
                        at = pl.ds(base + S, 8)
                        acc[part, at, :] += jnp.where(on, low, 0.0)
                        acc[part + 1, at, :] += jnp.where(on, 0.0, low)
                    at = pl.ds(base + 8 * g, 8)
                    acc[part, at, :] += jnp.where(on, rows, 0.0)
                    acc[part + 1, at, :] += jnp.where(on, 0.0, rows)

    @pl.when(step == steps - 1)
    def _():
        edge = full.shape[0] - PS
        full[0 : edge // 2, :] = jnp.zeros((edge // 2, PS), F32)
        full[PS + edge // 2 :, :] = jnp.zeros((edge // 2, PS), F32)
        for part in range(parts):
            at = slice(part * LANES, part * LANES + LANES)
            value = (acc[part, 0:PS, :] / jnp.maximum(cover_ref[:, at], 1.0)).astype(BF16)
            coadd_ref[:, at] = value
            full[edge // 2 : edge // 2 + PS, at] = value.astype(F32)
        for b in range(nband):
            start = edge // 2 - PAD + b * strip_rows
            strip_ref[b] = full[start : start + strip_ref.shape[1], :].astype(BF16)


def place(table, first, second, cover, nband):
    slots = first.shape[0]
    per_step = 8
    strip = PS // nband + 8
    spec = pl.BlockSpec((per_step, S, S), lambda i, *_: (i, 0, 0))
    return pl.pallas_call(
        lambda *refs: place_kernel(per_step, nband, *refs),
        name="place",
        out_shape=(
            jax.ShapeDtypeStruct((PS, PS), BF16),
            jax.ShapeDtypeStruct((nband, strip, PS), BF16),
        ),
        grid_spec=pltpu.PrefetchScalarGridSpec(
            num_scalar_prefetch=1,
            grid=(slots // per_step,),
            in_specs=[spec, spec, pl.BlockSpec((PS, PS), lambda i, *_: (0, 0))],
            out_specs=(
                pl.BlockSpec((PS, PS), lambda i, *_: (0, 0)),
                pl.BlockSpec((nband, strip, PS), lambda i, *_: (0, 0, 0)),
            ),
            scratch_shapes=[
                pltpu.VMEM((PS // LANES + 1, PS + 8, LANES), F32),
                pltpu.VMEM((PS + 16, PS), F32),
            ],
        ),
        compiler_params=pltpu.CompilerParams(
            dimension_semantics=("arbitrary",), vmem_limit_bytes=24 << 20
        ),
    )(table, first, second, cover)


def detect_kernel(nband, strip_ref, weight_ref, bias_ref, out_ref, main, edge):
    step = pl.program_id(0)
    groups = main.shape[0]
    channels = out_ref.shape[0]

    @pl.when(step == 0)
    def _():
        column = lax.broadcasted_iota(jnp.int32, (8, PS), 1)
        for g in range(groups):
            pieces = []
            for s in range(KS):
                for b in range(nband):
                    x = strip_ref[b, 8 * g : 8 * g + 8, :].astype(F32)
                    d = s - PAD
                    if d:
                        x = pltpu.roll(x, (-d) % PS, 1)
                        x = jnp.where((column + d >= 0) & (column + d < PS), x, 0.0)
                    pieces.append(x)
            main[g] = jnp.concatenate(pieces, axis=0).astype(BF16)
            pairs = []
            for i in range(0, len(pieces), 2):
                pairs.append(pieces[i][0:4])
                pairs.append(pieces[i + 1][0:4])
            edge[g] = jnp.concatenate(pairs, axis=0).astype(BF16)

    rhs = jnp.concatenate([main[step], edge[step + 1]], axis=0)
    res = dot_nn(weight_ref[...], rhs) + bias_ref[...]
    out_ref[...] = res.reshape(channels, 8, PS).astype(BF16)


def detect(strips, weight, bias, channels, strip_rows):
    nband, rows, _ = strips.shape
    groups = rows // 8
    depth = nband * KS
    return pl.pallas_call(
        lambda *refs: detect_kernel(nband, *refs),
        name="detect",
        out_shape=jax.ShapeDtypeStruct((channels, strip_rows, PS), BF16),
        grid_spec=pltpu.PrefetchScalarGridSpec(
            num_scalar_prefetch=0,
            grid=(strip_rows // 8,),
            in_specs=[
                pl.BlockSpec(strips.shape, lambda i: (0, 0, 0)),
                pl.BlockSpec(weight.shape, lambda i: (0, 0)),
                pl.BlockSpec(bias.shape, lambda i: (0, 0)),
            ],
            out_specs=pl.BlockSpec((channels, 8, PS), lambda i: (0, i, 0)),
            scratch_shapes=[
                pltpu.VMEM((groups, depth * 8, PS), BF16),
                pltpu.VMEM((groups, depth * 4, PS), BF16),
            ],
        ),
        compiler_params=pltpu.CompilerParams(
            dimension_semantics=("arbitrary",), vmem_limit_bytes=32 << 20
        ),
    )(strips, weight, bias)


def toeplitz(det_weight, nband):
    channels = det_weight.shape[0]
    taps = det_weight.reshape(channels, nband, KS, KS).transpose(0, 3, 1, 2)
    row_out = jnp.arange(8)[:, None]
    out = []
    for lo, hi in ((0, 8), (8, 12)):
        row_in = jnp.arange(lo, hi)[None, :]
        total = jnp.zeros((channels, 8, KS, nband, hi - lo), det_weight.dtype)
        for r in range(KS):
            on = (row_in - row_out == r)[None, :, None, None, :]
            total = jnp.where(on, taps[:, None, :, :, r, None], total)
        out.append(total.reshape(channels * 8, KS * nband * (hi - lo)))
    return jnp.concatenate(out, axis=1)


def slot_select(targets, capacity):
    counts = jnp.cumsum(targets.astype(jnp.int32), axis=1) - 1
    slot_ids = jnp.arange(capacity, dtype=jnp.int32)
    return targets[None] & (counts[None] == slot_ids[:, None, None])


def body(exposures, psf_taps, warp_rows, warp_cols, routes, offsets, weights, det_weight, det_bias):
    npatch = lax.axis_size("patch")
    nband = lax.axis_size("band")
    tiles = exposures.shape[0]
    capacity = 2
    owner = lax.axis_index("patch").astype(jnp.int32)
    routes_row = routes.transpose(0, 2, 1).reshape(1, -1)
    offs_rows = offsets.transpose(0, 2, 1).reshape(2, -1)
    taps = psf_taps[:, 0].transpose(1, 2, 0).reshape(2 * TAPS, tiles).astype(F32)
    buf0, buf1, extra = front(
        owner[None], routes_row, offs_rows, weights, taps, exposures, warp_rows, warp_cols, npatch
    )
    dest_all = routes_row.reshape(npatch, tiles)
    same = (dest_all[:, :, None] == dest_all[:, None, :]) & (
        jnp.arange(tiles)[None, :, None] > jnp.arange(tiles)[None, None, :]
    )
    repeats = jnp.max(jnp.sum(jnp.any(same, axis=2).astype(F32), axis=1))
    repeats = lax.pmax(repeats, "band")
    first = lax.all_to_all(buf0, "patch", split_axis=0, concat_axis=0, tiled=True)
    second = lax.cond(
        repeats <= 1.0,
        lambda: lax.all_gather(extra, "patch"),
        lambda: lax.all_to_all(buf1, "patch", split_axis=0, concat_axis=0, tiled=True),
    )
    landed = slot_select(dest_all == owner, capacity)
    corner = (offs_rows[0] * PS + offs_rows[1] + 1).reshape(npatch, tiles)
    table = jnp.sum(jnp.where(landed, corner[None], 0), axis=-1)
    slot_weights = jnp.sum(
        jnp.where(landed, weights.reshape(npatch, tiles)[None], 0.0), axis=-1
    ).reshape(-1)
    slot_corner = jnp.maximum(table.reshape(-1) - 1, 0)
    pixels = jnp.arange(PS, dtype=jnp.int32)
    down = pixels[None, :] - (slot_corner // PS)[:, None]
    right = pixels[None, :] - (slot_corner % PS)[:, None]
    row_cover = jnp.where((down >= 0) & (down < S), slot_weights[:, None], 0.0)
    col_cover = ((right >= 0) & (right < S)).astype(F32)
    cover = jnp.einsum("ky,kx->yx", row_cover, col_cover, precision=lax.Precision.HIGHEST)
    coadd, strips = place(table, first, second, cover, nband)
    strips = lax.all_to_all(strips, "band", split_axis=0, concat_axis=0, tiled=True)
    channels = det_weight.shape[0]
    strip_rows = PS // nband
    bias = jnp.broadcast_to(det_bias[:, None, None], (channels, 8, 1)).reshape(channels * 8, 1)
    detection = detect(strips, toeplitz(det_weight, nband), bias, channels, strip_rows)
    return (coadd[None, None], detection[None])


def solution(mesh):
    placed = (
        P("patch", "band", None, None),
        P("patch", "band", None, None),
        P("patch", "band", None, None),
        P("patch", "band", None, None),
        P("band", None, None),
        P("band", None, None),
        P("band", None),
        P(),
        P(),
    )
    return jax.shard_map(
        body,
        mesh=mesh,
        in_specs=placed,
        out_specs=(P("patch", "band", None, None), P("patch", None, "band", None)),
        check_vma=False,
    )
```

time: 245 us -> 234 us (0.955)
  matrix products: 55.1 us -> 1.34 us
  Pallas kernels: 0 us -> 41.4 us
  waiting for transfers between devices: 97.9 us -> 124 us
  local copies, waits for them, and re-layouts: 44.3 us -> 19.4 us
  between operations: 1.06 us -> 15 us
  other arithmetic: 16.1 us -> 7.2 us
  starting transfers between devices: 15.8 us -> 12.2 us
    all_gather x0 -> x1, waiting for transfers between devices: none -> 80 us  [body(): lax.all_gather(extra, 'patch')]
    dot_general x20 -> x1, matrix products: 55.1 us -> 1.34 us  [body(): jnp.einsum('ky,kx->yx', row_cover, col_cover, precision=lax.Precision.HIG...]
    all_to_all x1 -> x2, waiting for transfers between devices: 93.9 us -> 43.6 us  [the longest x1 39.6 us: body(): lax.all_to_all(buf0, 'patch', split_axis=0, concat_axis=0, tiled=True)]
    pallas_call x0 -> x3, Pallas kernels: none -> 41.4 us  [the longest x1 24.7 us: front(): pl.pallas_call(lambda *refs: front_kernel(per_step, *refs), name='front',...]
    unnamed x45 -> x47, local copies, waits for them, and re-layouts: 36.8 us -> 9.73 us
    all_to_all x1 -> x0, blocking collectives: 13.6 us -> none  [body(): lax.all_to_all(coadd.reshape(nband, strip_rows, PS), 'band', split_axis=0...]
    reduce_sum x18 -> x3, other arithmetic: 11.4 us -> 0.1 us  [the longest x1 0.04 us: body(): table = jnp.sum(jnp.where(landed, corner[None], 0), axis=-1)]
    pmax x0 -> x1, blocking collectives: none -> 11.3 us  [body(): repeats = lax.pmax(repeats, 'band')]
  transfers between devices with their start and end apart: 3 -> 3, of which waited for: 2 -> 3; matrix products, arithmetic and copies ran while one was open for 1% -> 7% of each run, Pallas kernels for 0% -> 0%
where the time goes in v1:
time: 234 us; the launch traced here: 232 us
  waiting for transfers between devices  124 us (53%)
  Pallas kernels  41.4 us (18%)
  local copies, waits for them, and re-layouts  19.4 us (8%)
  between operations  15 us (6%)
  starting transfers between devices  12.2 us (5%)
  blocking collectives  11.3 us (5%)
  other arithmetic  7.2 us (3%)
    all_gather x1, waiting for transfers between devices, body(): lax.all_gather(extra, 'patch')  80 us
    all_to_all x1, waiting for transfers between devices, body(): lax.all_to_all(buf0, 'patch', split_axis=0, concat_axis=0, tiled=True)  39.6 us
    pallas_call x1, Pallas kernels, front(): pl.pallas_call(lambda *refs: front_kernel(per_step, *refs), name='front',...  24.7 us
    pmax x1, blocking collectives, body(): repeats = lax.pmax(repeats, 'band')  11.3 us
    pallas_call x1, Pallas kernels, detect(): pl.pallas_call(lambda *refs: detect_kernel(nband, *refs), name='detect',...  9.81 us
    unnamed x47, local copies, waits for them, and re-layouts  9.73 us
    all_to_all x1, starting transfers between devices, body(): lax.all_to_all(buf0, 'patch', split_axis=0, concat_axis=0, tiled=True)  7.94 us
    pallas_call x1, Pallas kernels, place(): pl.pallas_call(lambda *refs: place_kernel(per_step, nband, *refs), name='...  6.92 us
  transfers between devices with their start and end apart: 3, of which 3 were waited for; matrix products, arithmetic and copies ran while one was open for 7% of the time, Pallas kernels for 0%

profile of v1, /device:TPU:32, one launch (start us, length us, event | category | flops | bytes accessed | tf_op | source)
XLA Modules:
  0.0 232.2 jit_solution(6234899586440778006)
XLA Ops:
  7.2 0.5 broadcast.326
  7.7 1.4 reduce.10
  9.1 0.1 reshape_reshape_transpose.3
  9.1 0.7 convert_bitcast_fusion
  9.8 0.1 copy.36
  9.9 0.2 and_reduce_fusion
  10.2 0.6 reduce_max.9
  10.8 11.3 %pmax.7 = f32[]{:T(128)} all-reduce(f32[]{:T(128)} %reduce_max.9), channel_id=1, replica_groups=mesh['patch'=64,'band'=4] {'band'}, use_global_device_ids=true, to_apply=%region_5.0 | all-reduce | flops 1 | bytes 8 | tf_op jit(solution)/shard_map/pmax | solution.py:291
  22.8 0.0 copy-start.1
  22.8 1.2 copy-done.1
  24.0 1.2 copy-done.2
  25.2 1.2 copy-done.3
  26.5 0.7 copy-done.5
  27.2 0.7 copy-done.7
  27.9 0.7 copy-done.8
  28.6 24.7 %front.1 = (bf16[64,128,128]{2,1,0:T(8,128)(2,1)S(1)}, bf16[64,128,128]{2,1,0:T(8,128)(2,1)S(1)}, bf16[128,128]{1,0:T(8,128)(2,1)}) custom-call(s32[1]{0:T(128)} %bitcast.2.refs_0_, s32[1,2048]{1,0:T(1,128)S(1)} %bitcast.38, s32[2,2048]{1,0:T(2,128)S(1)} %bitcast.36, f32[1,2048]{1,0:T(1,128)S(1)} %copy-done.8, f32[14,32]{1,0:T(8,128)S(1)} %reshape.306.refs_4_, ...), custom_call_target="tpu_custom_call" | custom-call | tf_op jit(solution)/shard_map/front/pallas_call | solution.py:86
  53.3 0.0 copy-start
  53.3 1.3 copy-done
  54.6 80.7 %conditional.1 = (bf16[64,128,128]{2,1,0:T(8,128)(2,1)}) conditional(s32[]{:T(128)} %convert_element_type.29, bf16[64,128,128]{2,1,0:T(8,128)(2,1)S(1)} %get-tuple-element.13, bf16[128,128]{1,0:T(8,128)(2,1)} %get-tuple-element.14), branch_computations={%region_6.0_spmd, %region_7.8_spmd} | conditional | bytes 6389808 | solution.py:293
  54.6 0.0 all-gather.3.cloned.1.call-start
  54.6 0.7 all-gather.3.cloned.1.call-update
  55.3 80.0 %all-gather.3.cloned.1.call-done = bf16[8192,128]{1,0:T(8,128)(2,1)} async-done(((bf16[128,128]{1,0:T(8,128)(2,1)}), bf16[8192,128]{1,0:T(8,128)(2,1)}) %all-gather.3.cloned.1.call-update) | async-done | bytes 2097168 | tf_op jit(solution)/shard_map/cond/branch_1_fun/all_gather | solution.py:295
  135.3 7.9 %all-to-all-start.1 = ((bf16[64,128,128]{2,1,0:T(8,128)(2,1)}), bf16[64,128,128]{2,1,0:T(8,128)(2,1)S(1)}, u32[]{:S(2)}, u32[]{:S(2)}) async-start(bf16[64,128,128]{2,1,0:T(8,128)(2,1)} %copy-done), calls=%async_computation.1 | async-start | bytes 4194304 | tf_op jit(solution)/shard_map/all_to_all | solution.py:292
  143.3 0.0 copy-done.6
  143.3 0.1 add.68
  143.4 0.1 copy.34
  143.5 0.2 reduce_window_sum.11
  143.7 0.1 copy.33
  143.8 0.1 copy.32
  143.9 0.6 div.12
  144.5 0.6 ne.41
  145.1 0.7 rem.19
  145.8 0.6 broadcast.327
  146.4 0.7 reduce.11
  147.1 0.1 broadcast_in_dim.218
  147.1 0.1 copy.38
  147.3 0.6 broadcast_in_dim.221
  147.8 0.1 copy.39
  148.0 0.0 copy-start.10
  148.0 0.1 fusion.30
  148.2 0.4 copy-done.10
  148.6 0.1 copy-done.12
  148.7 0.0 copy-done.14
  148.7 0.0 copy-done.16
  148.8 0.0 copy-done.18
  148.8 1.0 select_select_fusion.1
  149.8 2.1 reshape.308
  151.9 0.1 copy.46
  152.0 0.7 and_select_fusion.1
  152.7 1.3 fusion.2.refs_3_
  154.1 0.0 copy-start.11
  154.1 39.6 %all-to-all-done.1.refs_1_ = bf16[64,128,128]{2,1,0:T(8,128)(2,1)S(1)} async-done(((bf16[64,128,128]{2,1,0:T(8,128)(2,1)}), bf16[64,128,128]{2,1,0:T(8,128)(2,1)S(1)}, u32[]{:S(2)}, u32[]{:S(2)}) %all-to-all-start.1) | async-done | bytes 2097184 | tf_op jit(solution)/shard_map/all_to_all | solution.py:292
  193.7 6.9 %place.1 = (bf16[512,512]{1,0:T(8,128)(2,1)}, bf16[4,136,512]{2,1,0:T(8,128)(2,1)S(1)}) custom-call(s32[2,64]{1,0:T(2,128)S(1)} %select_reduce_fusion.1.refs_0_, bf16[64,128,128]{2,1,0:T(8,128)(2,1)S(1)} %all-to-all-done.1.refs_1_, bf16[64,128,128]{2,1,0:T(8,128)(2,1)} %get-tuple-element.41.refs_2_, f32[512,512]{1,0:T(8,128)S(1)} %fusion.2.refs_3_), custom_call_target="tpu_custom_call" | custom-call | tf_op jit(solution)/shard_map/place/pallas_call | solution.py:169
  200.6 0.8 copy-done.4
  201.4 4.2 %all-to-all-start.2 = ((bf16[4,136,512]{2,1,0:T(8,128)(2,1)}), bf16[4,136,512]{2,1,0:T(8,128)(2,1)S(1)}, u32[]{:S(2)}, u32[]{:S(2)}) async-start(bf16[4,136,512]{2,1,0:T(8,128)(2,1)} %copy-done.4), calls=%async_computation.2 | async-start | bytes 1114112 | tf_op jit(solution)/shard_map/all_to_all | solution.py:312
  205.7 1.3 select_select_fusion
  207.0 0.0 copy-start.21
  207.0 4.1 %reshape.307 = bf16[512,160]{0,1:T(8,128)(2,1)S(1)} reshape(bf16[64,8,5,4,8]{1,0,4,3,2:T(8,128)(2,1)S(1)} %select_select_fusion) | data formatting | bytes 327680 | tf_op jit(solution)/shard_map/jit(_where)/select_n | solution.py:263
  211.1 0.1 copy.45
  211.2 0.1 broadcast_in_dim.256
  211.3 0.1 broadcast_in_dim.259.refs_2_
  211.4 0.1 pad_maximum_fusion.refs_1_
  211.5 4.0 %all-to-all-done.2.refs_0_ = bf16[4,136,512]{2,1,0:T(8,128)(2,1)S(1)} async-done(((bf16[4,136,512]{2,1,0:T(8,128)(2,1)}), bf16[4,136,512]{2,1,0:T(8,128)(2,1)S(1)}, u32[]{:S(2)}, u32[]{:S(2)}) %all-to-all-start.2) | async-done | bytes 557088 | tf_op jit(solution)/shard_map/all_to_all | solution.py:312
  215.5 9.8 %detect.1 = bf16[64,128,512]{2,1,0:T(8,128)(2,1)} custom-call(bf16[4,136,512]{2,1,0:T(8,128)(2,1)S(1)} %all-to-all-done.2.refs_0_, bf16[512,240]{1,0:T(8,128)(2,1)S(1)} %pad_maximum_fusion.refs_1_, f32[512,1]{1,0:T(8,128)S(1)} %broadcast_in_dim.259.refs_2_), custom_call_target="tpu_custom_call" | custom-call | tf_op jit(solution)/shard_map/detect/pallas_call | solution.py:229
  (45 shorter events, 0.3 us)
Async XLA Ops:
  22.8 1.2 copy-start.1
  24.0 1.2 copy-start.2
  25.2 1.2 copy-start.3
  26.5 0.7 copy-start.5
  27.2 0.7 copy-start.7
  27.9 0.7 copy-start.8
  53.3 1.3 copy-start
  54.6 80.7 %all-gather.3.cloned.1.call-start = ((), (), s32[]{:S(2)}) async-start(), calls=%async_computation.3 | async-start | bytes 2129920 | tf_op jit(solution)/shard_map/cond/branch_1_fun/all_gather | solution.py:295
  135.3 8.0 %copy-start.6 = (s32[1,2048,2]{1,2,0:T(2,128)S(1)}, s32[1,2048,2]{1,2,0:T(2,128)}, u32[]{:S(2)}) copy-start(s32[1,2048,2]{1,2,0:T(2,128)} %param.16) | copy-start | bytes 49156
  135.3 11.0 %copy-start.9 = (f32[1,2048]{1,0:T(1,128)S(1)}, f32[1,2048]{1,0:T(1,128)}, u32[]{:S(2)}) copy-start(f32[1,2048]{1,0:T(1,128)} %refs_3_.1) | copy-start | bytes 24580
  135.3 12.5 %copy-start.20 = (bf16[64,100]{1,0:T(8,128)(2,1)S(1)}, bf16[64,100]{1,0:T(8,128)(2,1)}, u32[]{:S(2)}) copy-start(bf16[64,100]{1,0:T(8,128)(2,1)} %param.18) | copy-start | bytes 38404
  135.3 58.4 %all-to-all-start.1 = ((bf16[64,128,128]{2,1,0:T(8,128)(2,1)}), bf16[64,128,128]{2,1,0:T(8,128)(2,1)S(1)}, u32[]{:S(2)}, u32[]{:S(2)}) async-start(bf16[64,128,128]{2,1,0:T(8,128)(2,1)} %copy-done), calls=%async_computation.1 | async-start | bytes 4194304 | tf_op jit(solution)/shard_map/all_to_all | solution.py:292
  148.0 0.6 copy-start.10
  148.1 0.6 copy-start.12
  148.1 0.6 copy-start.14
  148.2 0.6 copy-start.16
  148.2 0.6 copy-start.18
  154.1 51.6 %copy-start.11 = (bf16[64,5,4,1]{0,2,1,3:T(4,128)(2,1)S(1)}, bf16[64,5,4,1]{0,2,1,3:T(4,128)(2,1)}, u32[]{:S(2)}) copy-start(bf16[64,5,4,1]{0,2,1,3:T(4,128)(2,1)} %copy-done.10) | copy-start | bytes 7684
  154.1 51.6 %copy-start.13 = (bf16[64,5,4]{0,2,1:T(4,128)(2,1)S(1)}, bf16[64,5,4]{0,2,1:T(4,128)(2,1)}, u32[]{:S(2)}) copy-start(bf16[64,5,4]{0,2,1:T(4,128)(2,1)} %copy-done.12) | copy-start | bytes 7684
  154.1 51.5 %copy-start.15 = (bf16[64,5,4]{0,2,1:T(4,128)(2,1)S(1)}, bf16[64,5,4]{0,2,1:T(4,128)(2,1)}, u32[]{:S(2)}) copy-start(bf16[64,5,4]{0,2,1:T(4,128)(2,1)} %copy-done.14) | copy-start | bytes 7684
  154.1 51.5 %copy-start.17 = (bf16[64,5,4]{0,2,1:T(4,128)(2,1)S(1)}, bf16[64,5,4]{0,2,1:T(4,128)(2,1)}, u32[]{:S(2)}) copy-start(bf16[64,5,4]{0,2,1:T(4,128)(2,1)} %copy-done.16) | copy-start | bytes 7684
  154.1 51.5 %copy-start.19 = (bf16[64,5,4]{0,2,1:T(4,128)(2,1)S(1)}, bf16[64,5,4]{0,2,1:T(4,128)(2,1)}, u32[]{:S(2)}) copy-start(bf16[64,5,4]{0,2,1:T(4,128)(2,1)} %copy-done.18) | copy-start | bytes 7684
  200.6 0.8 copy-start.4
  201.4 14.1 %all-to-all-start.2 = ((bf16[4,136,512]{2,1,0:T(8,128)(2,1)}), bf16[4,136,512]{2,1,0:T(8,128)(2,1)S(1)}, u32[]{:S(2)}, u32[]{:S(2)}) async-start(bf16[4,136,512]{2,1,0:T(8,128)(2,1)} %copy-done.4), calls=%async_computation.2 | async-start | bytes 1114112 | tf_op jit(solution)/shard_map/all_to_all | solution.py:312
  207.0 4.2 %copy-start.21 = (f32[64]{0:T(128)S(1)}, f32[64]{0:T(128)}, u32[]{:S(2)}) copy-start(f32[64]{0:T(128)} %param.19) | copy-start | bytes 772
Sparse Core Ops, SparseCore 0:
  58.7 76.5 all-gather.2

commit v2 on v1

--- a/solution.py
+++ b/solution.py
@@ -40,36 +40,40 @@
             count[i] = 0
 
     diag = lax.broadcasted_iota(jnp.int32, (S, S), 1) - lax.broadcasted_iota(jnp.int32, (S, S), 0)
-    for k in range(per_step):
-        tile = step * per_step + k
-        psf_rows = jnp.zeros((S, S), F32)
-        psf_cols = jnp.zeros((S, S), F32)
+
+    def band(first_tap, tile):
+        matrix = jnp.zeros((S, S), F32)
         for tap in range(TAPS):
-            on = diag == tap - HALF
-            psf_rows = jnp.where(on, taps_ref[tap, tile], psf_rows)
-            psf_cols = jnp.where(on, taps_ref[TAPS + tap, tile], psf_cols)
-        half_done = dot_nt(exp_ref[k], psf_cols.astype(BF16)).astype(BF16)
-        matched = dot_nn(psf_rows.astype(BF16), half_done).astype(BF16)
-        across = dot_nt(matched, cols_ref[k]).astype(BF16)
-        product = dot_nn(rows_ref[k], across)
-        place = base + tile
-        warped = wts_ref[0, place] * product
+            matrix = jnp.where(diag == tap - HALF, taps_ref[first_tap + tap, tile], matrix)
+        return matrix.astype(BF16)
+
+    each = range(per_step)
+    here = [step * per_step + k for k in each]
+    psf_rows = [band(0, t) for t in here]
+    psf_cols = [band(TAPS, t) for t in here]
+    half_done = [dot_nt(exp_ref[k], psf_cols[k]).astype(BF16) for k in each]
+    matched = [dot_nn(psf_rows[k], half_done[k]).astype(BF16) for k in each]
+    across = [dot_nt(matched[k], cols_ref[k]).astype(BF16) for k in each]
+    product = [dot_nn(rows_ref[k], across[k]) for k in each]
+    for k in each:
+        place = base + here[k]
+        warped = wts_ref[0, place] * product[k]
         warped = pltpu.roll(warped, offs_ref[1, place] & (LANES - 1), 1)
         warped = pltpu.roll(warped, offs_ref[0, place] & 7, 0)
-        warped = warped.astype(BF16)
-        stage[tile] = warped
-        dest = routes_ref[0, place]
+        stage[here[k]] = warped.astype(BF16)
+    for k in each:
+        dest = routes_ref[0, base + here[k]]
         rank = count[dest]
         count[dest] = rank + 1
 
         @pl.when(rank == 0)
         def _():
-            pltpu.make_async_copy(stage.at[tile], buf0_ref.at[dest], sems.at[tile]).start()
+            pltpu.make_async_copy(stage.at[here[k]], buf0_ref.at[dest], sems.at[here[k]]).start()
 
         @pl.when(rank > 0)
         def _():
-            extra_ref[...] = warped
-            pltpu.make_async_copy(stage.at[tile], buf1_ref.at[dest], sems.at[tile]).start()
+            extra_ref[...] = stage[here[k]]
+            pltpu.make_async_copy(stage.at[here[k]], buf1_ref.at[dest], sems.at[here[k]]).start()
 
     @pl.when(step == steps - 1)
     def _():
@@ -80,7 +84,7 @@
 
 def front(owner, routes, offs, wts, taps, exposures, warp_rows, warp_cols, npatch):
     tiles = exposures.shape[0]
-    per_step = 4
+    per_step = 16
     spec = pl.BlockSpec((per_step, None, S, S), lambda i, *_: (i, 0, 0, 0))
     anywhere = pl.BlockSpec(memory_space=pl.ANY)
     return pl.pallas_call(
@@ -103,12 +107,24 @@
             ],
         ),
         compiler_params=pltpu.CompilerParams(
-            dimension_semantics=("arbitrary",), vmem_limit_bytes=24 << 20
+            dimension_semantics=("arbitrary",)
         ),
     )(owner, routes, offs, wts, taps, exposures, warp_rows, warp_cols)
 
 
-def place_kernel(per_step, nband, table_ref, first_ref, second_ref, cover_ref, coadd_ref, strip_ref, acc, full):
+def spread(index, masks):
+    total = 0
+    for bit, mask in enumerate(masks):
+        total = total | (((index >> bit) & 1) * mask)
+    return total
+
+
+def swap(x, axis, mask):
+    size = lax.axis_size(axis)
+    return lax.ppermute(x, axis, [(i, i ^ mask) for i in range(size)])
+
+
+def place_kernel(per_step, nband, masks, owner_ref, table_ref, first_ref, second_ref, cover_ref, coadd_ref, strip_ref, acc, full):
     step = pl.program_id(0)
     steps = pl.num_programs(0)
     strip_rows = PS // nband
@@ -122,7 +138,10 @@
     sub = lax.broadcasted_iota(jnp.int32, (8, LANES), 0)
     for slot, src in ((0, first_ref), (1, second_ref)):
         for k in range(per_step):
-            code = table_ref[slot, step * per_step + k]
+            source = step * per_step + k
+            if slot == 1 and masks:
+                source = owner_ref[0] ^ spread(source, masks)
+            code = table_ref[slot, source]
 
             @pl.when(code > 0)
             def _():
@@ -161,20 +180,20 @@
             strip_ref[b] = full[start : start + strip_ref.shape[1], :].astype(BF16)
 
 
-def place(table, first, second, cover, nband):
+def place(owner, table, first, second, cover, nband, masks):
     slots = first.shape[0]
-    per_step = 8
+    per_step = 16
     strip = PS // nband + 8
     spec = pl.BlockSpec((per_step, S, S), lambda i, *_: (i, 0, 0))
     return pl.pallas_call(
-        lambda *refs: place_kernel(per_step, nband, *refs),
+        lambda *refs: place_kernel(per_step, nband, masks, *refs),
         name="place",
         out_shape=(
             jax.ShapeDtypeStruct((PS, PS), BF16),
             jax.ShapeDtypeStruct((nband, strip, PS), BF16),
         ),
         grid_spec=pltpu.PrefetchScalarGridSpec(
-            num_scalar_prefetch=1,
+            num_scalar_prefetch=2,
             grid=(slots // per_step,),
             in_specs=[spec, spec, pl.BlockSpec((PS, PS), lambda i, *_: (0, 0))],
             out_specs=(
@@ -187,9 +206,9 @@
             ],
         ),
         compiler_params=pltpu.CompilerParams(
-            dimension_semantics=("arbitrary",), vmem_limit_bytes=24 << 20
-        ),
-    )(table, first, second, cover)
+            dimension_semantics=("arbitrary",)
+        ),
+    )(owner, table, first, second, cover)
 
 
 def detect_kernel(nband, strip_ref, weight_ref, bias_ref, out_ref, main, edge):
@@ -217,35 +236,39 @@
                 pairs.append(pieces[i + 1][0:4])
             edge[g] = jnp.concatenate(pairs, axis=0).astype(BF16)
 
-    rhs = jnp.concatenate([main[step], edge[step + 1]], axis=0)
-    res = dot_nn(weight_ref[...], rhs) + bias_ref[...]
-    out_ref[...] = res.reshape(channels, 8, PS).astype(BF16)
+    per_step = out_ref.shape[1] // 8
+    for i in range(per_step):
+        g = step * per_step + i
+        rhs = jnp.concatenate([main[g], edge[g + 1]], axis=0)
+        res = dot_nn(weight_ref[...], rhs) + bias_ref[...]
+        out_ref[:, 8 * i : 8 * i + 8, :] = res.reshape(channels, 8, PS).astype(BF16)
 
 
 def detect(strips, weight, bias, channels, strip_rows):
     nband, rows, _ = strips.shape
     groups = rows // 8
     depth = nband * KS
+    step_rows = 32
     return pl.pallas_call(
         lambda *refs: detect_kernel(nband, *refs),
         name="detect",
         out_shape=jax.ShapeDtypeStruct((channels, strip_rows, PS), BF16),
         grid_spec=pltpu.PrefetchScalarGridSpec(
             num_scalar_prefetch=0,
-            grid=(strip_rows // 8,),
+            grid=(strip_rows // step_rows,),
             in_specs=[
                 pl.BlockSpec(strips.shape, lambda i: (0, 0, 0)),
                 pl.BlockSpec(weight.shape, lambda i: (0, 0)),
                 pl.BlockSpec(bias.shape, lambda i: (0, 0)),
             ],
-            out_specs=pl.BlockSpec((channels, 8, PS), lambda i: (0, i, 0)),
+            out_specs=pl.BlockSpec((channels, step_rows, PS), lambda i: (0, i, 0)),
             scratch_shapes=[
                 pltpu.VMEM((groups, depth * 8, PS), BF16),
                 pltpu.VMEM((groups, depth * 4, PS), BF16),
             ],
         ),
         compiler_params=pltpu.CompilerParams(
-            dimension_semantics=("arbitrary",), vmem_limit_bytes=32 << 20
+            dimension_semantics=("arbitrary",)
         ),
     )(strips, weight, bias)
 
@@ -283,18 +306,19 @@
     buf0, buf1, extra = front(
         owner[None], routes_row, offs_rows, weights, taps, exposures, warp_rows, warp_cols, npatch
     )
+    first = lax.all_to_all(buf0, "patch", split_axis=0, concat_axis=0, tiled=True)
+    bits = npatch.bit_length() - 1
+    masks = [1 << bit for bit in [*range(3, bits), 1, 2, 0] if bit < bits]
+    second = extra[None]
+    for mask in masks:
+        second = jnp.concatenate([second, swap(second, "patch", mask)], axis=0)
     dest_all = routes_row.reshape(npatch, tiles)
     same = (dest_all[:, :, None] == dest_all[:, None, :]) & (
         jnp.arange(tiles)[None, :, None] > jnp.arange(tiles)[None, None, :]
     )
     repeats = jnp.max(jnp.sum(jnp.any(same, axis=2).astype(F32), axis=1))
-    repeats = lax.pmax(repeats, "band")
-    first = lax.all_to_all(buf0, "patch", split_axis=0, concat_axis=0, tiled=True)
-    second = lax.cond(
-        repeats <= 1.0,
-        lambda: lax.all_gather(extra, "patch"),
-        lambda: lax.all_to_all(buf1, "patch", split_axis=0, concat_axis=0, tiled=True),
-    )
+    for bit in range(nband.bit_length() - 1):
+        repeats = jnp.maximum(repeats, swap(repeats, "band", 1 << bit))
     landed = slot_select(dest_all == owner, capacity)
     corner = (offs_rows[0] * PS + offs_rows[1] + 1).reshape(npatch, tiles)
     table = jnp.sum(jnp.where(landed, corner[None], 0), axis=-1)
@@ -308,12 +332,23 @@
     row_cover = jnp.where((down >= 0) & (down < S), slot_weights[:, None], 0.0)
     col_cover = ((right >= 0) & (right < S)).astype(F32)
     cover = jnp.einsum("ky,kx->yx", row_cover, col_cover, precision=lax.Precision.HIGHEST)
-    coadd, strips = place(table, first, second, cover, nband)
-    strips = lax.all_to_all(strips, "band", split_axis=0, concat_axis=0, tiled=True)
     channels = det_weight.shape[0]
     strip_rows = PS // nband
     bias = jnp.broadcast_to(det_bias[:, None, None], (channels, 8, 1)).reshape(channels * 8, 1)
-    detection = detect(strips, toeplitz(det_weight, nband), bias, channels, strip_rows)
+    first, second, table, cover, kernel, bias, repeats = lax.optimization_barrier(
+        (first, second, table, cover, toeplitz(det_weight, nband), bias, repeats)
+    )
+
+    def one_repeat():
+        return place(owner[None], table, first, second, cover, nband, masks)
+
+    def any_repeats():
+        rest = lax.all_to_all(buf1, "patch", split_axis=0, concat_axis=0, tiled=True)
+        return place(owner[None], table, first, rest, cover, nband, None)
+
+    coadd, strips = lax.cond(repeats <= 1.0, one_repeat, any_repeats)
+    strips = lax.all_to_all(strips, "band", split_axis=0, concat_axis=0, tiled=True)
+    detection = detect(strips, kernel, bias, channels, strip_rows)
     return (coadd[None, None], detection[None])
 
 

time: 234 us -> 153 us (0.65)
  the two profiles are of different devices: /device:TPU:32 before, /device:TPU:96 now
where the time goes in v2:
time: 153 us; the launch traced here: 152 us
  waiting for transfers between devices  67.3 us (44%)
  starting transfers between devices  31.6 us (21%)
  Pallas kernels  21.8 us (14%)
  local copies, waits for them, and re-layouts  19.9 us (13%)
  other arithmetic  7.65 us (5%)
  between operations  2.83 us (2%)
    ppermute x8, waiting for transfers between devices, swap(): return lax.ppermute(x, axis, [(i, i ^ mask) for i in range(size)])  59.6 us
    ppermute x8, starting transfers between devices, swap(): return lax.ppermute(x, axis, [(i, i ^ mask) for i in range(size)])  15.7 us
    all_to_all x1, starting transfers between devices, body(): lax.all_to_all(buf0, 'patch', split_axis=0, concat_axis=0, tiled=True)  11.7 us
    pallas_call x1, Pallas kernels, front(): pl.pallas_call(lambda *refs: front_kernel(per_step, *refs), name='front',...  8.44 us
    all_to_all x1, waiting for transfers between devices, body(): lax.all_to_all(strips, 'band', split_axis=0, concat_axis=0, tiled=True)  7.74 us
    select_n x4, local copies, waits for them, and re-layouts, toeplitz(): total = jnp.where(on, taps[:, None, :, :, r, None], total)  6.82 us
    pallas_call x1, Pallas kernels, detect(): pl.pallas_call(lambda *refs: detect_kernel(nband, *refs), name='detect',...  6.75 us
    pallas_call x1, Pallas kernels, place(): pl.pallas_call(lambda *refs: place_kernel(per_step, nband, masks, *refs),...  6.64 us
  transfers between devices with their start and end apart: 10, of which 6 were waited for; matrix products, arithmetic and copies ran while one was open for 17% of the time, Pallas kernels for 0%

profile of v2, /device:TPU:96, one launch (start us, length us, event | category | flops | bytes accessed | tf_op | source)
XLA Modules:
  0.0 151.9 jit_solution(5734189457940088964)
XLA Ops:
  0.6 0.0 copy-start.3
  0.6 0.7 convert_bitcast_fusion
  1.3 0.6 reshape.306.refs_4_
  1.9 8.4 %front.1 = (bf16[64,128,128]{2,1,0:T(8,128)(2,1)}, bf16[64,128,128]{2,1,0:T(8,128)(2,1)}, bf16[128,128]{1,0:T(8,128)(2,1)}) custom-call(s32[1]{0:T(128)} %bitcast.4.refs_0_, s32[1,2048]{1,0:T(1,128)} %bitcast.52, s32[2,2048]{1,0:T(2,128)} %bitcast.48, f32[1,2048]{1,0:T(1,128)} %refs_3_.1, f32[14,32]{1,0:T(8,128)} %reshape.306.refs_4_, ...), custom_call_target="tpu_custom_call" | custom-call | tf_op jit(solution)/shard_map/front/pallas_call | solution.py:90
  10.4 0.2 collective-permute-start
  10.6 0.5 broadcast.326
  11.1 0.7 reduce.10
  11.8 0.1 reshape_reshape_transpose.3
  11.9 0.1 copy.45
  12.0 0.3 and_reduce_fusion
  12.2 0.6 reduce_max.9
  12.9 1.6 %collective-permute-start.6 = (f32[]{:T(128)}, f32[]{:T(128)}, u32[]{:S(2)}, u32[]{:S(2)}) collective-permute-start(f32[]{:T(128)} %reduce_max.9), channel_id=1, source_target_pairs={{0,1},{1,0},{2,3},{3,2},{4,5},{5,4},{6,7},{7,6},{8,9},{9,8},{10,11... | collective-permute-start | bytes 20 | tf_op jit(solution)/shard_map/ppermute | solution.py:124
  14.4 11.7 %all-to-all-start.1 = ((bf16[64,128,128]{2,1,0:T(8,128)(2,1)}), bf16[64,128,128]{2,1,0:T(8,128)(2,1)S(1)}, u32[]{:S(2)}, u32[]{:S(2)}) async-start(bf16[64,128,128]{2,1,0:T(8,128)(2,1)} %get-tuple-element.53), calls=%async_computation.1 | async-start | bytes 4194304 | tf_op jit(solution)/shard_map/all_to_all | solution.py:309
  26.2 0.0 copy-start.1
  26.3 0.1 copy.37
  26.5 2.4 %select_select_fusion = bf16[64,8,5,4,8]{1,0,4,3,2:T(8,128)(2,1)} fusion(pred[8,8]{0,1:T(8,128)(4,1)S(1)} %get-tuple-element.102, pred[8,8]{0,1:T(8,128)(4,1)S(1)} %get-tuple-element.103, pred[8,8]{0,1:T(8,128)(4,1)S(1)} %get-tuple-element.104, pred[8,8]{0,1:T(8,128)(4,1)S(1)} %get-tuple-element.105, pred[8,8]{0,1:T(8,128)(4,1)S(1)} %fusion.25, ...), kind=kLoop, calls=%fused_computation | loop fusion | flops 409600 | bytes 176960 | tf_op jit(solution)/shard_map/jit(_where)/select_n | solution.py:286
  28.8 0.1 fusion.30
  28.9 0.6 collective-permute-start.1
  29.6 1.0 select_select_fusion.1
  30.6 44.4 %collective-permute-done.1 = bf16[2,128,128]{2,1,0:T(8,128)(2,1)S(1)} collective-permute-done((bf16[2,128,128]{2,1,0:T(8,128)(2,1)S(1)}, bf16[2,128,128]{2,1,0:T(8,128)(2,1)S(1)}, u32[]{:S(2)}, u32[]{:S(2)}) %collective-permute-start.1) | collective-permute-done | bytes 65568 | tf_op jit(solution)/shard_map/ppermute | solution.py:124
  75.0 5.0 %collective-permute-start.2 = (bf16[4,128,128]{2,1,0:T(8,128)(2,1)S(1)}, bf16[4,128,128]{2,1,0:T(8,128)(2,1)S(1)}, u32[]{:S(2)}, u32[]{:S(2)}) collective-permute-start(bf16[4,128,128]{2,1,0:T(8,128)(2,1)S(1)} %pad_maximum_fusion.2), channel_id=1, source_target_pairs={{0,128},{4,132},{8,136},{12,140},{16,144},{20,148},{24,152},{28,15... | collective-permute-start | bytes 393224 | tf_op jit(solution)/shard_map/ppermute | solution.py:124
  80.0 0.6 constant_dynamic-update-slice_fusion.10
  80.7 6.4 %collective-permute-done.2 = bf16[4,128,128]{2,1,0:T(8,128)(2,1)S(1)} collective-permute-done((bf16[4,128,128]{2,1,0:T(8,128)(2,1)S(1)}, bf16[4,128,128]{2,1,0:T(8,128)(2,1)S(1)}, u32[]{:S(2)}, u32[]{:S(2)}) %collective-permute-start.2) | collective-permute-done | bytes 131104 | tf_op jit(solution)/shard_map/ppermute | solution.py:124
  87.1 1.5 collective-permute-start.3
  88.5 0.6 constant_dynamic-update-slice_fusion.9
  89.2 0.7 constant_dynamic-update-slice_fusion.8
  89.9 0.8 constant_dynamic-update-slice_fusion.7
  90.6 3.9 %collective-permute-done.3 = bf16[8,128,128]{2,1,0:T(8,128)(2,1)S(1)} collective-permute-done((bf16[8,128,128]{2,1,0:T(8,128)(2,1)S(1)}, bf16[8,128,128]{2,1,0:T(8,128)(2,1)S(1)}, u32[]{:S(2)}, u32[]{:S(2)}) %collective-permute-start.3) | collective-permute-done | bytes 262176 | tf_op jit(solution)/shard_map/ppermute | solution.py:124
  94.6 1.0 constant_dynamic-update-slice_fusion.6
  95.6 2.5 %collective-permute-start.4 = (bf16[16,128,128]{2,1,0:T(8,128)(2,1)}, bf16[16,128,128]{2,1,0:T(8,128)(2,1)}, u32[]{:S(2)}, u32[]{:S(2)}) collective-permute-start(bf16[16,128,128]{2,1,0:T(8,128)(2,1)} %get-tuple-element.71), channel_id=1, source_target_pairs={{0,16},{4,20},{8,24},{12,28},{16,0},{20,4},{24,8},{28,12},{32,48},... | collective-permute-start | bytes 1572872 | tf_op jit(solution)/shard_map/ppermute | solution.py:124
  98.1 2.0 %reshape.308 = bf16[512,80]{0,1:T(8,128)(2,1)S(1)} reshape(bf16[64,8,5,4,4]{1,0,4,3,2:T(8,128)(2,1)S(1)} %select_select_fusion.1) | data formatting | bytes 163840 | tf_op jit(solution)/shard_map/jit(_where)/select_n | solution.py:286
  100.1 0.1 copy.44
  100.2 0.0 copy-start.4
  100.3 4.5 %reshape.307 = bf16[512,160]{0,1:T(8,128)(2,1)S(1)} reshape(bf16[64,8,5,4,8]{1,0,4,3,2:T(8,128)(2,1)} %select_select_fusion) | data formatting | bytes 327680 | tf_op jit(solution)/shard_map/jit(_where)/select_n | solution.py:286
  104.8 0.1 copy.43
  105.0 0.2 reduce_window_sum.11
  105.2 0.1 copy.34
  105.2 0.1 copy.33
  105.4 0.1 add.68
  105.4 0.1 copy.35
  105.6 3.9 %collective-permute-done.4 = bf16[16,128,128]{2,1,0:T(8,128)(2,1)} collective-permute-done((bf16[16,128,128]{2,1,0:T(8,128)(2,1)}, bf16[16,128,128]{2,1,0:T(8,128)(2,1)}, u32[]{:S(2)}, u32[]{:S(2)}) %collective-permute-start.4) | collective-permute-done | bytes 524320 | tf_op jit(solution)/shard_map/ppermute | solution.py:124
  109.5 2.4 %constant_dynamic-update-slice_fusion.5 = (bf16[32,128,128]{2,1,0:T(8,128)(2,1)}, bf16[64,128,128]{2,1,0:T(8,128)(2,1)}) fusion(bf16[32,128,128]{2,1,0:T(8,128)(2,1)} %copy-done.6, bf16[16,128,128]{2,1,0:T(8,128)(2,1)} %collective-permute-done.4, bf16[64,128,128]{2,1,0:T(8,128)(2,1)} %get-tuple-element.70), kind=kLoop, calls=%fused_computation.28 | loop fusion | bytes 1572864 | tf_op jit(solution)/shard_map/concatenate | solution.py:314
  111.9 0.1 div.12
  112.0 0.1 rem.19
  112.1 0.1 ne.41
  112.2 0.5 broadcast.327
  112.7 0.7 reduce.11
  113.4 0.1 broadcast_in_dim.232
  113.4 0.1 copy.36
  113.5 0.1 broadcast_in_dim.235
  113.6 0.1 broadcast_in_dim.269
  113.7 0.1 broadcast_in_dim.270
  113.8 0.8 pad_maximum_fusion.1.refs_1_
  114.6 0.7 fusion.2
  116.7 4.3 %collective-permute-start.7 = (f32[]{:T(128)}, f32[]{:T(128)}, u32[]{:S(2)}, u32[]{:S(2)}) collective-permute-start(f32[]{:T(128)} %max.25), channel_id=1, source_target_pairs={{0,2},{1,3},{2,0},{3,1},{4,6},{5,7},{6,4},{7,5},{8,10},{9,11},{10,... | collective-permute-start | bytes 20 | tf_op jit(solution)/shard_map/ppermute | solution.py:124
  121.0 0.9 collective-permute-done.7
  122.6 2.4 %constant_dynamic-update-slice_fusion.11 = bf16[64,128,128]{2,1,0:T(8,128)(2,1)} fusion(bf16[64,128,128]{2,1,0:T(8,128)(2,1)} %get-tuple-element.68, bf16[32,128,128]{2,1,0:T(8,128)(2,1)} %collective-permute-done.5), kind=kLoop, calls=%fused_computation.34 | loop fusion | bytes 2097152 | tf_op jit(solution)/shard_map/concatenate | solution.py:314
  124.9 6.6 %conditional.1 = (bf16[4,136,512]{2,1,0:T(8,128)(2,1)}, bf16[1,1,512,512]{3,2,1,0:T(8,128)(2,1)}) conditional(s32[]{:T(128)} %convert_element_type.29, (s32[]{:T(128)}, bf16[64,128,128]{2,1,0:T(8,128)(2,1)}, s32[2,64]{1,0:T(2,128)S(1)}, bf16[64,128,128]{2,1,0:T(8,128)(2,1)S(1)}, f32[512,512]{1,0:T(8,128)S(1)}) %tuple.20, (s32[]{:T(128)}, ...), branch_computations={%region_6.7_spmd, %region_7.8_spmd} | conditional | bytes 4194320 | solution.py:349
  124.9 6.6 %place.3 = (bf16[512,512]{1,0:T(8,128)(2,1)}, bf16[4,136,512]{2,1,0:T(8,128)(2,1)}) custom-call(s32[1]{0:T(128)} %bitcast.2.refs_0_, s32[2,64]{1,0:T(2,128)S(1)} %get-tuple-element.33.refs_1_, bf16[64,128,128]{2,1,0:T(8,128)(2,1)S(1)} %get-tuple-element.34.refs_2_, bf16[64,128,128]{2,1,0:T(8,128)(2,1)} %get-tuple-element.35.refs_3_, ...), custom_call_target="tpu_custom_call" | custom-call | tf_op jit(solution)/shard_map/cond/branch_1_fun/place/pallas_call | solution.py:188
  131.6 4.2 %all-to-all-start.2 = ((bf16[4,136,512]{2,1,0:T(8,128)(2,1)}), bf16[4,136,512]{2,1,0:T(8,128)(2,1)S(1)}, u32[]{:S(2)}, u32[]{:S(2)}) async-start(bf16[4,136,512]{2,1,0:T(8,128)(2,1)} %get-tuple-element.62), calls=%async_computation.2 | async-start | bytes 1114112 | tf_op jit(solution)/shard_map/all_to_all | solution.py:350
  135.7 0.9 copy.47.refs_2_
  136.6 7.7 %all-to-all-done.2.refs_0_ = bf16[4,136,512]{2,1,0:T(8,128)(2,1)S(1)} async-done(((bf16[4,136,512]{2,1,0:T(8,128)(2,1)}), bf16[4,136,512]{2,1,0:T(8,128)(2,1)S(1)}, u32[]{:S(2)}, u32[]{:S(2)}) %all-to-all-start.2) | async-done | bytes 557088 | tf_op jit(solution)/shard_map/all_to_all | solution.py:350
  144.3 0.8 copy-done
  145.1 6.7 %detect.1 = bf16[64,128,512]{2,1,0:T(8,128)(2,1)} custom-call(bf16[4,136,512]{2,1,0:T(8,128)(2,1)} %copy-done, bf16[512,240]{1,0:T(8,128)(2,1)} %pad_maximum_fusion.1.refs_1_, f32[512,1]{1,0:T(8,128)} %copy.47.refs_2_), custom_call_target="tpu_custom_call" | custom-call | tf_op jit(solution)/shard_map/detect/pallas_call | solution.py:252
  (40 shorter events, 0.4 us)
Async XLA Ops:
  0.6 10.5 %copy-start.3 = (s32[1,2048,1]{1,2,0:T(1,128)S(1)}, s32[1,2048,1]{1,2,0:T(1,128)}, u32[]{:S(2)}) copy-start(s32[1,2048,1]{1,2,0:T(1,128)} %param.15) | copy-start | bytes 24580
  10.4 18.5 %collective-permute-start = (bf16[1,128,128]{2,1,0:T(8,128)(2,1)}, bf16[1,128,128]{2,1,0:T(8,128)(2,1)S(1)}, u32[]{:S(2)}, u32[]{:S(2)}) collective-permute-start(bf16[1,128,128]{2,1,0:T(8,128)(2,1)} %bitcast.43), channel_id=1, source_target_pairs={{0,32},{4,36},{8,40},{12,44},{16,48},{20,52},{24,56},{28,60},{32,0... | collective-permute-start | bytes 98312 | tf_op jit(solution)/shard_map/ppermute | solution.py:124
  12.9 102.5 %collective-permute-start.6 = (f32[]{:T(128)}, f32[]{:T(128)}, u32[]{:S(2)}, u32[]{:S(2)}) collective-permute-start(f32[]{:T(128)} %reduce_max.9), channel_id=1, source_target_pairs={{0,1},{1,0},{2,3},{3,2},{4,5},{5,4},{6,7},{7,6},{8,9},{9,8},{10,11... | collective-permute-start | bytes 20 | tf_op jit(solution)/shard_map/ppermute | solution.py:124
  14.4 11.8 %copy-start.5 = (bf16[64,100]{1,0:T(8,128)(2,1)S(1)}, bf16[64,100]{1,0:T(8,128)(2,1)}, u32[]{:S(2)}) copy-start(bf16[64,100]{1,0:T(8,128)(2,1)} %param.18) | copy-start | bytes 38404
  14.4 110.5 %all-to-all-start.1 = ((bf16[64,128,128]{2,1,0:T(8,128)(2,1)}), bf16[64,128,128]{2,1,0:T(8,128)(2,1)S(1)}, u32[]{:S(2)}, u32[]{:S(2)}) async-start(bf16[64,128,128]{2,1,0:T(8,128)(2,1)} %get-tuple-element.53), calls=%async_computation.1 | async-start | bytes 4194304 | tf_op jit(solution)/shard_map/all_to_all | solution.py:309
  26.2 2.7 %copy-start.1 = (bf16[128,128]{1,0:T(8,128)(2,1)S(1)}, bf16[128,128]{1,0:T(8,128)(2,1)}, u32[]{:S(2)}) copy-start(bf16[128,128]{1,0:T(8,128)(2,1)} %get-tuple-element.54) | copy-start | bytes 98308
  28.9 46.0 %collective-permute-start.1 = (bf16[2,128,128]{2,1,0:T(8,128)(2,1)S(1)}, bf16[2,128,128]{2,1,0:T(8,128)(2,1)S(1)}, u32[]{:S(2)}, u32[]{:S(2)}) collective-permute-start(bf16[2,128,128]{2,1,0:T(8,128)(2,1)S(1)} %pad_maximum_fusion.3), channel_id=1, source_target_pairs={{0,64},{4,68},{8,72},{12,76},{16,80},{20,84},{24,88},{28,92},{32,9... | collective-permute-start | bytes 196616 | tf_op jit(solution)/shard_map/ppermute | solution.py:124
  75.0 12.1 %collective-permute-start.2 = (bf16[4,128,128]{2,1,0:T(8,128)(2,1)S(1)}, bf16[4,128,128]{2,1,0:T(8,128)(2,1)S(1)}, u32[]{:S(2)}, u32[]{:S(2)}) collective-permute-start(bf16[4,128,128]{2,1,0:T(8,128)(2,1)S(1)} %pad_maximum_fusion.2), channel_id=1, source_target_pairs={{0,128},{4,132},{8,136},{12,140},{16,144},{20,148},{24,152},{28,15... | collective-permute-start | bytes 393224 | tf_op jit(solution)/shard_map/ppermute | solution.py:124
  87.1 7.5 %collective-permute-start.3 = (bf16[8,128,128]{2,1,0:T(8,128)(2,1)S(1)}, bf16[8,128,128]{2,1,0:T(8,128)(2,1)S(1)}, u32[]{:S(2)}, u32[]{:S(2)}) collective-permute-start(bf16[8,128,128]{2,1,0:T(8,128)(2,1)S(1)} %pad_maximum_fusion), channel_id=1, source_target_pairs={{0,8},{4,12},{8,0},{12,4},{16,24},{20,28},{24,16},{28,20},{32,40},... | collective-permute-start | bytes 786440 | tf_op jit(solution)/shard_map/ppermute | solution.py:124
  95.6 2.5 %copy-start.6 = (bf16[32,128,128]{2,1,0:T(8,128)(2,1)}, bf16[32,128,128]{2,1,0:T(8,128)(2,1)S(1)}, u32[]{:S(2)}) copy-start(bf16[32,128,128]{2,1,0:T(8,128)(2,1)S(1)} %get-tuple-element.69) | copy-start | bytes 3145732
  95.6 13.9 %collective-permute-start.4 = (bf16[16,128,128]{2,1,0:T(8,128)(2,1)}, bf16[16,128,128]{2,1,0:T(8,128)(2,1)}, u32[]{:S(2)}, u32[]{:S(2)}) collective-permute-start(bf16[16,128,128]{2,1,0:T(8,128)(2,1)} %get-tuple-element.71), channel_id=1, source_target_pairs={{0,16},{4,20},{8,24},{12,28},{16,0},{20,4},{24,8},{28,12},{32,48},... | collective-permute-start | bytes 1572872 | tf_op jit(solution)/shard_map/ppermute | solution.py:124
  100.1 5.2 %copy-start.2 = (s32[1,2048,2]{1,2,0:T(2,128)S(1)}, s32[1,2048,2]{1,2,0:T(2,128)}, u32[]{:S(2)}) copy-start(s32[1,2048,2]{1,2,0:T(2,128)} %param.16) | copy-start | bytes 49156
  100.2 12.4 %copy-start.4 = (f32[1,2048]{1,0:T(1,128)S(1)}, f32[1,2048]{1,0:T(1,128)}, u32[]{:S(2)}) copy-start(f32[1,2048]{1,0:T(1,128)} %refs_3_.1) | copy-start | bytes 24580
  100.2 13.4 %copy-start.7 = (f32[64]{0:T(128)S(1)}, f32[64]{0:T(128)}, u32[]{:S(2)}) copy-start(f32[64]{0:T(128)} %param.19) | copy-start | bytes 772
  111.9 10.6 %collective-permute-start.5 = (bf16[32,128,128]{2,1,0:T(8,128)(2,1)}, bf16[32,128,128]{2,1,0:T(8,128)(2,1)}, u32[]{:S(2)}, u32[]{:S(2)}) collective-permute-start(bf16[32,128,128]{2,1,0:T(8,128)(2,1)} %get-tuple-element.67), channel_id=1, source_target_pairs={{0,4},{4,0},{8,12},{12,8},{16,20},{20,16},{24,28},{28,24},{32,36},... | collective-permute-start | bytes 3145736 | tf_op jit(solution)/shard_map/ppermute | solution.py:124
  116.7 5.2 %collective-permute-start.7 = (f32[]{:T(128)}, f32[]{:T(128)}, u32[]{:S(2)}, u32[]{:S(2)}) collective-permute-start(f32[]{:T(128)} %max.25), channel_id=1, source_target_pairs={{0,2},{1,3},{2,0},{3,1},{4,6},{5,7},{6,4},{7,5},{8,10},{9,11},{10,... | collective-permute-start | bytes 20 | tf_op jit(solution)/shard_map/ppermute | solution.py:124
  131.6 12.8 %all-to-all-start.2 = ((bf16[4,136,512]{2,1,0:T(8,128)(2,1)}), bf16[4,136,512]{2,1,0:T(8,128)(2,1)S(1)}, u32[]{:S(2)}, u32[]{:S(2)}) async-start(bf16[4,136,512]{2,1,0:T(8,128)(2,1)} %get-tuple-element.62), calls=%async_computation.2 | async-start | bytes 1114112 | tf_op jit(solution)/shard_map/all_to_all | solution.py:350
  144.3 0.8 copy-start

commit v3 on v2

--- a/solution.py
+++ b/solution.py
@@ -24,9 +24,88 @@
     return lax.dot_general(a, b, (((1,), (0,)), ((), ())), preferred_element_type=F32)
 
 
+def warp_tiles(here, base, offs_ref, wts_ref, taps_ref, tiles, rows, cols):
+    diag = lax.broadcasted_iota(jnp.int32, (S, S), 1) - lax.broadcasted_iota(jnp.int32, (S, S), 0)
+
+    def band(first_tap, tile):
+        matrix = jnp.zeros((S, S), F32)
+        for tap in range(TAPS):
+            matrix = jnp.where(diag == tap - HALF, taps_ref[first_tap + tap, tile], matrix)
+        return matrix.astype(BF16)
+
+    each = range(len(here))
+    psf_rows = [band(0, t) for t in here]
+    psf_cols = [band(TAPS, t) for t in here]
+    half_done = [dot_nt(tiles[k], psf_cols[k]).astype(BF16) for k in each]
+    matched = [dot_nn(psf_rows[k], half_done[k]).astype(BF16) for k in each]
+    across = [dot_nt(matched[k], cols[k]).astype(BF16) for k in each]
+    product = [dot_nn(rows[k], across[k]) for k in each]
+    out = []
+    for k in each:
+        place = base + here[k]
+        warped = wts_ref[0, place] * product[k]
+        warped = pltpu.roll(warped, offs_ref[1, place] & (LANES - 1), 1)
+        warped = pltpu.roll(warped, offs_ref[0, place] & 7, 0)
+        out.append(warped.astype(BF16))
+    return out
+
+
+def repeat_kernel(
+    tiles, owner_ref, routes_ref, offs_ref, wts_ref, taps_ref,
+    exp_ref, rows_ref, cols_ref, out_ref, held, count, found, sems,
+):
+    base = owner_ref[0] * tiles
+    found[0] = 0
+
+    @pl.loop(0, count.shape[0])
+    def _(i):
+        count[i] = 0
+
+    @pl.loop(0, tiles)
+    def _(i):
+        dest = routes_ref[0, base + i]
+        rank = count[dest]
+        count[dest] = rank + 1
+        found[0] = jnp.where(rank > 0, i, found[0])
+
+    tile = found[0]
+    copies = [
+        pltpu.make_async_copy(src.at[tile, 0], held.at[i], sems.at[i])
+        for i, src in enumerate((exp_ref, rows_ref, cols_ref))
+    ]
+    for copy in copies:
+        copy.start()
+    for copy in copies:
+        copy.wait()
+    out_ref[0] = warp_tiles(
+        [tile], base, offs_ref, wts_ref, taps_ref, [held[0]], [held[1]], [held[2]]
+    )[0]
+
+
+def repeat(owner, routes, offs, wts, taps, exposures, warp_rows, warp_cols, npatch):
+    anywhere = pl.BlockSpec(memory_space=pl.ANY)
+    return pl.pallas_call(
+        lambda *refs: repeat_kernel(exposures.shape[0], *refs),
+        name="repeat",
+        out_shape=jax.ShapeDtypeStruct((1, S, S), BF16),
+        grid_spec=pltpu.PrefetchScalarGridSpec(
+            num_scalar_prefetch=5,
+            grid=(1,),
+            in_specs=[anywhere] * 3,
+            out_specs=pl.BlockSpec((1, S, S), lambda i, *_: (0, 0, 0)),
+            scratch_shapes=[
+                pltpu.VMEM((3, S, S), BF16),
+                pltpu.SMEM((npatch,), jnp.int32),
+                pltpu.SMEM((1,), jnp.int32),
+                pltpu.SemaphoreType.DMA((3,)),
+            ],
+        ),
+    )(owner, routes, offs, wts, taps, exposures, warp_rows, warp_cols)
+
+
 def front_kernel(
     per_step, owner_ref, routes_ref, offs_ref, wts_ref, taps_ref,
-    exp_ref, rows_ref, cols_ref, buf0_ref, buf1_ref, extra_ref, stage, count, sems,
+    exp_ref, rows_ref, cols_ref, buf0_ref, buf1_ref, stage, count, sems,
 ):
     step = pl.program_id(0)
     steps = pl.num_programs(0)
@@ -39,41 +118,23 @@
         def _(i):
             count[i] = 0
 
-    diag = lax.broadcasted_iota(jnp.int32, (S, S), 1) - lax.broadcasted_iota(jnp.int32, (S, S), 0)
-
-    def band(first_tap, tile):
-        matrix = jnp.zeros((S, S), F32)
-        for tap in range(TAPS):
-            matrix = jnp.where(diag == tap - HALF, taps_ref[first_tap + tap, tile], matrix)
-        return matrix.astype(BF16)
-
-    each = range(per_step)
-    here = [step * per_step + k for k in each]
-    psf_rows = [band(0, t) for t in here]
-    psf_cols = [band(TAPS, t) for t in here]
-    half_done = [dot_nt(exp_ref[k], psf_cols[k]).astype(BF16) for k in each]
-    matched = [dot_nn(psf_rows[k], half_done[k]).astype(BF16) for k in each]
-    across = [dot_nt(matched[k], cols_ref[k]).astype(BF16) for k in each]
-    product = [dot_nn(rows_ref[k], across[k]) for k in each]
-    for k in each:
-        place = base + here[k]
-        warped = wts_ref[0, place] * product[k]
-        warped = pltpu.roll(warped, offs_ref[1, place] & (LANES - 1), 1)
-        warped = pltpu.roll(warped, offs_ref[0, place] & 7, 0)
-        stage[here[k]] = warped.astype(BF16)
-    for k in each:
-        dest = routes_ref[0, base + here[k]]
+    here = [step * per_step + k for k in range(per_step)]
+    inputs = [[ref[k] for k in range(per_step)] for ref in (exp_ref, rows_ref, cols_ref)]
+    warped = warp_tiles(here, base, offs_ref, wts_ref, taps_ref, *inputs)
+    for tile, value in zip(here, warped):
+        stage[tile] = value
+    for tile in here:
+        dest = routes_ref[0, base + tile]
         rank = count[dest]
         count[dest] = rank + 1
 
         @pl.when(rank == 0)
         def _():
-            pltpu.make_async_copy(stage.at[here[k]], buf0_ref.at[dest], sems.at[here[k]]).start()
+            pltpu.make_async_copy(stage.at[tile], buf0_ref.at[dest], sems.at[tile]).start()
 
         @pl.when(rank > 0)
         def _():
-            extra_ref[...] = stage[here[k]]
-            pltpu.make_async_copy(stage.at[here[k]], buf1_ref.at[dest], sems.at[here[k]]).start()
+            pltpu.make_async_copy(stage.at[tile], buf1_ref.at[dest], sems.at[tile]).start()
 
     @pl.when(step == steps - 1)
     def _():
@@ -93,13 +154,13 @@
         out_shape=(
             jax.ShapeDtypeStruct((npatch, S, S), BF16),
             jax.ShapeDtypeStruct((npatch, S, S), BF16),
-            jax.ShapeDtypeStruct((S, S), BF16),
-        ),
+        ),
+        cost_estimate=pl.CostEstimate(flops=0, bytes_accessed=24 << 20, transcendentals=0),
         grid_spec=pltpu.PrefetchScalarGridSpec(
             num_scalar_prefetch=5,
             grid=(tiles // per_step,),
             in_specs=[spec, spec, spec],
-            out_specs=(anywhere, anywhere, pl.BlockSpec((S, S), lambda i, *_: (0, 0))),
+            out_specs=(anywhere, anywhere),
             scratch_shapes=[
                 pltpu.VMEM((tiles, S, S), BF16),
                 pltpu.SMEM((npatch,), jnp.int32),
@@ -124,7 +185,8 @@
     return lax.ppermute(x, axis, [(i, i ^ mask) for i in range(size)])
 
 
-def place_kernel(per_step, nband, masks, owner_ref, table_ref, first_ref, second_ref, cover_ref, coadd_ref, strip_ref, acc, full):
+def place_kernel(per_step, nband, masks, owner_ref, table_ref, first_ref, *refs):
+    *second_refs, cover_ref, coadd_ref, strip_ref, acc, full = refs
     step = pl.program_id(0)
     steps = pl.num_programs(0)
     strip_rows = PS // nband
@@ -136,12 +198,14 @@
 
     lane = lax.broadcasted_iota(jnp.int32, (8, LANES), 1)
     sub = lax.broadcasted_iota(jnp.int32, (8, LANES), 0)
-    for slot, src in ((0, first_ref), (1, second_ref)):
-        for k in range(per_step):
-            source = step * per_step + k
-            if slot == 1 and masks:
+    for slot, src in ((0, first_ref), *((1 + i, ref) for i, ref in enumerate(second_refs))):
+        for k in range(src.shape[0]):
+            source = step * src.shape[0] + k
+            if slot > 1:
+                source = source + (slot - 1) * src.shape[0] * steps
+            if slot and masks:
                 source = owner_ref[0] ^ spread(source, masks)
-            code = table_ref[slot, source]
+            code = table_ref[min(slot, 1), source]
 
             @pl.when(code > 0)
             def _():
@@ -180,11 +244,13 @@
             strip_ref[b] = full[start : start + strip_ref.shape[1], :].astype(BF16)
 
 
-def place(owner, table, first, second, cover, nband, masks):
-    slots = first.shape[0]
+def place(owner, table, first, seconds, cover, nband, masks):
     per_step = 16
+    steps = first.shape[0] // per_step
     strip = PS // nband + 8
-    spec = pl.BlockSpec((per_step, S, S), lambda i, *_: (i, 0, 0))
+    specs = [
+        pl.BlockSpec((x.shape[0] // steps, S, S), lambda i, *_: (i, 0, 0)) for x in (first, *seconds)
+    ]
     return pl.pallas_call(
         lambda *refs: place_kernel(per_step, nband, masks, *refs),
         name="place",
@@ -194,8 +260,8 @@
         ),
         grid_spec=pltpu.PrefetchScalarGridSpec(
             num_scalar_prefetch=2,
-            grid=(slots // per_step,),
-            in_specs=[spec, spec, pl.BlockSpec((PS, PS), lambda i, *_: (0, 0))],
+            grid=(steps,),
+            in_specs=[*specs, pl.BlockSpec((PS, PS), lambda i, *_: (0, 0))],
             out_specs=(
                 pl.BlockSpec((PS, PS), lambda i, *_: (0, 0)),
                 pl.BlockSpec((nband, strip, PS), lambda i, *_: (0, 0, 0)),
@@ -208,7 +274,7 @@
         compiler_params=pltpu.CompilerParams(
             dimension_semantics=("arbitrary",)
         ),
-    )(owner, table, first, second, cover)
+    )(owner, table, first, *seconds, cover)
 
 
 def detect_kernel(nband, strip_ref, weight_ref, bias_ref, out_ref, main, edge):
@@ -303,15 +369,16 @@
     routes_row = routes.transpose(0, 2, 1).reshape(1, -1)
     offs_rows = offsets.transpose(0, 2, 1).reshape(2, -1)
     taps = psf_taps[:, 0].transpose(1, 2, 0).reshape(2 * TAPS, tiles).astype(F32)
-    buf0, buf1, extra = front(
-        owner[None], routes_row, offs_rows, weights, taps, exposures, warp_rows, warp_cols, npatch
-    )
-    first = lax.all_to_all(buf0, "patch", split_axis=0, concat_axis=0, tiled=True)
+    inputs = (owner[None], routes_row, offs_rows, weights, taps, exposures, warp_rows, warp_cols)
+    near = repeat(*inputs, npatch)
     bits = npatch.bit_length() - 1
     masks = [1 << bit for bit in [*range(3, bits), 1, 2, 0] if bit < bits]
-    second = extra[None]
-    for mask in masks:
-        second = jnp.concatenate([second, swap(second, "patch", mask)], axis=0)
+    for mask in masks[:-3]:
+        near = jnp.concatenate([near, swap(near, "patch", mask)], axis=0)
+    buf0, buf1 = front(*inputs, npatch)
+    buf0, near = lax.optimization_barrier((buf0, near))
+    near = jnp.concatenate([near] + [swap(near, "patch", m) for m in (2, 4, 6)], axis=0)
+    first = lax.all_to_all(buf0, "patch", split_axis=0, concat_axis=0, tiled=True)
     dest_all = routes_row.reshape(npatch, tiles)
     same = (dest_all[:, :, None] == dest_all[:, None, :]) & (
         jnp.arange(tiles)[None, :, None] > jnp.arange(tiles)[None, None, :]
@@ -335,16 +402,18 @@
     channels = det_weight.shape[0]
     strip_rows = PS // nband
     bias = jnp.broadcast_to(det_bias[:, None, None], (channels, 8, 1)).reshape(channels * 8, 1)
-    first, second, table, cover, kernel, bias, repeats = lax.optimization_barrier(
-        (first, second, table, cover, toeplitz(det_weight, nband), bias, repeats)
+    first, near = lax.optimization_barrier((first, near))
+    far = swap(near, "patch", 1)
+    first, far, table, cover, kernel, bias, repeats = lax.optimization_barrier(
+        (first, far, table, cover, toeplitz(det_weight, nband), bias, repeats)
     )
 
     def one_repeat():
-        return place(owner[None], table, first, second, cover, nband, masks)
+        return place(owner[None], table, first, (near, far), cover, nband, masks)
 
     def any_repeats():
         rest = lax.all_to_all(buf1, "patch", split_axis=0, concat_axis=0, tiled=True)
-        return place(owner[None], table, first, rest, cover, nband, None)
+        return place(owner[None], table, first, (rest,), cover, nband, None)
 
     coadd, strips = lax.cond(repeats <= 1.0, one_repeat, any_repeats)
     strips = lax.all_to_all(strips, "band", split_axis=0, concat_axis=0, tiled=True)

time: 153 us -> 135 us (0.88)
  the two profiles are of different devices: /device:TPU:96 before, /device:TPU:32 now
where the time goes in v3:
time: 135 us; the launch traced here: 134 us
  waiting for transfers between devices  48 us (36%)
  starting transfers between devices  34.2 us (25%)
  Pallas kernels  24.5 us (18%)
  other arithmetic  12 us (9%)
  local copies, waits for them, and re-layouts  12 us (9%)
  between operations  2.79 us (2%)
    ppermute x9, waiting for transfers between devices, swap(): return lax.ppermute(x, axis, [(i, i ^ mask) for i in range(size)])  24.7 us
    ppermute x9, starting transfers between devices, swap(): return lax.ppermute(x, axis, [(i, i ^ mask) for i in range(size)])  21.6 us
    all_to_all x1, waiting for transfers between devices, body(): lax.all_to_all(buf0, 'patch', split_axis=0, concat_axis=0, tiled=True)  13.9 us
    all_to_all x1, waiting for transfers between devices, body(): lax.all_to_all(strips, 'band', split_axis=0, concat_axis=0, tiled=True)  9.39 us
    all_to_all x1, starting transfers between devices, body(): lax.all_to_all(buf0, 'patch', split_axis=0, concat_axis=0, tiled=True)  7.97 us
    pallas_call x1, Pallas kernels, front(): pl.pallas_call(lambda *refs: front_kernel(per_step, *refs), name='front',...  7.59 us
    select_n x4, local copies, waits for them, and re-layouts, toeplitz(): total = jnp.where(on, taps[:, None, :, :, r, None], total)  6.82 us
    pallas_call x1, Pallas kernels, detect(): pl.pallas_call(lambda *refs: detect_kernel(nband, *refs), name='detect',...  6.75 us
  transfers between devices with their start and end apart: 11, of which 6 were waited for; matrix products, arithmetic and copies ran while one was open for 15% of the time, Pallas kernels for 6%

profile of v3, /device:TPU:32, one launch (start us, length us, event | category | flops | bytes accessed | tf_op | source)
XLA Modules:
  0.0 134.3 jit_solution(1729508280048127476)
XLA Ops:
  0.6 0.7 convert_bitcast_fusion
  1.3 0.6 reshape.306.refs_4_
  1.9 4.2 %repeat.1 = bf16[1,128,128]{2,1,0:T(8,128)(2,1)} custom-call(s32[1]{0:T(128)} %bitcast.4.refs_0_, s32[1,2048]{1,0:T(1,128)} %bitcast.43, s32[2,2048]{1,0:T(2,128)} %bitcast.40, f32[1,2048]{1,0:T(1,128)} %refs_3_.3, f32[14,32]{1,0:T(8,128)} %reshape.306.refs_4_, bf16[32,1,128,128]{3,2,1,0:T(8,128)(2,1)} %refs_5_.3, bf16[32,1,128,128]{3,2,1,0:T(8,128)(2,1)} %refs_6_.3, ...), custom_call_target="tpu_custom_call" | custom-call | tf_op jit(solution)/shard_map/repeat/pallas_call | solution.py:87
  6.2 0.0 copy-start.1
  6.2 1.9 %collective-permute-start = (bf16[1,128,128]{2,1,0:T(8,128)(2,1)}, bf16[1,128,128]{2,1,0:T(8,128)(2,1)S(1)}, u32[]{:S(2)}, u32[]{:S(2)}) collective-permute-start(bf16[1,128,128]{2,1,0:T(8,128)(2,1)} %repeat.1), channel_id=1, source_target_pairs={{0,32},{4,36},{8,40},{12,44},{16,48},{20,52},{24,56},{28,60},{32,0... | collective-permute-start | bytes 98312 | tf_op jit(solution)/shard_map/ppermute | solution.py:185
  8.1 2.3 %collective-permute-done = bf16[1,128,128]{2,1,0:T(8,128)(2,1)S(1)} collective-permute-done((bf16[1,128,128]{2,1,0:T(8,128)(2,1)}, bf16[1,128,128]{2,1,0:T(8,128)(2,1)S(1)}, u32[]{:S(2)}, u32[]{:S(2)}) %collective-permute-start) | collective-permute-done | bytes 32800 | tf_op jit(solution)/shard_map/ppermute | solution.py:185
  10.4 0.8 pad_maximum_fusion.4
  11.2 3.3 %collective-permute-start.1 = (bf16[2,128,128]{2,1,0:T(8,128)(2,1)S(1)}, bf16[2,128,128]{2,1,0:T(8,128)(2,1)S(1)}, u32[]{:S(2)}, u32[]{:S(2)}) collective-permute-start(bf16[2,128,128]{2,1,0:T(8,128)(2,1)S(1)} %pad_maximum_fusion.4), channel_id=1, source_target_pairs={{0,64},{4,68},{8,72},{12,76},{16,80},{20,84},{24,88},{28,92},{32,9... | collective-permute-start | bytes 196616 | tf_op jit(solution)/shard_map/ppermute | solution.py:185
  14.4 2.3 %collective-permute-done.1 = bf16[2,128,128]{2,1,0:T(8,128)(2,1)S(1)} collective-permute-done((bf16[2,128,128]{2,1,0:T(8,128)(2,1)S(1)}, bf16[2,128,128]{2,1,0:T(8,128)(2,1)S(1)}, u32[]{:S(2)}, u32[]{:S(2)}) %collective-permute-start.1) | collective-permute-done | bytes 65568 | tf_op jit(solution)/shard_map/ppermute | solution.py:185
  16.8 0.8 pad_maximum_fusion.3
  17.5 6.1 %collective-permute-start.2 = (bf16[4,128,128]{2,1,0:T(8,128)(2,1)S(1)}, bf16[4,128,128]{2,1,0:T(8,128)(2,1)S(1)}, u32[]{:S(2)}, u32[]{:S(2)}) collective-permute-start(bf16[4,128,128]{2,1,0:T(8,128)(2,1)S(1)} %pad_maximum_fusion.3), channel_id=1, source_target_pairs={{0,128},{4,132},{8,136},{12,140},{16,144},{20,148},{24,152},{28,15... | collective-permute-start | bytes 393224 | tf_op jit(solution)/shard_map/ppermute | solution.py:185
  23.6 7.6 %front.1 = (bf16[64,128,128]{2,1,0:T(8,128)(2,1)}, bf16[64,128,128]{2,1,0:T(8,128)(2,1)}) custom-call(s32[1]{0:T(128)} %bitcast.4.refs_0_, s32[1,2048]{1,0:T(1,128)} %bitcast.44, s32[2,2048]{1,0:T(2,128)} %bitcast.41, f32[1,2048]{1,0:T(1,128)} %refs_3_.3, f32[14,32]{1,0:T(8,128)} %reshape.306.refs_4_, bf16[32,1,128,128]{3,2,1,0:T(8,128)(2,1)} %refs_5_.3, ...), custom_call_target="tpu_custom_call" | custom-call | bytes 25165824 | tf_op jit(solution)/shard_map/front/pallas_call | solution.py:151
  31.2 0.7 pad_maximum_fusion.1
  31.9 8.0 %all-to-all-start.1 = ((bf16[64,128,128]{2,1,0:T(8,128)(2,1)}), bf16[64,128,128]{2,1,0:T(8,128)(2,1)S(1)}, u32[]{:S(2)}, u32[]{:S(2)}) async-start(bf16[64,128,128]{2,1,0:T(8,128)(2,1)} %get-tuple-element.60), calls=%async_computation.1 | async-start | bytes 4194304 | tf_op jit(solution)/shard_map/all_to_all | solution.py:381
  39.9 0.0 copy-start.6
  39.9 0.6 broadcast.326
  40.5 0.6 reduce.10
  41.2 0.1 reshape_reshape_transpose.3
  41.2 0.1 copy.45
  41.3 0.2 and_reduce_fusion
  41.6 0.6 reduce_max.9
  42.2 1.6 %collective-permute-start.7 = (f32[]{:T(128)}, f32[]{:T(128)}, u32[]{:S(2)}, u32[]{:S(2)}) collective-permute-start(f32[]{:T(128)} %reduce_max.9), channel_id=1, source_target_pairs={{0,1},{1,0},{2,3},{3,2},{4,5},{5,4},{6,7},{7,6},{8,9},{9,8},{10,11... | collective-permute-start | bytes 20 | tf_op jit(solution)/shard_map/ppermute | solution.py:185
  43.8 0.6 broadcast.327
  44.3 0.6 reduce.11
  45.0 0.2 reduce_window_sum.11
  45.2 0.1 copy.34
  45.3 0.1 copy.33
  45.4 0.0 copy-done.2
  45.4 0.1 add.68
  45.5 0.1 copy.35
  45.6 0.1 broadcast_in_dim.228
  45.6 0.1 copy.36
  45.7 0.1 copy.37
  46.0 0.1 fusion.30
  46.1 1.0 select_select_fusion.1
  47.1 2.8 %collective-permute-start.5 = (bf16[8,128,128]{2,1,0:T(8,128)(2,1)}, bf16[8,128,128]{2,1,0:T(8,128)(2,1)}, u32[]{:S(2)}, u32[]{:S(2)}) collective-permute-start(bf16[8,128,128]{2,1,0:T(8,128)(2,1)} %pad_maximum_fusion.1), channel_id=1, source_target_pairs={{0,24},{4,28},{8,16},{12,20},{16,8},{20,12},{24,0},{28,4},{32,56},... | collective-permute-start | bytes 786440 | tf_op jit(solution)/shard_map/ppermute | solution.py:185
  49.9 0.9 collective-permute-start.4
  50.8 0.6 collective-permute-start.3
  51.3 0.1 ne.41
  51.4 0.1 div.12
  51.5 0.6 rem.19
  52.1 0.1 broadcast_in_dim.231
  52.2 0.1 broadcast_in_dim.265
  52.3 0.1 broadcast_in_dim.266
  52.3 2.0 %reshape.308 = bf16[512,80]{0,1:T(8,128)(2,1)S(1)} reshape(bf16[64,8,5,4,4]{1,0,4,3,2:T(8,128)(2,1)S(1)} %select_select_fusion.1) | data formatting | bytes 163840 | tf_op jit(solution)/shard_map/jit(_where)/select_n | solution.py:352
  54.4 0.1 copy.44
  54.5 19.6 %collective-permute-done.5 = bf16[8,128,128]{2,1,0:T(8,128)(2,1)} collective-permute-done((bf16[8,128,128]{2,1,0:T(8,128)(2,1)}, bf16[8,128,128]{2,1,0:T(8,128)(2,1)}, u32[]{:S(2)}, u32[]{:S(2)}) %collective-permute-start.5) | collective-permute-done | bytes 262176 | tf_op jit(solution)/shard_map/ppermute | solution.py:185
  74.1 2.3 %pad_maximum_fusion = bf16[32,128,128]{2,1,0:T(8,128)(2,1)} fusion(bf16[8,128,128]{2,1,0:T(8,128)(2,1)} %collective-permute-done.5, bf16[8,128,128]{2,1,0:T(8,128)(2,1)} %collective-permute-done.4, bf16[8,128,128]{2,1,0:T(8,128)(2,1)} %collective-permute-done.3, bf16[8,128,128]{2,1,0:T(8,128)(2,1)} %pad_maximum_fusion.1), kind=kLoop, calls=%fused_computation.2 | loop fusion | flops 1572864 | bytes 2097152 | tf_op jit(solution)/shard_map/concatenate | solution.py:380
  76.4 13.9 %all-to-all-done.1 = bf16[64,128,128]{2,1,0:T(8,128)(2,1)S(1)} async-done(((bf16[64,128,128]{2,1,0:T(8,128)(2,1)}), bf16[64,128,128]{2,1,0:T(8,128)(2,1)S(1)}, u32[]{:S(2)}, u32[]{:S(2)}) %all-to-all-start.1) | async-done | bytes 2097184 | tf_op jit(solution)/shard_map/all_to_all | solution.py:381
  90.3 0.0 collective-permute-start.6
  90.3 2.4 %select_select_fusion = bf16[64,8,5,4,8]{1,0,4,3,2:T(8,128)(2,1)} fusion(pred[8,8]{0,1:T(8,128)(4,1)S(1)} %get-tuple-element.94, pred[8,8]{0,1:T(8,128)(4,1)S(1)} %get-tuple-element.95, pred[8,8]{0,1:T(8,128)(4,1)S(1)} %get-tuple-element.96, pred[8,8]{0,1:T(8,128)(4,1)S(1)} %get-tuple-element.97, pred[8,8]{0,1:T(8,128)(4,1)S(1)} %fusion.25, ...), kind=kLoop, calls=%fused_computation | loop fusion | flops 409600 | bytes 176960 | tf_op jit(solution)/shard_map/jit(_where)/select_n | solution.py:352
  92.7 4.5 %reshape.307 = bf16[512,160]{0,1:T(8,128)(2,1)S(1)} reshape(bf16[64,8,5,4,8]{1,0,4,3,2:T(8,128)(2,1)} %select_select_fusion) | data formatting | bytes 327680 | tf_op jit(solution)/shard_map/jit(_where)/select_n | solution.py:352
  97.2 0.1 copy.43
  97.4 0.8 pad_maximum_fusion.2.refs_1_
  98.2 0.7 fusion.2
  100.2 4.6 %collective-permute-start.8 = (f32[]{:T(128)}, f32[]{:T(128)}, u32[]{:S(2)}, u32[]{:S(2)}) collective-permute-start(f32[]{:T(128)} %max.25), channel_id=1, source_target_pairs={{0,2},{1,3},{2,0},{3,1},{4,6},{5,7},{6,4},{7,5},{8,10},{9,11},{10,... | collective-permute-start | bytes 20 | tf_op jit(solution)/shard_map/ppermute | solution.py:185
  104.8 0.5 collective-permute-done.8
  105.9 5.9 %conditional.1 = (bf16[4,136,512]{2,1,0:T(8,128)(2,1)}, bf16[1,1,512,512]{3,2,1,0:T(8,128)(2,1)}) conditional(s32[]{:T(128)} %convert_element_type.29, (s32[]{:T(128)}, bf16[64,128,128]{2,1,0:T(8,128)(2,1)}, s32[2,64]{1,0:T(2,128)S(1)}, bf16[64,128,128]{2,1,0:T(8,128)(2,1)S(1)}, f32[512,512]{1,0:T(8,128)S(1)}) %tuple.24, (s32[]{:T(128)}, ...), branch_computations={%region_6.7_spmd, %region_7.8_spmd} | conditional | bytes 4194320 | solution.py:418
  105.9 5.9 %place.3 = (bf16[512,512]{1,0:T(8,128)(2,1)}, bf16[4,136,512]{2,1,0:T(8,128)(2,1)}) custom-call(s32[1]{0:T(128)} %bitcast.2.refs_0_, s32[2,64]{1,0:T(2,128)S(1)} %get-tuple-element.35.refs_1_, bf16[64,128,128]{2,1,0:T(8,128)(2,1)S(1)} %get-tuple-element.36.refs_2_, bf16[32,128,128]{2,1,0:T(8,128)(2,1)} %get-tuple-element.37.refs_3_, ...), custom_call_target="tpu_custom_call" | custom-call | tf_op jit(solution)/shard_map/cond/branch_1_fun/place/pallas_call | solution.py:254
  111.8 4.6 %all-to-all-start.2 = ((bf16[4,136,512]{2,1,0:T(8,128)(2,1)}), bf16[4,136,512]{2,1,0:T(8,128)(2,1)S(1)}, u32[]{:S(2)}, u32[]{:S(2)}) async-start(bf16[4,136,512]{2,1,0:T(8,128)(2,1)} %get-tuple-element.71), calls=%async_computation.2 | async-start | bytes 1114112 | tf_op jit(solution)/shard_map/all_to_all | solution.py:419
  116.5 0.9 copy.47.refs_2_
  117.3 9.4 %all-to-all-done.2.refs_0_ = bf16[4,136,512]{2,1,0:T(8,128)(2,1)S(1)} async-done(((bf16[4,136,512]{2,1,0:T(8,128)(2,1)}), bf16[4,136,512]{2,1,0:T(8,128)(2,1)S(1)}, u32[]{:S(2)}, u32[]{:S(2)}) %all-to-all-start.2) | async-done | bytes 557088 | tf_op jit(solution)/shard_map/all_to_all | solution.py:419
  126.7 0.8 copy-done
  127.5 6.7 %detect.1 = bf16[64,128,512]{2,1,0:T(8,128)(2,1)} custom-call(bf16[4,136,512]{2,1,0:T(8,128)(2,1)} %copy-done, bf16[512,240]{1,0:T(8,128)(2,1)} %pad_maximum_fusion.2.refs_1_, f32[512,1]{1,0:T(8,128)} %copy.47.refs_2_), custom_call_target="tpu_custom_call" | custom-call | tf_op jit(solution)/shard_map/detect/pallas_call | solution.py:318
  (37 shorter events, 0.3 us)
Async XLA Ops:
  6.2 25.0 %copy-start.1 = (bf16[1,128,128]{2,1,0:T(8,128)(2,1)S(1)}, bf16[1,128,128]{2,1,0:T(8,128)(2,1)}, u32[]{:S(2)}) copy-start(bf16[1,128,128]{2,1,0:T(8,128)(2,1)} %repeat.1) | copy-start | bytes 98308
  6.2 4.2 %collective-permute-start = (bf16[1,128,128]{2,1,0:T(8,128)(2,1)}, bf16[1,128,128]{2,1,0:T(8,128)(2,1)S(1)}, u32[]{:S(2)}, u32[]{:S(2)}) collective-permute-start(bf16[1,128,128]{2,1,0:T(8,128)(2,1)} %repeat.1), channel_id=1, source_target_pairs={{0,32},{4,36},{8,40},{12,44},{16,48},{20,52},{24,56},{28,60},{32,0... | collective-permute-start | bytes 98312 | tf_op jit(solution)/shard_map/ppermute | solution.py:185
  11.2 5.6 %collective-permute-start.1 = (bf16[2,128,128]{2,1,0:T(8,128)(2,1)S(1)}, bf16[2,128,128]{2,1,0:T(8,128)(2,1)S(1)}, u32[]{:S(2)}, u32[]{:S(2)}) collective-permute-start(bf16[2,128,128]{2,1,0:T(8,128)(2,1)S(1)} %pad_maximum_fusion.4), channel_id=1, source_target_pairs={{0,64},{4,68},{8,72},{12,76},{16,80},{20,84},{24,88},{28,92},{32,9... | collective-permute-start | bytes 196616 | tf_op jit(solution)/shard_map/ppermute | solution.py:185
  17.5 13.7 %collective-permute-start.2 = (bf16[4,128,128]{2,1,0:T(8,128)(2,1)S(1)}, bf16[4,128,128]{2,1,0:T(8,128)(2,1)S(1)}, u32[]{:S(2)}, u32[]{:S(2)}) collective-permute-start(bf16[4,128,128]{2,1,0:T(8,128)(2,1)S(1)} %pad_maximum_fusion.3), channel_id=1, source_target_pairs={{0,128},{4,132},{8,136},{12,140},{16,144},{20,148},{24,152},{28,15... | collective-permute-start | bytes 393224 | tf_op jit(solution)/shard_map/ppermute | solution.py:185
  31.9 8.6 %copy-start.3 = (s32[1,2048,1]{1,2,0:T(1,128)S(1)}, s32[1,2048,1]{1,2,0:T(1,128)}, u32[]{:S(2)}) copy-start(s32[1,2048,1]{1,2,0:T(1,128)} %param.15) | copy-start | bytes 24580
  31.9 12.4 %copy-start.4 = (f32[1,2048]{1,0:T(1,128)S(1)}, f32[1,2048]{1,0:T(1,128)}, u32[]{:S(2)}) copy-start(f32[1,2048]{1,0:T(1,128)} %refs_3_.3) | copy-start | bytes 24580
  31.9 13.4 %copy-start.2 = (s32[1,2048,2]{1,2,0:T(2,128)S(1)}, s32[1,2048,2]{1,2,0:T(2,128)}, u32[]{:S(2)}) copy-start(s32[1,2048,2]{1,2,0:T(2,128)} %param.16) | copy-start | bytes 49156
  31.9 13.8 %copy-start.5 = (bf16[64,100]{1,0:T(8,128)(2,1)S(1)}, bf16[64,100]{1,0:T(8,128)(2,1)}, u32[]{:S(2)}) copy-start(bf16[64,100]{1,0:T(8,128)(2,1)} %param.18) | copy-start | bytes 38404
  31.9 58.4 %all-to-all-start.1 = ((bf16[64,128,128]{2,1,0:T(8,128)(2,1)}), bf16[64,128,128]{2,1,0:T(8,128)(2,1)S(1)}, u32[]{:S(2)}, u32[]{:S(2)}) async-start(bf16[64,128,128]{2,1,0:T(8,128)(2,1)} %get-tuple-element.60), calls=%async_computation.1 | async-start | bytes 4194304 | tf_op jit(solution)/shard_map/all_to_all | solution.py:381
  39.9 12.2 %copy-start.6 = (f32[64]{0:T(128)S(1)}, f32[64]{0:T(128)}, u32[]{:S(2)}) copy-start(f32[64]{0:T(128)} %param.19) | copy-start | bytes 772
  42.2 56.8 %collective-permute-start.7 = (f32[]{:T(128)}, f32[]{:T(128)}, u32[]{:S(2)}, u32[]{:S(2)}) collective-permute-start(f32[]{:T(128)} %reduce_max.9), channel_id=1, source_target_pairs={{0,1},{1,0},{2,3},{3,2},{4,5},{5,4},{6,7},{7,6},{8,9},{9,8},{10,11... | collective-permute-start | bytes 20 | tf_op jit(solution)/shard_map/ppermute | solution.py:185
  47.1 27.0 %collective-permute-start.5 = (bf16[8,128,128]{2,1,0:T(8,128)(2,1)}, bf16[8,128,128]{2,1,0:T(8,128)(2,1)}, u32[]{:S(2)}, u32[]{:S(2)}) collective-permute-start(bf16[8,128,128]{2,1,0:T(8,128)(2,1)} %pad_maximum_fusion.1), channel_id=1, source_target_pairs={{0,24},{4,28},{8,16},{12,20},{16,8},{20,12},{24,0},{28,4},{32,56},... | collective-permute-start | bytes 786440 | tf_op jit(solution)/shard_map/ppermute | solution.py:185
  49.9 24.2 %collective-permute-start.4 = (bf16[8,128,128]{2,1,0:T(8,128)(2,1)}, bf16[8,128,128]{2,1,0:T(8,128)(2,1)}, u32[]{:S(2)}, u32[]{:S(2)}) collective-permute-start(bf16[8,128,128]{2,1,0:T(8,128)(2,1)} %pad_maximum_fusion.1), channel_id=1, source_target_pairs={{0,16},{4,20},{8,24},{12,28},{16,0},{20,4},{24,8},{28,12},{32,48},... | collective-permute-start | bytes 786440 | tf_op jit(solution)/shard_map/ppermute | solution.py:185
  50.8 23.4 %collective-permute-start.3 = (bf16[8,128,128]{2,1,0:T(8,128)(2,1)}, bf16[8,128,128]{2,1,0:T(8,128)(2,1)}, u32[]{:S(2)}, u32[]{:S(2)}) collective-permute-start(bf16[8,128,128]{2,1,0:T(8,128)(2,1)} %pad_maximum_fusion.1), channel_id=1, source_target_pairs={{0,8},{4,12},{8,0},{12,4},{16,24},{20,28},{24,16},{28,20},{32,40},... | collective-permute-start | bytes 786440 | tf_op jit(solution)/shard_map/ppermute | solution.py:185
  90.3 15.6 %collective-permute-start.6 = (bf16[32,128,128]{2,1,0:T(8,128)(2,1)}, bf16[32,128,128]{2,1,0:T(8,128)(2,1)}, u32[]{:S(2)}, u32[]{:S(2)}) collective-permute-start(bf16[32,128,128]{2,1,0:T(8,128)(2,1)} %pad_maximum_fusion), channel_id=1, source_target_pairs={{0,4},{4,0},{8,12},{12,8},{16,20},{20,16},{24,28},{28,24},{32,36},... | collective-permute-start | bytes 3145736 | tf_op jit(solution)/shard_map/ppermute | solution.py:185
  92.7 5.5 %copy-start.7 = (s32[128]{0:T(128)S(1)}, s32[128]{0:T(128)}, u32[]{:S(2)}) copy-start(s32[128]{0:T(128)} %rem.19) | copy-start | bytes 1540
  100.2 5.1 %collective-permute-start.8 = (f32[]{:T(128)}, f32[]{:T(128)}, u32[]{:S(2)}, u32[]{:S(2)}) collective-permute-start(f32[]{:T(128)} %max.25), channel_id=1, source_target_pairs={{0,2},{1,3},{2,0},{3,1},{4,6},{5,7},{6,4},{7,5},{8,10},{9,11},{10,... | collective-permute-start | bytes 20 | tf_op jit(solution)/shard_map/ppermute | solution.py:185
  111.8 14.9 %all-to-all-start.2 = ((bf16[4,136,512]{2,1,0:T(8,128)(2,1)}), bf16[4,136,512]{2,1,0:T(8,128)(2,1)S(1)}, u32[]{:S(2)}, u32[]{:S(2)}) async-start(bf16[4,136,512]{2,1,0:T(8,128)(2,1)} %get-tuple-element.71), calls=%async_computation.2 | async-start | bytes 1114112 | tf_op jit(solution)/shard_map/all_to_all | solution.py:419
  126.7 0.8 copy-start

commit v4 on v3

--- a/solution.py
+++ b/solution.py
@@ -186,7 +186,9 @@
 
 
 def place_kernel(per_step, nband, masks, owner_ref, table_ref, first_ref, *refs):
-    *second_refs, cover_ref, coadd_ref, strip_ref, acc, full = refs
+    second_refs, (cover_ref, coadd_ref, *strip_refs), (acc, full) = (
+        refs[: -nband - 4], refs[-nband - 4 : -2], refs[-2:]
+    )
     step = pl.program_id(0)
     steps = pl.num_programs(0)
     strip_rows = PS // nband
@@ -239,9 +241,11 @@
             value = (acc[part, 0:PS, :] / jnp.maximum(cover_ref[:, at], 1.0)).astype(BF16)
             coadd_ref[:, at] = value
             full[edge // 2 : edge // 2 + PS, at] = value.astype(F32)
-        for b in range(nband):
-            start = edge // 2 - PAD + b * strip_rows
-            strip_ref[b] = full[start : start + strip_ref.shape[1], :].astype(BF16)
+        height = strip_refs[0].shape[0]
+        for i, ref in enumerate(strip_refs):
+            start = pl.multiple_of((owner_ref[1] ^ i) * strip_rows, 8)
+            rows = full[pl.ds(start, height + 8), :]
+            ref[...] = rows[edge // 2 - PAD : edge // 2 - PAD + height].astype(BF16)
 
 
 def place(owner, table, first, seconds, cover, nband, masks):
@@ -256,7 +260,7 @@
         name="place",
         out_shape=(
             jax.ShapeDtypeStruct((PS, PS), BF16),
-            jax.ShapeDtypeStruct((nband, strip, PS), BF16),
+            *[jax.ShapeDtypeStruct((strip, PS), BF16)] * nband,
         ),
         grid_spec=pltpu.PrefetchScalarGridSpec(
             num_scalar_prefetch=2,
@@ -264,7 +268,7 @@
             in_specs=[*specs, pl.BlockSpec((PS, PS), lambda i, *_: (0, 0))],
             out_specs=(
                 pl.BlockSpec((PS, PS), lambda i, *_: (0, 0)),
-                pl.BlockSpec((nband, strip, PS), lambda i, *_: (0, 0, 0)),
+                *[pl.BlockSpec((strip, PS), lambda i, *_: (0, 0))] * nband,
             ),
             scratch_shapes=[
                 pltpu.VMEM((PS // LANES + 1, PS + 8, LANES), F32),
@@ -277,7 +281,8 @@
     )(owner, table, first, *seconds, cover)
 
 
-def detect_kernel(nband, strip_ref, weight_ref, bias_ref, out_ref, main, edge):
+def detect_kernel(nband, *refs):
+    strip_refs, (weight_ref, bias_ref, out_ref, main, edge) = refs[:nband], refs[nband:]
     step = pl.program_id(0)
     groups = main.shape[0]
     channels = out_ref.shape[0]
@@ -289,7 +294,7 @@
             pieces = []
             for s in range(KS):
                 for b in range(nband):
-                    x = strip_ref[b, 8 * g : 8 * g + 8, :].astype(F32)
+                    x = strip_refs[b][8 * g : 8 * g + 8, :].astype(F32)
                     d = s - PAD
                     if d:
                         x = pltpu.roll(x, (-d) % PS, 1)
@@ -311,7 +316,8 @@
 
 
 def detect(strips, weight, bias, channels, strip_rows):
-    nband, rows, _ = strips.shape
+    nband = len(strips)
+    rows = strips[0].shape[0]
     groups = rows // 8
     depth = nband * KS
     step_rows = 32
@@ -323,7 +329,7 @@
             num_scalar_prefetch=0,
             grid=(strip_rows // step_rows,),
             in_specs=[
-                pl.BlockSpec(strips.shape, lambda i: (0, 0, 0)),
+                *[pl.BlockSpec(x.shape, lambda i: (0, 0)) for x in strips],
                 pl.BlockSpec(weight.shape, lambda i: (0, 0)),
                 pl.BlockSpec(bias.shape, lambda i: (0, 0)),
             ],
@@ -334,14 +340,18 @@
             ],
         ),
         compiler_params=pltpu.CompilerParams(
-            dimension_semantics=("arbitrary",)
-        ),
-    )(strips, weight, bias)
-
-
-def toeplitz(det_weight, nband):
+            dimension_semantics=("arbitrary",), vmem_limit_bytes=24 << 20
+        ),
+    )(*strips, weight, bias)
+
+
+def toeplitz(det_weight, nband, band):
     channels = det_weight.shape[0]
     taps = det_weight.reshape(channels, nband, KS, KS).transpose(0, 3, 1, 2)
+    order = jnp.arange(nband) ^ band
+    taps = sum(
+        jnp.where((order == b)[None, None, :, None], taps[:, :, b : b + 1], 0) for b in range(nband)
+    )
     row_out = jnp.arange(8)[:, None]
     out = []
     for lo, hi in ((0, 8), (8, 12)):
@@ -373,11 +383,14 @@
     near = repeat(*inputs, npatch)
     bits = npatch.bit_length() - 1
     masks = [1 << bit for bit in [*range(3, bits), 1, 2, 0] if bit < bits]
-    for mask in masks[:-3]:
-        near = jnp.concatenate([near, swap(near, "patch", mask)], axis=0)
+    near = [near] + [swap(near, "patch", mask) for mask in range(8, npatch, 8)]
     buf0, buf1 = front(*inputs, npatch)
-    buf0, near = lax.optimization_barrier((buf0, near))
+    buf0, near, routes_row, offs_rows, weights, det_weight, det_bias = lax.optimization_barrier(
+        (buf0, near, routes_row, offs_rows, weights, det_weight, det_bias)
+    )
+    near = jnp.concatenate(near, axis=0)
     near = jnp.concatenate([near] + [swap(near, "patch", m) for m in (2, 4, 6)], axis=0)
+    far = swap(near, "patch", 1)
     first = lax.all_to_all(buf0, "patch", split_axis=0, concat_axis=0, tiled=True)
     dest_all = routes_row.reshape(npatch, tiles)
     same = (dest_all[:, :, None] == dest_all[:, None, :]) & (
@@ -402,21 +415,21 @@
     channels = det_weight.shape[0]
     strip_rows = PS // nband
     bias = jnp.broadcast_to(det_bias[:, None, None], (channels, 8, 1)).reshape(channels * 8, 1)
-    first, near = lax.optimization_barrier((first, near))
-    far = swap(near, "patch", 1)
-    first, far, table, cover, kernel, bias, repeats = lax.optimization_barrier(
-        (first, far, table, cover, toeplitz(det_weight, nband), bias, repeats)
-    )
+    band = lax.axis_index("band").astype(jnp.int32)
+    first, near, far, table, cover, kernel, bias, repeats = lax.optimization_barrier(
+        (first, near, far, table, cover, toeplitz(det_weight, nband, band), bias, repeats)
+    )
+    where = jnp.stack([owner, band])
 
     def one_repeat():
-        return place(owner[None], table, first, (near, far), cover, nband, masks)
+        return place(where, table, first, (near, far), cover, nband, masks)
 
     def any_repeats():
         rest = lax.all_to_all(buf1, "patch", split_axis=0, concat_axis=0, tiled=True)
-        return place(owner[None], table, first, (rest,), cover, nband, None)
-
-    coadd, strips = lax.cond(repeats <= 1.0, one_repeat, any_repeats)
-    strips = lax.all_to_all(strips, "band", split_axis=0, concat_axis=0, tiled=True)
+        return place(where, table, first, (rest,), cover, nband, None)
+
+    coadd, *strips = lax.cond(repeats <= 1.0, one_repeat, any_repeats)
+    strips = strips[:1] + [swap(x, "band", i) for i, x in enumerate(strips) if i]
     detection = detect(strips, kernel, bias, channels, strip_rows)
     return (coadd[None, None], detection[None])
 

time: 135 us -> 121 us (0.90); the launches traced: 134 us -> 119 us
  waiting for transfers between devices: 48 us -> 18 us
  local copies, waits for them, and re-layouts: 12 us -> 23.4 us
  starting transfers between devices: 34.2 us -> 40.4 us
  other arithmetic: 12 us -> 9.99 us
    all_to_all x1, waiting for transfers between devices: 13.9 us -> 0.01 us  [body(): lax.all_to_all(buf0, 'patch', split_axis=0, concat_axis=0, tiled=True)]
    all_to_all x1 -> x0, waiting for transfers between devices: 9.39 us -> none  [body(): lax.all_to_all(strips, 'band', split_axis=0, concat_axis=0, tiled=True)]
    ppermute x9 -> x16, starting transfers between devices: 21.6 us -> 29.8 us  [swap(): return lax.ppermute(x, axis, [(i, i ^ mask) for i in range(size)])]
    ppermute x9 -> x16, waiting for transfers between devices: 24.7 us -> 18 us  [swap(): return lax.ppermute(x, axis, [(i, i ^ mask) for i in range(size)])]
    unnamed x19 -> x47, local copies, waits for them, and re-layouts: 2.1 us -> 8.38 us
    all_to_all x1 -> x0, starting transfers between devices: 4.64 us -> none  [body(): lax.all_to_all(strips, 'band', split_axis=0, concat_axis=0, tiled=True)]
    concatenate x4 -> x0, other arithmetic: 4.55 us -> none  [the longest x1 2.28 us: body(): jnp.concatenate([near] + [swap(near, 'patch', m) for m in (2, 4, 6)], axi...]
    all_to_all x1, starting transfers between devices: 7.97 us -> 10.6 us  [body(): lax.all_to_all(buf0, 'patch', split_axis=0, concat_axis=0, tiled=True)]
  transfers between devices with their start and end apart: 11 -> 17, of which waited for: 6 -> 5; matrix products, arithmetic and copies ran while one was open for 15% -> 27% of each run, Pallas kernels for 6% -> 6%
where the time goes in v4:
time: 121 us; the launch traced here: 119 us
  starting transfers between devices  40.4 us (33%)
  local copies, waits for them, and re-layouts  23.4 us (19%)
  Pallas kernels  23.4 us (19%)
  waiting for transfers between devices  18 us (15%)
  other arithmetic  9.99 us (8%)
  between operations  2.9 us (2%)
    ppermute x16, starting transfers between devices, swap(): return lax.ppermute(x, axis, [(i, i ^ mask) for i in range(size)])  29.8 us
    ppermute x16, waiting for transfers between devices, swap(): return lax.ppermute(x, axis, [(i, i ^ mask) for i in range(size)])  18 us
    all_to_all x1, starting transfers between devices, body(): lax.all_to_all(buf0, 'patch', split_axis=0, concat_axis=0, tiled=True)  10.6 us
    unnamed x47, local copies, waits for them, and re-layouts  8.38 us
    pallas_call x1, Pallas kernels, front(): pl.pallas_call(lambda *refs: front_kernel(per_step, *refs), name='front',...  7.63 us
    select_n x4, local copies, waits for them, and re-layouts, toeplitz(): total = jnp.where(on, taps[:, None, :, :, r, None], total)  6.82 us
    pallas_call x1, Pallas kernels, place(): pl.pallas_call(lambda *refs: place_kernel(per_step, nband, masks, *refs),...  6 us
    pallas_call x1, Pallas kernels, detect(): pl.pallas_call(lambda *refs: detect_kernel(nband, *refs), name='detect',...  5.56 us
  transfers between devices with their start and end apart: 17, of which 5 were waited for; matrix products, arithmetic and copies ran while one was open for 27% of the time, Pallas kernels for 6%

profile of v4, /device:TPU:32, one launch (start us, length us, event | category | flops | bytes accessed | tf_op | source)
XLA Modules:
  0.0 118.9 jit_solution(12953075135215202540)
XLA Ops:
  0.6 0.7 convert_bitcast_fusion
  1.3 0.6 reshape.320.refs_4_
  1.9 4.2 %repeat.1 = bf16[1,128,128]{2,1,0:T(8,128)(2,1)} custom-call(s32[1]{0:T(128)} %bitcast.2.refs_0_, s32[1,2048]{1,0:T(1,128)} %bitcast.48, s32[2,2048]{1,0:T(2,128)} %bitcast.45, f32[1,2048]{1,0:T(1,128)} %refs_3_.3, f32[14,32]{1,0:T(8,128)} %reshape.320.refs_4_, bf16[32,1,128,128]{3,2,1,0:T(8,128)(2,1)} %refs_5_.3, bf16[32,1,128,128]{3,2,1,0:T(8,128)(2,1)} %refs_6_.3, ...), custom_call_target="tpu_custom_call" | custom-call | tf_op jit(solution)/shard_map/repeat/pallas_call | solution.py:87
  6.2 5.9 %collective-permute-start.6 = (bf16[1,128,128]{2,1,0:T(8,128)(2,1)}, bf16[1,128,128]{2,1,0:T(8,128)(2,1)S(1)}, u32[]{:S(2)}, u32[]{:S(2)}) collective-permute-start(bf16[1,128,128]{2,1,0:T(8,128)(2,1)} %repeat.1), channel_id=1, source_target_pairs={{0,224},{4,228},{8,232},{12,236},{16,240},{20,244},{24,248},{28,25... | collective-permute-start | bytes 98312 | tf_op jit(solution)/shard_map/ppermute | solution.py:185
  12.1 4.6 %collective-permute-start.4 = (bf16[1,128,128]{2,1,0:T(8,128)(2,1)}, bf16[1,128,128]{2,1,0:T(8,128)(2,1)S(1)}, u32[]{:S(2)}, u32[]{:S(2)}) collective-permute-start(bf16[1,128,128]{2,1,0:T(8,128)(2,1)} %repeat.1), channel_id=1, source_target_pairs={{0,160},{4,164},{8,168},{12,172},{16,176},{20,180},{24,184},{28,18... | collective-permute-start | bytes 98312 | tf_op jit(solution)/shard_map/ppermute | solution.py:185
  16.7 0.6 collective-permute-start.3
  17.3 1.0 collective-permute-start.2
  18.3 0.5 fusion.23
  18.8 0.6 fusion.21
  19.4 0.6 fusion.19
  20.1 2.8 %collective-permute-start.1 = (bf16[1,128,128]{2,1,0:T(8,128)(2,1)}, bf16[1,128,128]{2,1,0:T(8,128)(2,1)S(1)}, u32[]{:S(2)}, u32[]{:S(2)}) collective-permute-start(bf16[1,128,128]{2,1,0:T(8,128)(2,1)} %repeat.1), channel_id=1, source_target_pairs={{0,64},{4,68},{8,72},{12,76},{16,80},{20,84},{24,88},{28,92},{32,9... | collective-permute-start | bytes 98312 | tf_op jit(solution)/shard_map/ppermute | solution.py:185
  22.9 0.6 pad_add_fusion
  23.5 7.6 %front.1 = (bf16[64,128,128]{2,1,0:T(8,128)(2,1)}, bf16[64,128,128]{2,1,0:T(8,128)(2,1)}) custom-call(s32[1]{0:T(128)} %bitcast.2.refs_0_, s32[1,2048]{1,0:T(1,128)} %bitcast.49, s32[2,2048]{1,0:T(2,128)} %bitcast.46, f32[1,2048]{1,0:T(1,128)} %refs_3_.3, f32[14,32]{1,0:T(8,128)} %reshape.320.refs_4_, bf16[32,1,128,128]{3,2,1,0:T(8,128)(2,1)} %refs_5_.3, ...), custom_call_target="tpu_custom_call" | custom-call | bytes 25165824 | tf_op jit(solution)/shard_map/front/pallas_call | solution.py:151
  31.2 10.6 %all-to-all-start.1 = ((bf16[64,128,128]{2,1,0:T(8,128)(2,1)}), bf16[64,128,128]{2,1,0:T(8,128)(2,1)S(1)}, u32[]{:S(2)}, u32[]{:S(2)}) async-start(bf16[64,128,128]{2,1,0:T(8,128)(2,1)} %get-tuple-element.82), calls=%async_computation.1 | async-start | bytes 4194304 | tf_op jit(solution)/shard_map/all_to_all | solution.py:394
  41.9 0.6 constant_dynamic-update-slice_fusion.7
  42.5 0.6 constant_dynamic-update-slice_fusion.6
  43.1 0.6 constant_dynamic-update-slice_fusion.5
  43.8 0.6 constant_dynamic-update-slice_fusion.4
  44.4 0.6 constant_dynamic-update-slice_fusion.3
  45.0 0.6 constant_dynamic-update-slice_fusion.2
  45.7 0.6 constant_dynamic-update-slice_fusion.1
  46.3 0.6 constant_dynamic-update-slice_fusion
  46.9 2.7 %collective-permute-start.9 = (bf16[8,128,128]{2,1,0:T(8,128)(2,1)}, bf16[8,128,128]{2,1,0:T(8,128)(2,1)}, u32[]{:S(2)}, u32[]{:S(2)}) collective-permute-start(bf16[8,128,128]{2,1,0:T(8,128)(2,1)} %get-tuple-element.127), channel_id=1, source_target_pairs={{0,24},{4,28},{8,16},{12,20},{16,8},{20,12},{24,0},{28,4},{32,56},... | collective-permute-start | bytes 786440 | tf_op jit(solution)/shard_map/ppermute | solution.py:185
  49.6 0.9 collective-permute-start.8
  50.4 0.6 collective-permute-start.7
  51.0 0.5 broadcast.375
  51.5 0.7 reduce.10
  52.4 0.2 reduce_window_sum.11
  52.9 0.1 copy.26
  53.2 0.5 copy-done.10
  53.9 1.0 select_select_fusion.1
  54.9 0.2 and_reduce_fusion
  55.2 0.7 reduce_max.9
  55.8 1.6 %collective-permute-start.11 = (f32[]{:T(128)}, f32[]{:T(128)}, u32[]{:S(2)}, u32[]{:S(2)}) collective-permute-start(f32[]{:T(128)} %reduce_max.9), channel_id=1, source_target_pairs={{0,1},{1,0},{2,3},{3,2},{4,5},{5,4},{6,7},{7,6},{8,9},{9,8},{10,11... | collective-permute-start | bytes 20 | tf_op jit(solution)/shard_map/ppermute | solution.py:185
  57.4 0.5 broadcast.376
  58.0 0.7 reduce.11
  58.8 0.7 ne.41
  59.5 0.6 div.12
  60.1 0.7 rem.19
  60.8 0.6 broadcast_in_dim.289
  61.4 0.7 broadcast_in_dim.337
  62.1 2.0 %reshape.322 = bf16[512,80]{0,1:T(8,128)(2,1)S(1)} reshape(bf16[64,8,5,4,4]{1,0,4,3,2:T(8,128)(2,1)S(1)} %select_select_fusion.1) | data formatting | bytes 163840 | tf_op jit(solution)/shard_map/jit(_where)/select_n | solution.py:362
  64.2 0.1 copy.28
  64.3 10.0 %collective-permute-done.7 = bf16[8,128,128]{2,1,0:T(8,128)(2,1)} collective-permute-done((bf16[8,128,128]{2,1,0:T(8,128)(2,1)}, bf16[8,128,128]{2,1,0:T(8,128)(2,1)}, u32[]{:S(2)}, u32[]{:S(2)}) %collective-permute-start.7) | collective-permute-done | bytes 262176 | tf_op jit(solution)/shard_map/ppermute | solution.py:185
  74.2 1.7 %constant_dynamic-update-slice_fusion.10 = bf16[32,128,128]{2,1,0:T(8,128)(2,1)} fusion(bf16[32,128,128]{2,1,0:T(8,128)(2,1)} %get-tuple-element.128, bf16[8,128,128]{2,1,0:T(8,128)(2,1)} %collective-permute-done.7), kind=kLoop, calls=%fused_computation.30 | loop fusion | bytes 524288
  75.9 1.7 %constant_dynamic-update-slice_fusion.9 = bf16[32,128,128]{2,1,0:T(8,128)(2,1)} fusion(bf16[32,128,128]{2,1,0:T(8,128)(2,1)} %constant_dynamic-update-slice_fusion.10, bf16[8,128,128]{2,1,0:T(8,128)(2,1)} %collective-permute-done.8), kind=kLoop, calls=%fused_computation.29 | loop fusion | bytes 524288
  77.6 1.7 %constant_dynamic-update-slice_fusion.8 = bf16[32,128,128]{2,1,0:T(8,128)(2,1)} fusion(bf16[32,128,128]{2,1,0:T(8,128)(2,1)} %constant_dynamic-update-slice_fusion.9, bf16[8,128,128]{2,1,0:T(8,128)(2,1)} %collective-permute-done.9), kind=kLoop, calls=%fused_computation.28 | loop fusion | bytes 524288 | tf_op jit(solution)/shard_map/concatenate | solution.py:392
  79.3 3.1 %select_select_fusion = bf16[64,8,5,4,8]{1,0,4,3,2:T(8,128)(2,1)} fusion(pred[8,8]{0,1:T(8,128)(4,1)} %get-tuple-element.161, pred[8,8]{0,1:T(8,128)(4,1)} %get-tuple-element.162, pred[8,8]{0,1:T(8,128)(4,1)} %get-tuple-element.163, pred[8,8]{0,1:T(8,128)(4,1)} %get-tuple-element.164, pred[8,8]{0,1:T(8,128)(4,1)} %fusion.23, ...), kind=kLoop, calls=%fused_computation | loop fusion | flops 409600 | bytes 176960 | tf_op jit(solution)/shard_map/jit(_where)/select_n | solution.py:362
  82.4 4.5 %reshape.321 = bf16[512,160]{0,1:T(8,128)(2,1)S(1)} reshape(bf16[64,8,5,4,8]{1,0,4,3,2:T(8,128)(2,1)} %select_select_fusion) | data formatting | bytes 327680 | tf_op jit(solution)/shard_map/jit(_where)/select_n | solution.py:362
  86.9 0.1 copy.27
  87.1 0.1 pad_maximum_fusion.refs_4_
  87.3 0.7 fusion.2
  89.2 4.6 %collective-permute-start.12 = (f32[]{:T(128)}, f32[]{:T(128)}, u32[]{:S(2)}, u32[]{:S(2)}) collective-permute-start(f32[]{:T(128)} %max.25), channel_id=1, source_target_pairs={{0,2},{1,3},{2,0},{3,1},{4,6},{5,7},{6,4},{7,5},{8,10},{9,11},{10,... | collective-permute-start | bytes 20 | tf_op jit(solution)/shard_map/ppermute | solution.py:185
  93.7 0.7 collective-permute-done.12
  95.1 6.0 %conditional.1 = (bf16[136,512]{1,0:T(8,128)(2,1)S(1)}, bf16[136,512]{1,0:T(8,128)(2,1)}, bf16[136,512]{1,0:T(8,128)(2,1)}, bf16[136,512]{1,0:T(8,128)(2,1)}, bf16[1,1,512,512]{3,2,1,0:T(8,128)(2,1)}) conditional(s32[]{:T(128)} %convert_element_type.34, (bf16[64,128,128]{2,1,0:T(8,128)(2,1)}, s32[2]{0:T(128)}, s32[2,64]{1,0:T(2,128)S(1)}, ...), branch_computations={%region_6.7_spmd, %region_7.8_spmd} | conditional | bytes 4194344 | solution.py:431
  95.1 6.0 %place.3 = (bf16[512,512]{1,0:T(8,128)(2,1)}, bf16[136,512]{1,0:T(8,128)(2,1)S(1)}, bf16[136,512]{1,0:T(8,128)(2,1)}, bf16[136,512]{1,0:T(8,128)(2,1)}, bf16[136,512]{1,0:T(8,128)(2,1)}) custom-call(s32[2]{0:T(128)} %get-tuple-element.44.refs_0_, s32[2,64]{1,0:T(2,128)S(1)} %get-tuple-element.45.refs_1_, ...), custom_call_target="tpu_custom_call" | custom-call | tf_op jit(solution)/shard_map/cond/branch_1_fun/place/pallas_call | solution.py:258
  101.1 1.5 %collective-permute-start.13 = (bf16[136,512]{1,0:T(8,128)(2,1)}, bf16[136,512]{1,0:T(8,128)(2,1)S(1)}, u32[]{:S(2)}, u32[]{:S(2)}) collective-permute-start(bf16[136,512]{1,0:T(8,128)(2,1)} %get-tuple-element.105), channel_id=1, source_target_pairs={{0,1},{1,0},{2,3},{3,2},{4,5},{5,4},{6,7},{7,6},{8,9},{9,8},{10,11... | collective-permute-start | bytes 417800 | tf_op jit(solution)/shard_map/ppermute | solution.py:185
  102.6 2.9 %collective-permute-start.14 = (bf16[136,512]{1,0:T(8,128)(2,1)}, bf16[136,512]{1,0:T(8,128)(2,1)S(1)}, u32[]{:S(2)}, u32[]{:S(2)}) collective-permute-start(bf16[136,512]{1,0:T(8,128)(2,1)} %get-tuple-element.106), channel_id=1, source_target_pairs={{0,2},{1,3},{2,0},{3,1},{4,6},{5,7},{6,4},{7,5},{8,10},{9,11},{10,... | collective-permute-start | bytes 417800 | tf_op jit(solution)/shard_map/ppermute | solution.py:185
  105.5 0.3 collective-permute-start.15
  105.8 0.1 copy.31.refs_5_
  106.0 1.5 %collective-permute-done.13.refs_1_ = bf16[136,512]{1,0:T(8,128)(2,1)S(1)} collective-permute-done((bf16[136,512]{1,0:T(8,128)(2,1)}, bf16[136,512]{1,0:T(8,128)(2,1)S(1)}, u32[]{:S(2)}, u32[]{:S(2)}) %collective-permute-start.13) | collective-permute-done | bytes 139296 | tf_op jit(solution)/shard_map/ppermute | solution.py:185
  107.4 4.1 %collective-permute-done.14.refs_2_ = bf16[136,512]{1,0:T(8,128)(2,1)S(1)} collective-permute-done((bf16[136,512]{1,0:T(8,128)(2,1)}, bf16[136,512]{1,0:T(8,128)(2,1)S(1)}, u32[]{:S(2)}, u32[]{:S(2)}) %collective-permute-start.14) | collective-permute-done | bytes 139296 | tf_op jit(solution)/shard_map/ppermute | solution.py:185
  111.5 1.8 %collective-permute-done.15.refs_3_ = bf16[136,512]{1,0:T(8,128)(2,1)S(1)} collective-permute-done((bf16[136,512]{1,0:T(8,128)(2,1)}, bf16[136,512]{1,0:T(8,128)(2,1)S(1)}, u32[]{:S(2)}, u32[]{:S(2)}) %collective-permute-start.15) | collective-permute-done | bytes 139296 | tf_op jit(solution)/shard_map/ppermute | solution.py:185
  113.3 5.6 %detect.1 = bf16[64,128,512]{2,1,0:T(8,128)(2,1)} custom-call(bf16[136,512]{1,0:T(8,128)(2,1)S(1)} %get-tuple-element.104.refs_0_, bf16[136,512]{1,0:T(8,128)(2,1)S(1)} %collective-permute-done.13.refs_1_, bf16[136,512]{1,0:T(8,128)(2,1)S(1)} %collective-permute-done.14.refs_2_, bf16[136,512]{1,0:T(8,128)(2,1)S(1)} %collective-permute-done.15.refs_3_, ...), custom_call_target="tpu_custom_call" | custom-call | tf_op jit(solution)/shard_map/detect/pallas_call | solution.py:324
  (80 shorter events, 1.2 us)
Async XLA Ops:
  6.2 13.9 %collective-permute-start.6 = (bf16[1,128,128]{2,1,0:T(8,128)(2,1)}, bf16[1,128,128]{2,1,0:T(8,128)(2,1)S(1)}, u32[]{:S(2)}, u32[]{:S(2)}) collective-permute-start(bf16[1,128,128]{2,1,0:T(8,128)(2,1)} %repeat.1), channel_id=1, source_target_pairs={{0,224},{4,228},{8,232},{12,236},{16,240},{20,244},{24,248},{28,25... | collective-permute-start | bytes 98312 | tf_op jit(solution)/shard_map/ppermute | solution.py:185
  12.1 10.8 %collective-permute-start.5 = (bf16[1,128,128]{2,1,0:T(8,128)(2,1)}, bf16[1,128,128]{2,1,0:T(8,128)(2,1)S(1)}, u32[]{:S(2)}, u32[]{:S(2)}) collective-permute-start(bf16[1,128,128]{2,1,0:T(8,128)(2,1)} %repeat.1), channel_id=1, source_target_pairs={{0,192},{4,196},{8,200},{12,204},{16,208},{20,212},{24,216},{28,22... | collective-permute-start | bytes 98312 | tf_op jit(solution)/shard_map/ppermute | solution.py:185
  12.1 19.0 %collective-permute-start.4 = (bf16[1,128,128]{2,1,0:T(8,128)(2,1)}, bf16[1,128,128]{2,1,0:T(8,128)(2,1)S(1)}, u32[]{:S(2)}, u32[]{:S(2)}) collective-permute-start(bf16[1,128,128]{2,1,0:T(8,128)(2,1)} %repeat.1), channel_id=1, source_target_pairs={{0,160},{4,164},{8,168},{12,172},{16,176},{20,180},{24,184},{28,18... | collective-permute-start | bytes 98312 | tf_op jit(solution)/shard_map/ppermute | solution.py:185
  16.7 14.4 %collective-permute-start.3 = (bf16[1,128,128]{2,1,0:T(8,128)(2,1)}, bf16[1,128,128]{2,1,0:T(8,128)(2,1)S(1)}, u32[]{:S(2)}, u32[]{:S(2)}) collective-permute-start(bf16[1,128,128]{2,1,0:T(8,128)(2,1)} %repeat.1), channel_id=1, source_target_pairs={{0,128},{4,132},{8,136},{12,140},{16,144},{20,148},{24,152},{28,15... | collective-permute-start | bytes 98312 | tf_op jit(solution)/shard_map/ppermute | solution.py:185
  17.3 13.9 %collective-permute-start.2 = (bf16[1,128,128]{2,1,0:T(8,128)(2,1)}, bf16[1,128,128]{2,1,0:T(8,128)(2,1)S(1)}, u32[]{:S(2)}, u32[]{:S(2)}) collective-permute-start(bf16[1,128,128]{2,1,0:T(8,128)(2,1)} %repeat.1), channel_id=1, source_target_pairs={{0,96},{4,100},{8,104},{12,108},{16,112},{20,116},{24,120},{28,124... | collective-permute-start | bytes 98312 | tf_op jit(solution)/shard_map/ppermute | solution.py:185
  20.1 11.1 %collective-permute-start.1 = (bf16[1,128,128]{2,1,0:T(8,128)(2,1)}, bf16[1,128,128]{2,1,0:T(8,128)(2,1)S(1)}, u32[]{:S(2)}, u32[]{:S(2)}) collective-permute-start(bf16[1,128,128]{2,1,0:T(8,128)(2,1)} %repeat.1), channel_id=1, source_target_pairs={{0,64},{4,68},{8,72},{12,76},{16,80},{20,84},{24,88},{28,92},{32,9... | collective-permute-start | bytes 98312 | tf_op jit(solution)/shard_map/ppermute | solution.py:185
  22.9 8.3 %collective-permute-start = (bf16[1,128,128]{2,1,0:T(8,128)(2,1)}, bf16[1,128,128]{2,1,0:T(8,128)(2,1)S(1)}, u32[]{:S(2)}, u32[]{:S(2)}) collective-permute-start(bf16[1,128,128]{2,1,0:T(8,128)(2,1)} %repeat.1), channel_id=1, source_target_pairs={{0,32},{4,36},{8,40},{12,44},{16,48},{20,52},{24,56},{28,60},{32,0... | collective-permute-start | bytes 98312 | tf_op jit(solution)/shard_map/ppermute | solution.py:185
  31.2 10.7 %copy-start.1 = (bf16[1,128,128]{2,1,0:T(8,128)(2,1)S(1)}, bf16[1,128,128]{2,1,0:T(8,128)(2,1)}, u32[]{:S(2)}) copy-start(bf16[1,128,128]{2,1,0:T(8,128)(2,1)} %repeat.1) | copy-start | bytes 98308
  31.2 20.3 %copy-start.2 = (s32[1,2048,1]{1,2,0:T(1,128)S(1)}, s32[1,2048,1]{1,2,0:T(1,128)}, u32[]{:S(2)}) copy-start(s32[1,2048,1]{1,2,0:T(1,128)} %param.15) | copy-start | bytes 24580
  31.2 21.5 %copy-start = (s32[1,2048,2]{1,2,0:T(2,128)S(1)}, s32[1,2048,2]{1,2,0:T(2,128)}, u32[]{:S(2)}) copy-start(s32[1,2048,2]{1,2,0:T(2,128)} %param.16) | copy-start | bytes 49156
  31.2 21.7 %copy-start.12 = (bf16[64,100]{1,0:T(8,128)(2,1)S(1)}, bf16[64,100]{1,0:T(8,128)(2,1)}, u32[]{:S(2)}) copy-start(bf16[64,100]{1,0:T(8,128)(2,1)} %param.18) | copy-start | bytes 38404
  31.2 63.8 %all-to-all-start.1 = ((bf16[64,128,128]{2,1,0:T(8,128)(2,1)}), bf16[64,128,128]{2,1,0:T(8,128)(2,1)S(1)}, u32[]{:S(2)}, u32[]{:S(2)}) async-start(bf16[64,128,128]{2,1,0:T(8,128)(2,1)} %get-tuple-element.82), calls=%async_computation.1 | async-start | bytes 4194304 | tf_op jit(solution)/shard_map/all_to_all | solution.py:394
  41.9 16.1 %copy-start.3 = (f32[1,2048]{1,0:T(1,128)S(1)}, f32[1,2048]{1,0:T(1,128)}, u32[]{:S(2)}) copy-start(f32[1,2048]{1,0:T(1,128)} %refs_3_.3) | copy-start | bytes 24580
  41.9 19.5 %copy-start.14 = (f32[64]{0:T(128)S(1)}, f32[64]{0:T(128)}, u32[]{:S(2)}) copy-start(f32[64]{0:T(128)} %param.19) | copy-start | bytes 772
  46.9 30.7 %collective-permute-start.9 = (bf16[8,128,128]{2,1,0:T(8,128)(2,1)}, bf16[8,128,128]{2,1,0:T(8,128)(2,1)}, u32[]{:S(2)}, u32[]{:S(2)}) collective-permute-start(bf16[8,128,128]{2,1,0:T(8,128)(2,1)} %get-tuple-element.127), channel_id=1, source_target_pairs={{0,24},{4,28},{8,16},{12,20},{16,8},{20,12},{24,0},{28,4},{32,56},... | collective-permute-start | bytes 786440 | tf_op jit(solution)/shard_map/ppermute | solution.py:185
  49.6 26.3 %collective-permute-start.8 = (bf16[8,128,128]{2,1,0:T(8,128)(2,1)}, bf16[8,128,128]{2,1,0:T(8,128)(2,1)}, u32[]{:S(2)}, u32[]{:S(2)}) collective-permute-start(bf16[8,128,128]{2,1,0:T(8,128)(2,1)} %get-tuple-element.127), channel_id=1, source_target_pairs={{0,16},{4,20},{8,24},{12,28},{16,0},{20,4},{24,8},{28,12},{32,48},... | collective-permute-start | bytes 786440 | tf_op jit(solution)/shard_map/ppermute | solution.py:185
  50.4 23.8 %collective-permute-start.7 = (bf16[8,128,128]{2,1,0:T(8,128)(2,1)}, bf16[8,128,128]{2,1,0:T(8,128)(2,1)}, u32[]{:S(2)}, u32[]{:S(2)}) collective-permute-start(bf16[8,128,128]{2,1,0:T(8,128)(2,1)} %get-tuple-element.127), channel_id=1, source_target_pairs={{0,8},{4,12},{8,0},{12,4},{16,24},{20,28},{24,16},{28,20},{32,40},... | collective-permute-start | bytes 786440 | tf_op jit(solution)/shard_map/ppermute | solution.py:185
  53.1 0.6 copy-start.10
  53.8 4.1 %copy-start.4 = (bf16[64,5,4]{0,2,1:T(4,128)(2,1)}, bf16[64,5,4]{0,2,1:T(4,128)(2,1)S(1)}, u32[]{:S(2)}) copy-start(bf16[64,5,4]{0,2,1:T(4,128)(2,1)S(1)} %get-tuple-element.145) | copy-start | bytes 7684
  53.8 4.1 %copy-start.6 = (bf16[64,5,4]{0,2,1:T(4,128)(2,1)}, bf16[64,5,4]{0,2,1:T(4,128)(2,1)S(1)}, u32[]{:S(2)}) copy-start(bf16[64,5,4]{0,2,1:T(4,128)(2,1)S(1)} %get-tuple-element.146) | copy-start | bytes 7684
  53.9 4.8 %copy-start.8 = (bf16[64,5,4]{0,2,1:T(4,128)(2,1)}, bf16[64,5,4]{0,2,1:T(4,128)(2,1)S(1)}, u32[]{:S(2)}) copy-start(bf16[64,5,4]{0,2,1:T(4,128)(2,1)S(1)} %get-tuple-element.147) | copy-start | bytes 7684
  55.8 32.2 %collective-permute-start.11 = (f32[]{:T(128)}, f32[]{:T(128)}, u32[]{:S(2)}, u32[]{:S(2)}) collective-permute-start(f32[]{:T(128)} %reduce_max.9), channel_id=1, source_target_pairs={{0,1},{1,0},{2,3},{3,2},{4,5},{5,4},{6,7},{7,6},{8,9},{9,8},{10,11... | collective-permute-start | bytes 20 | tf_op jit(solution)/shard_map/ppermute | solution.py:185
  58.8 20.5 %copy-start.5 = (bf16[64,5,4]{0,2,1:T(4,128)(2,1)S(1)}, bf16[64,5,4]{0,2,1:T(4,128)(2,1)}, u32[]{:S(2)}) copy-start(bf16[64,5,4]{0,2,1:T(4,128)(2,1)} %copy-done.4) | copy-start | bytes 7684
  58.8 20.5 %copy-start.7 = (bf16[64,5,4]{0,2,1:T(4,128)(2,1)S(1)}, bf16[64,5,4]{0,2,1:T(4,128)(2,1)}, u32[]{:S(2)}) copy-start(bf16[64,5,4]{0,2,1:T(4,128)(2,1)} %copy-done.6) | copy-start | bytes 7684
  62.1 17.2 %copy-start.9 = (bf16[64,5,4]{0,2,1:T(4,128)(2,1)S(1)}, bf16[64,5,4]{0,2,1:T(4,128)(2,1)}, u32[]{:S(2)}) copy-start(bf16[64,5,4]{0,2,1:T(4,128)(2,1)} %copy-done.8) | copy-start | bytes 7684
  79.3 15.8 %collective-permute-start.10 = (bf16[32,128,128]{2,1,0:T(8,128)(2,1)}, bf16[32,128,128]{2,1,0:T(8,128)(2,1)}, u32[]{:S(2)}, u32[]{:S(2)}) collective-permute-start(bf16[32,128,128]{2,1,0:T(8,128)(2,1)} %constant_dynamic-update-slice_fusion.8), channel_id=1, source_target_pairs={{0,4},{4,0},{8,12},{12,8},{16,20},{20,16},{24,28},{28,24},{32,36},... | collective-permute-start | bytes 3145736 | tf_op jit(solution)/shard_map/ppermute | solution.py:185
  82.4 4.8 %copy-start.16 = (pred[128]{0:T(512)(128)(4,1)S(1)}, pred[128]{0:T(512)(128)(4,1)}, u32[]{:S(2)}) copy-start(pred[128]{0:T(512)(128)(4,1)} %ne.41) | copy-start | bytes 388
  82.4 4.8 %copy-start.17 = (s32[128]{0:T(128)S(1)}, s32[128]{0:T(128)}, u32[]{:S(2)}) copy-start(s32[128]{0:T(128)} %div.12) | copy-start | bytes 1540
  82.4 4.8 %copy-start.18 = (s32[128]{0:T(128)S(1)}, s32[128]{0:T(128)}, u32[]{:S(2)}) copy-start(s32[128]{0:T(128)} %rem.19) | copy-start | bytes 1540
  82.4 4.9 %copy-start.15 = (f32[128]{0:T(128)S(1)}, f32[128]{0:T(128)}, u32[]{:S(2)}) copy-start(f32[128]{0:T(128)} %broadcast_in_dim.289) | copy-start | bytes 1540
  82.4 12.7 %copy-start.11 = (s32[2,64]{1,0:T(2,128)S(1)}, s32[2,64]{1,0:T(2,128)}, u32[]{:S(2)}) copy-start(s32[2,64]{1,0:T(2,128)} %copy-done.10) | copy-start | bytes 1540
  89.2 5.2 %collective-permute-start.12 = (f32[]{:T(128)}, f32[]{:T(128)}, u32[]{:S(2)}, u32[]{:S(2)}) collective-permute-start(f32[]{:T(128)} %max.25), channel_id=1, source_target_pairs={{0,2},{1,3},{2,0},{3,1},{4,6},{5,7},{6,4},{7,5},{8,10},{9,11},{10,... | collective-permute-start | bytes 20 | tf_op jit(solution)/shard_map/ppermute | solution.py:185
  95.1 10.7 %copy-start.13 = (f32[512,1]{0,1:T(1,128)S(1)}, f32[512,1]{0,1:T(1,128)}, u32[]{:S(2)}) copy-start(f32[512,1]{0,1:T(1,128)} %broadcast_in_dim.337) | copy-start | bytes 6148
  101.1 6.3 %collective-permute-start.13 = (bf16[136,512]{1,0:T(8,128)(2,1)}, bf16[136,512]{1,0:T(8,128)(2,1)S(1)}, u32[]{:S(2)}, u32[]{:S(2)}) collective-permute-start(bf16[136,512]{1,0:T(8,128)(2,1)} %get-tuple-element.105), channel_id=1, source_target_pairs={{0,1},{1,0},{2,3},{3,2},{4,5},{5,4},{6,7},{7,6},{8,9},{9,8},{10,11... | collective-permute-start | bytes 417800 | tf_op jit(solution)/shard_map/ppermute | solution.py:185
  102.6 8.9 %collective-permute-start.14 = (bf16[136,512]{1,0:T(8,128)(2,1)}, bf16[136,512]{1,0:T(8,128)(2,1)S(1)}, u32[]{:S(2)}, u32[]{:S(2)}) collective-permute-start(bf16[136,512]{1,0:T(8,128)(2,1)} %get-tuple-element.106), channel_id=1, source_target_pairs={{0,2},{1,3},{2,0},{3,1},{4,6},{5,7},{6,4},{7,5},{8,10},{9,11},{10,... | collective-permute-start | bytes 417800 | tf_op jit(solution)/shard_map/ppermute | solution.py:185
  105.5 7.8 %collective-permute-start.15 = (bf16[136,512]{1,0:T(8,128)(2,1)}, bf16[136,512]{1,0:T(8,128)(2,1)S(1)}, u32[]{:S(2)}, u32[]{:S(2)}) collective-permute-start(bf16[136,512]{1,0:T(8,128)(2,1)} %get-tuple-element.107), channel_id=1, source_target_pairs={{0,3},{1,2},{2,1},{3,0},{4,7},{5,6},{6,5},{7,4},{8,11},{9,10},{10,... | collective-permute-start | bytes 417800 | tf_op jit(solution)/shard_map/ppermute | solution.py:185

commit v5 on v4

--- a/solution.py
+++ b/solution.py
@@ -8,6 +8,7 @@
 PS = 512
 S = 128
 TAPS = 7
+PLANE = 8
 HALF = TAPS // 2
 KS = 5
 PAD = KS // 2
@@ -50,62 +51,9 @@
     return out
 
 
-def repeat_kernel(
-    tiles, owner_ref, routes_ref, offs_ref, wts_ref, taps_ref,
-    exp_ref, rows_ref, cols_ref, out_ref, held, count, found, sems,
-):
-    base = owner_ref[0] * tiles
-    found[0] = 0
-
-    @pl.loop(0, count.shape[0])
-    def _(i):
-        count[i] = 0
-
-    @pl.loop(0, tiles)
-    def _(i):
-        dest = routes_ref[0, base + i]
-        rank = count[dest]
-        count[dest] = rank + 1
-        found[0] = jnp.where(rank > 0, i, found[0])
-
-    tile = found[0]
-    copies = [
-        pltpu.make_async_copy(src.at[tile, 0], held.at[i], sems.at[i])
-        for i, src in enumerate((exp_ref, rows_ref, cols_ref))
-    ]
-    for copy in copies:
-        copy.start()
-    for copy in copies:
-        copy.wait()
-    out_ref[0] = warp_tiles(
-        [tile], base, offs_ref, wts_ref, taps_ref, [held[0]], [held[1]], [held[2]]
-    )[0]
-
-
-def repeat(owner, routes, offs, wts, taps, exposures, warp_rows, warp_cols, npatch):
-    anywhere = pl.BlockSpec(memory_space=pl.ANY)
-    return pl.pallas_call(
-        lambda *refs: repeat_kernel(exposures.shape[0], *refs),
-        name="repeat",
-        out_shape=jax.ShapeDtypeStruct((1, S, S), BF16),
-        grid_spec=pltpu.PrefetchScalarGridSpec(
-            num_scalar_prefetch=5,
-            grid=(1,),
-            in_specs=[anywhere] * 3,
-            out_specs=pl.BlockSpec((1, S, S), lambda i, *_: (0, 0, 0)),
-            scratch_shapes=[
-                pltpu.VMEM((3, S, S), BF16),
-                pltpu.SMEM((npatch,), jnp.int32),
-                pltpu.SMEM((1,), jnp.int32),
-                pltpu.SemaphoreType.DMA((3,)),
-            ],
-        ),
-    )(owner, routes, offs, wts, taps, exposures, warp_rows, warp_cols)
-
-
 def front_kernel(
     per_step, owner_ref, routes_ref, offs_ref, wts_ref, taps_ref,
-    exp_ref, rows_ref, cols_ref, buf0_ref, buf1_ref, stage, count, sems,
+    exp_ref, rows_ref, cols_ref, buf0_ref, buf1_ref, extra_ref, stage, count, sems,
 ):
     step = pl.program_id(0)
     steps = pl.num_programs(0)
@@ -134,6 +82,7 @@
 
         @pl.when(rank > 0)
         def _():
+            extra_ref[...] = jnp.broadcast_to(stage[tile][None], extra_ref.shape)
             pltpu.make_async_copy(stage.at[tile], buf1_ref.at[dest], sems.at[tile]).start()
 
     @pl.when(step == steps - 1)
@@ -143,7 +92,7 @@
             pltpu.make_async_copy(stage.at[i], buf0_ref.at[0], sems.at[i]).wait()
 
 
-def front(owner, routes, offs, wts, taps, exposures, warp_rows, warp_cols, npatch):
+def front(owner, routes, offs, wts, taps, exposures, warp_rows, warp_cols, npatch, copies):
     tiles = exposures.shape[0]
     per_step = 16
     spec = pl.BlockSpec((per_step, None, S, S), lambda i, *_: (i, 0, 0, 0))
@@ -154,13 +103,14 @@
         out_shape=(
             jax.ShapeDtypeStruct((npatch, S, S), BF16),
             jax.ShapeDtypeStruct((npatch, S, S), BF16),
+            jax.ShapeDtypeStruct((copies, S, S), BF16),
         ),
         cost_estimate=pl.CostEstimate(flops=0, bytes_accessed=24 << 20, transcendentals=0),
         grid_spec=pltpu.PrefetchScalarGridSpec(
             num_scalar_prefetch=5,
             grid=(tiles // per_step,),
             in_specs=[spec, spec, spec],
-            out_specs=(anywhere, anywhere),
+            out_specs=(anywhere, anywhere, pl.BlockSpec((copies, S, S), lambda i, *_: (0, 0, 0))),
             scratch_shapes=[
                 pltpu.VMEM((tiles, S, S), BF16),
                 pltpu.SMEM((npatch,), jnp.int32),
@@ -173,11 +123,11 @@
     )(owner, routes, offs, wts, taps, exposures, warp_rows, warp_cols)
 
 
-def spread(index, masks):
-    total = 0
-    for bit, mask in enumerate(masks):
-        total = total | (((index >> bit) & 1) * mask)
-    return total
+def gathered_source(index, owner, rows):
+    step = index // rows
+    return (index % rows) * PLANE + (
+        (owner % PLANE) ^ (((step & 1) << 1) | ((step & 2) << 1) | ((step & 4) >> 2))
+    )
 
 
 def swap(x, axis, mask):
@@ -185,7 +135,7 @@
     return lax.ppermute(x, axis, [(i, i ^ mask) for i in range(size)])
 
 
-def place_kernel(per_step, nband, masks, owner_ref, table_ref, first_ref, *refs):
+def place_kernel(per_step, nband, gathered, owner_ref, table_ref, first_ref, *refs):
     second_refs, (cover_ref, coadd_ref, *strip_refs), (acc, full) = (
         refs[: -nband - 4], refs[-nband - 4 : -2], refs[-2:]
     )
@@ -205,8 +155,8 @@
             source = step * src.shape[0] + k
             if slot > 1:
                 source = source + (slot - 1) * src.shape[0] * steps
-            if slot and masks:
-                source = owner_ref[0] ^ spread(source, masks)
+            if slot and gathered:
+                source = gathered_source(source, owner_ref[0], table_ref.shape[1] // PLANE)
             code = table_ref[min(slot, 1), source]
 
             @pl.when(code > 0)
@@ -248,7 +198,7 @@
             ref[...] = rows[edge // 2 - PAD : edge // 2 - PAD + height].astype(BF16)
 
 
-def place(owner, table, first, seconds, cover, nband, masks):
+def place(owner, table, first, seconds, cover, nband, gathered):
     per_step = 16
     steps = first.shape[0] // per_step
     strip = PS // nband + 8
@@ -256,7 +206,7 @@
         pl.BlockSpec((x.shape[0] // steps, S, S), lambda i, *_: (i, 0, 0)) for x in (first, *seconds)
     ]
     return pl.pallas_call(
-        lambda *refs: place_kernel(per_step, nband, masks, *refs),
+        lambda *refs: place_kernel(per_step, nband, gathered, *refs),
         name="place",
         out_shape=(
             jax.ShapeDtypeStruct((PS, PS), BF16),
@@ -380,15 +330,14 @@
     offs_rows = offsets.transpose(0, 2, 1).reshape(2, -1)
     taps = psf_taps[:, 0].transpose(1, 2, 0).reshape(2 * TAPS, tiles).astype(F32)
     inputs = (owner[None], routes_row, offs_rows, weights, taps, exposures, warp_rows, warp_cols)
-    near = repeat(*inputs, npatch)
-    bits = npatch.bit_length() - 1
-    masks = [1 << bit for bit in [*range(3, bits), 1, 2, 0] if bit < bits]
-    near = [near] + [swap(near, "patch", mask) for mask in range(8, npatch, 8)]
-    buf0, buf1 = front(*inputs, npatch)
+    buf0, buf1, extra = front(*inputs, npatch, npatch // PLANE)
+    lines = [list(range(i, npatch, PLANE)) for i in range(PLANE)]
+    near = lax.all_to_all(
+        extra, "patch", split_axis=0, concat_axis=0, axis_index_groups=lines, tiled=True
+    )
     buf0, near, routes_row, offs_rows, weights, det_weight, det_bias = lax.optimization_barrier(
         (buf0, near, routes_row, offs_rows, weights, det_weight, det_bias)
     )
-    near = jnp.concatenate(near, axis=0)
     near = jnp.concatenate([near] + [swap(near, "patch", m) for m in (2, 4, 6)], axis=0)
     far = swap(near, "patch", 1)
     first = lax.all_to_all(buf0, "patch", split_axis=0, concat_axis=0, tiled=True)
@@ -422,11 +371,11 @@
     where = jnp.stack([owner, band])
 
     def one_repeat():
-        return place(where, table, first, (near, far), cover, nband, masks)
+        return place(where, table, first, (near, far), cover, nband, True)
 
     def any_repeats():
         rest = lax.all_to_all(buf1, "patch", split_axis=0, concat_axis=0, tiled=True)
-        return place(where, table, first, (rest,), cover, nband, None)
+        return place(where, table, first, (rest,), cover, nband, False)
 
     coadd, *strips = lax.cond(repeats <= 1.0, one_repeat, any_repeats)
     strips = strips[:1] + [swap(x, "band", i) for i, x in enumerate(strips) if i]

time: 121 us -> 113 us (0.934)
  starting transfers between devices: 40.4 us -> 30 us
  waiting for transfers between devices: 18 us -> 27 us
  Pallas kernels: 23.4 us -> 20.4 us
  local copies, waits for them, and re-layouts: 23.4 us -> 20.8 us
    ppermute x16 -> x9, starting transfers between devices: 29.8 us -> 14.9 us  [swap(): return lax.ppermute(x, axis, [(i, i ^ mask) for i in range(size)])]
    all_to_all x0 -> x1, waiting for transfers between devices: none -> 9.81 us  [body(): lax.all_to_all(extra, 'patch', split_axis=0, concat_axis=0, axis_index_gr...]
    all_to_all x0 -> x1, starting transfers between devices: none -> 8.64 us  [body(): lax.all_to_all(extra, 'patch', split_axis=0, concat_axis=0, axis_index_gr...]
    all_to_all x1, starting transfers between devices: 10.6 us -> 6.47 us  [body(): lax.all_to_all(buf0, 'patch', split_axis=0, concat_axis=0, tiled=True)]
    pallas_call x2 -> x1, Pallas kernels: 10.2 us -> 6.31 us  [place(): pl.pallas_call(lambda *refs: place_kernel(per_step, nband, gathered, *ref...]
    unnamed x47 -> x19, local copies, waits for them, and re-layouts: 8.38 us -> 5.09 us
    ppermute x16 -> x9, waiting for transfers between devices: 18 us -> 16.4 us  [swap(): return lax.ppermute(x, axis, [(i, i ^ mask) for i in range(size)])]
  transfers between devices with their start and end apart: 17 -> 11, of which waited for: 5 -> 7; matrix products, arithmetic and copies ran while one was open for 27% -> 27% of each run, Pallas kernels for 6% -> 0%
where the time goes in v5:
time: 113 us; the launch traced here: 112 us
  starting transfers between devices  30 us (27%)
  waiting for transfers between devices  27 us (24%)
  local copies, waits for them, and re-layouts  20.8 us (18%)
  Pallas kernels  20.4 us (18%)
  other arithmetic  9.92 us (9%)
  between operations  2.8 us (2%)
    ppermute x9, waiting for transfers between devices, swap(): return lax.ppermute(x, axis, [(i, i ^ mask) for i in range(size)])  16.4 us
    ppermute x9, starting transfers between devices, swap(): return lax.ppermute(x, axis, [(i, i ^ mask) for i in range(size)])  14.9 us
    all_to_all x1, waiting for transfers between devices, body(): lax.all_to_all(extra, 'patch', split_axis=0, concat_axis=0, axis_index_gr...  9.81 us
    all_to_all x1, starting transfers between devices, body(): lax.all_to_all(extra, 'patch', split_axis=0, concat_axis=0, axis_index_gr...  8.64 us
    pallas_call x1, Pallas kernels, front(): pl.pallas_call(lambda *refs: front_kernel(per_step, *refs), name='front',...  8.5 us
    select_n x4, local copies, waits for them, and re-layouts, toeplitz(): total = jnp.where(on, taps[:, None, :, :, r, None], total)  6.83 us
    all_to_all x1, starting transfers between devices, body(): lax.all_to_all(buf0, 'patch', split_axis=0, concat_axis=0, tiled=True)  6.47 us
    pallas_call x1, Pallas kernels, place(): pl.pallas_call(lambda *refs: place_kernel(per_step, nband, gathered, *ref...  6.31 us
  transfers between devices with their start and end apart: 11, of which 7 were waited for; matrix products, arithmetic and copies ran while one was open for 27% of the time, Pallas kernels for 0%

profile of v5, /device:TPU:32, one launch (start us, length us, event | category | flops | bytes accessed | tf_op | source)
XLA Modules:
  0.0 111.6 jit_solution(12396169174381019549)
XLA Ops:
  0.6 0.7 convert_bitcast_fusion
  1.3 0.6 reshape.320.refs_4_
  1.9 8.5 %front.1 = (bf16[64,128,128]{2,1,0:T(8,128)(2,1)}, bf16[64,128,128]{2,1,0:T(8,128)(2,1)}, bf16[8,128,128]{2,1,0:T(8,128)(2,1)}) custom-call(s32[1]{0:T(128)} %bitcast.2.refs_0_, s32[1,2048]{1,0:T(1,128)} %bitcast.47, s32[2,2048]{1,0:T(2,128)} %bitcast.45, f32[1,2048]{1,0:T(1,128)} %refs_3_.1, f32[14,32]{1,0:T(8,128)} %reshape.320.refs_4_, ...), custom_call_target="tpu_custom_call" | custom-call | bytes 25165824 | tf_op jit(solution)/shard_map/front/pallas_call | solution.py:100
  10.4 8.6 %all-to-all-start.1 = ((bf16[8,128,128]{2,1,0:T(8,128)(2,1)}), bf16[8,128,128]{2,1,0:T(8,128)(2,1)}, u32[]{:S(2)}, u32[]{:S(2)}) async-start(bf16[8,128,128]{2,1,0:T(8,128)(2,1)} %get-tuple-element.76), calls=%async_computation.1 | async-start | bytes 524288 | tf_op jit(solution)/shard_map/all_to_all | solution.py:335
  19.1 0.5 fusion.23
  19.7 0.1 fusion.28
  19.7 9.8 %all-to-all-done.1 = bf16[8,128,128]{2,1,0:T(8,128)(2,1)} async-done(((bf16[8,128,128]{2,1,0:T(8,128)(2,1)}), bf16[8,128,128]{2,1,0:T(8,128)(2,1)}, u32[]{:S(2)}, u32[]{:S(2)}) %all-to-all-start.1) | async-done | bytes 262176 | tf_op jit(solution)/shard_map/all_to_all | solution.py:335
  29.6 6.5 %all-to-all-start.2 = ((bf16[64,128,128]{2,1,0:T(8,128)(2,1)}), bf16[64,128,128]{2,1,0:T(8,128)(2,1)S(1)}, u32[]{:S(2)}, u32[]{:S(2)}) async-start(bf16[64,128,128]{2,1,0:T(8,128)(2,1)} %get-tuple-element.77), calls=%async_computation.2 | async-start | bytes 4194304 | tf_op jit(solution)/shard_map/all_to_all | solution.py:343
  36.1 0.7 pad_add_fusion
  36.7 2.7 %collective-permute-start.2 = (bf16[8,128,128]{2,1,0:T(8,128)(2,1)}, bf16[8,128,128]{2,1,0:T(8,128)(2,1)}, u32[]{:S(2)}, u32[]{:S(2)}) collective-permute-start(bf16[8,128,128]{2,1,0:T(8,128)(2,1)} %all-to-all-done.1), channel_id=1, source_target_pairs={{0,24},{4,28},{8,16},{12,20},{16,8},{20,12},{24,0},{28,4},{32,56},... | collective-permute-start | bytes 786440 | tf_op jit(solution)/shard_map/ppermute | solution.py:135
  39.4 0.9 collective-permute-start.1
  40.2 0.6 collective-permute-start
  40.8 0.5 broadcast.375
  41.3 0.7 reduce.10
  42.0 0.1 reshape.318
  42.1 0.1 copy.29
  42.2 0.2 reduce_window_sum.11
  42.4 0.1 copy.23
  42.4 0.1 copy.22
  42.6 0.1 add.77
  42.6 0.1 copy.24
  42.7 0.1 copy.26
  42.9 0.2 and_reduce_fusion
  43.2 0.5 sign_compare_fusion
  43.7 0.6 broadcast_shift-right-logical_fusion
  44.3 0.1 select_add_fusion
  44.4 1.0 select_select_fusion.1
  45.4 1.7 %constant_dynamic-update-slice_fusion.3 = bf16[32,128,128]{2,1,0:T(8,128)(2,1)} fusion(bf16[8,128,128]{2,1,0:T(8,128)(2,1)} %all-to-all-done.1), kind=kLoop, calls=%fused_computation.36 | loop fusion | bytes 524288
  47.1 0.7 reduce_max.9
  47.8 1.5 %collective-permute-start.4 = (f32[]{:T(128)}, f32[]{:T(128)}, u32[]{:S(2)}, u32[]{:S(2)}) collective-permute-start(f32[]{:T(128)} %reduce_max.9), channel_id=1, source_target_pairs={{0,1},{1,0},{2,3},{3,2},{4,5},{5,4},{6,7},{7,6},{8,9},{9,8},{10,11... | collective-permute-start | bytes 20 | tf_op jit(solution)/shard_map/ppermute | solution.py:135
  49.4 0.6 broadcast.376
  49.9 0.7 reduce.11
  50.7 0.1 broadcast_in_dim.286
  50.7 0.1 copy.25
  50.8 1.2 %ne.41 = pred[128]{0:T(512)(128)(4,1)} reshape(pred[2,64]{1,0:T(4,128)(4,1)} %sign_compare_fusion) | data formatting | bytes 256 | tf_op jit(solution)/shard_map/jit(floor_divide)/ne | solution.py:359
  52.1 1.3 %div.12 = s32[128]{0:T(128)} reshape(s32[2,64]{1,0:T(2,128)} %get-tuple-element.120) | data formatting | bytes 1024 | tf_op jit(solution)/shard_map/jit(floor_divide)/div | solution.py:359
  53.4 0.6 rem.19
  54.0 0.6 broadcast_in_dim.289
  54.6 0.7 broadcast_in_dim.336
  55.4 0.1 broadcast_in_dim.337
  55.5 2.0 %reshape.322 = bf16[512,80]{0,1:T(8,128)(2,1)S(1)} reshape(bf16[64,8,5,4,4]{1,0,4,3,2:T(8,128)(2,1)S(1)} %select_select_fusion.1) | data formatting | bytes 163840 | tf_op jit(solution)/shard_map/jit(_where)/select_n | solution.py:312
  57.5 0.1 copy.28
  57.6 7.3 %collective-permute-done = bf16[8,128,128]{2,1,0:T(8,128)(2,1)} collective-permute-done((bf16[8,128,128]{2,1,0:T(8,128)(2,1)}, bf16[8,128,128]{2,1,0:T(8,128)(2,1)}, u32[]{:S(2)}, u32[]{:S(2)}) %collective-permute-start) | collective-permute-done | bytes 262176 | tf_op jit(solution)/shard_map/ppermute | solution.py:135
  64.9 1.7 %constant_dynamic-update-slice_fusion.2 = bf16[32,128,128]{2,1,0:T(8,128)(2,1)} fusion(bf16[32,128,128]{2,1,0:T(8,128)(2,1)} %constant_dynamic-update-slice_fusion.3, bf16[8,128,128]{2,1,0:T(8,128)(2,1)} %collective-permute-done), kind=kLoop, calls=%fused_computation.35 | loop fusion | bytes 524288
  66.6 1.7 %constant_dynamic-update-slice_fusion.1 = bf16[32,128,128]{2,1,0:T(8,128)(2,1)} fusion(bf16[32,128,128]{2,1,0:T(8,128)(2,1)} %constant_dynamic-update-slice_fusion.2, bf16[8,128,128]{2,1,0:T(8,128)(2,1)} %collective-permute-done.1), kind=kLoop, calls=%fused_computation.34 | loop fusion | bytes 524288
  68.3 1.7 %constant_dynamic-update-slice_fusion = bf16[32,128,128]{2,1,0:T(8,128)(2,1)} fusion(bf16[32,128,128]{2,1,0:T(8,128)(2,1)} %constant_dynamic-update-slice_fusion.1, bf16[8,128,128]{2,1,0:T(8,128)(2,1)} %collective-permute-done.2), kind=kLoop, calls=%fused_computation.33 | loop fusion | bytes 524288 | tf_op jit(solution)/shard_map/concatenate | solution.py:341
  69.9 3.0 %select_select_fusion = bf16[64,8,5,4,8]{1,0,4,3,2:T(8,128)(2,1)} fusion(pred[8,8]{0,1:T(8,128)(4,1)S(1)} %get-tuple-element.133, pred[8,8]{0,1:T(8,128)(4,1)S(1)} %get-tuple-element.134, pred[8,8]{0,1:T(8,128)(4,1)S(1)} %get-tuple-element.135, pred[8,8]{0,1:T(8,128)(4,1)S(1)} %get-tuple-element.136, pred[8,8]{0,1:T(8,128)(4,1)} %fusion.23, ...), kind=kLoop, calls=%fused_computation | loop fusion | flops 409600 | bytes 176960 | tf_op jit(solution)/shard_map/jit(_where)/select_n | solution.py:312
  72.9 4.5 %reshape.321 = bf16[512,160]{0,1:T(8,128)(2,1)S(1)} reshape(bf16[64,8,5,4,8]{1,0,4,3,2:T(8,128)(2,1)} %select_select_fusion) | data formatting | bytes 327680 | tf_op jit(solution)/shard_map/jit(_where)/select_n | solution.py:312
  77.5 0.1 copy.27
  77.6 0.1 pad_maximum_fusion.refs_4_
  77.8 0.7 fusion.2
  79.8 4.6 %collective-permute-start.5 = (f32[]{:T(128)}, f32[]{:T(128)}, u32[]{:S(2)}, u32[]{:S(2)}) collective-permute-start(f32[]{:T(128)} %max.25), channel_id=1, source_target_pairs={{0,2},{1,3},{2,0},{3,1},{4,6},{5,7},{6,4},{7,5},{8,10},{9,11},{10,... | collective-permute-start | bytes 20 | tf_op jit(solution)/shard_map/ppermute | solution.py:135
  84.4 0.7 collective-permute-done.5
  85.7 0.8 all-to-all-done.2
  86.5 6.3 %conditional.1 = (bf16[136,512]{1,0:T(8,128)(2,1)S(1)}, bf16[136,512]{1,0:T(8,128)(2,1)}, bf16[136,512]{1,0:T(8,128)(2,1)}, bf16[136,512]{1,0:T(8,128)(2,1)}, bf16[1,1,512,512]{3,2,1,0:T(8,128)(2,1)}) conditional(s32[]{:T(128)} %convert_element_type.34, (bf16[64,128,128]{2,1,0:T(8,128)(2,1)}, s32[2]{0:T(128)}, s32[2,64]{1,0:T(2,128)S(1)}, ...), branch_computations={%region_6.7_spmd, %region_7.8_spmd} | conditional | bytes 4194344 | solution.py:380
  86.5 6.3 %place.3 = (bf16[512,512]{1,0:T(8,128)(2,1)}, bf16[136,512]{1,0:T(8,128)(2,1)S(1)}, bf16[136,512]{1,0:T(8,128)(2,1)}, bf16[136,512]{1,0:T(8,128)(2,1)}, bf16[136,512]{1,0:T(8,128)(2,1)}) custom-call(s32[2]{0:T(128)} %get-tuple-element.44.refs_0_, s32[2,64]{1,0:T(2,128)S(1)} %get-tuple-element.45.refs_1_, ...), custom_call_target="tpu_custom_call" | custom-call | tf_op jit(solution)/shard_map/cond/branch_1_fun/place/pallas_call | solution.py:208
  92.8 1.5 %collective-permute-start.6 = (bf16[136,512]{1,0:T(8,128)(2,1)}, bf16[136,512]{1,0:T(8,128)(2,1)S(1)}, u32[]{:S(2)}, u32[]{:S(2)}) collective-permute-start(bf16[136,512]{1,0:T(8,128)(2,1)} %get-tuple-element.93), channel_id=1, source_target_pairs={{0,1},{1,0},{2,3},{3,2},{4,5},{5,4},{6,7},{7,6},{8,9},{9,8},{10,11... | collective-permute-start | bytes 417800 | tf_op jit(solution)/shard_map/ppermute | solution.py:135
  94.3 2.7 %collective-permute-start.7 = (bf16[136,512]{1,0:T(8,128)(2,1)}, bf16[136,512]{1,0:T(8,128)(2,1)S(1)}, u32[]{:S(2)}, u32[]{:S(2)}) collective-permute-start(bf16[136,512]{1,0:T(8,128)(2,1)} %get-tuple-element.94), channel_id=1, source_target_pairs={{0,2},{1,3},{2,0},{3,1},{4,6},{5,7},{6,4},{7,5},{8,10},{9,11},{10,... | collective-permute-start | bytes 417800 | tf_op jit(solution)/shard_map/ppermute | solution.py:135
  96.9 0.5 collective-permute-start.8
  97.5 0.1 copy.31.refs_5_
  97.6 1.5 %collective-permute-done.6.refs_1_ = bf16[136,512]{1,0:T(8,128)(2,1)S(1)} collective-permute-done((bf16[136,512]{1,0:T(8,128)(2,1)}, bf16[136,512]{1,0:T(8,128)(2,1)S(1)}, u32[]{:S(2)}, u32[]{:S(2)}) %collective-permute-start.6) | collective-permute-done | bytes 139296 | tf_op jit(solution)/shard_map/ppermute | solution.py:135
  99.1 4.7 %collective-permute-done.7.refs_2_ = bf16[136,512]{1,0:T(8,128)(2,1)S(1)} collective-permute-done((bf16[136,512]{1,0:T(8,128)(2,1)}, bf16[136,512]{1,0:T(8,128)(2,1)S(1)}, u32[]{:S(2)}, u32[]{:S(2)}) %collective-permute-start.7) | collective-permute-done | bytes 139296 | tf_op jit(solution)/shard_map/ppermute | solution.py:135
  103.8 2.2 %collective-permute-done.8.refs_3_ = bf16[136,512]{1,0:T(8,128)(2,1)S(1)} collective-permute-done((bf16[136,512]{1,0:T(8,128)(2,1)}, bf16[136,512]{1,0:T(8,128)(2,1)S(1)}, u32[]{:S(2)}, u32[]{:S(2)}) %collective-permute-start.8) | collective-permute-done | bytes 139296 | tf_op jit(solution)/shard_map/ppermute | solution.py:135
  106.0 5.6 %detect.1 = bf16[64,128,512]{2,1,0:T(8,128)(2,1)} custom-call(bf16[136,512]{1,0:T(8,128)(2,1)S(1)} %get-tuple-element.92.refs_0_, bf16[136,512]{1,0:T(8,128)(2,1)S(1)} %collective-permute-done.6.refs_1_, bf16[136,512]{1,0:T(8,128)(2,1)S(1)} %collective-permute-done.7.refs_2_, bf16[136,512]{1,0:T(8,128)(2,1)S(1)} %collective-permute-done.8.refs_3_, ...), custom_call_target="tpu_custom_call" | custom-call | tf_op jit(solution)/shard_map/detect/pallas_call | solution.py:274
  (38 shorter events, 0.3 us)
Async XLA Ops:
  10.4 19.1 %all-to-all-start.1 = ((bf16[8,128,128]{2,1,0:T(8,128)(2,1)}), bf16[8,128,128]{2,1,0:T(8,128)(2,1)}, u32[]{:S(2)}, u32[]{:S(2)}) async-start(bf16[8,128,128]{2,1,0:T(8,128)(2,1)} %get-tuple-element.76), calls=%async_computation.1 | async-start | bytes 524288 | tf_op jit(solution)/shard_map/all_to_all | solution.py:335
  29.6 11.8 %copy-start.1 = (s32[1,2048,1]{1,2,0:T(1,128)S(1)}, s32[1,2048,1]{1,2,0:T(1,128)}, u32[]{:S(2)}) copy-start(s32[1,2048,1]{1,2,0:T(1,128)} %param.15) | copy-start | bytes 24580
  29.6 13.0 %copy-start = (s32[1,2048,2]{1,2,0:T(2,128)S(1)}, s32[1,2048,2]{1,2,0:T(2,128)}, u32[]{:S(2)}) copy-start(s32[1,2048,2]{1,2,0:T(2,128)} %param.16) | copy-start | bytes 49156
  29.6 13.2 %copy-start.3 = (bf16[64,100]{1,0:T(8,128)(2,1)S(1)}, bf16[64,100]{1,0:T(8,128)(2,1)}, u32[]{:S(2)}) copy-start(bf16[64,100]{1,0:T(8,128)(2,1)} %param.18) | copy-start | bytes 38404
  29.6 56.9 %all-to-all-start.2 = ((bf16[64,128,128]{2,1,0:T(8,128)(2,1)}), bf16[64,128,128]{2,1,0:T(8,128)(2,1)S(1)}, u32[]{:S(2)}, u32[]{:S(2)}) async-start(bf16[64,128,128]{2,1,0:T(8,128)(2,1)} %get-tuple-element.77), calls=%async_computation.2 | async-start | bytes 4194304 | tf_op jit(solution)/shard_map/all_to_all | solution.py:343
  36.0 13.9 %copy-start.2 = (f32[1,2048]{1,0:T(1,128)S(1)}, f32[1,2048]{1,0:T(1,128)}, u32[]{:S(2)}) copy-start(f32[1,2048]{1,0:T(1,128)} %refs_3_.1) | copy-start | bytes 24580
  36.7 31.6 %collective-permute-start.2 = (bf16[8,128,128]{2,1,0:T(8,128)(2,1)}, bf16[8,128,128]{2,1,0:T(8,128)(2,1)}, u32[]{:S(2)}, u32[]{:S(2)}) collective-permute-start(bf16[8,128,128]{2,1,0:T(8,128)(2,1)} %all-to-all-done.1), channel_id=1, source_target_pairs={{0,24},{4,28},{8,16},{12,20},{16,8},{20,12},{24,0},{28,4},{32,56},... | collective-permute-start | bytes 786440 | tf_op jit(solution)/shard_map/ppermute | solution.py:135
  39.4 27.2 %collective-permute-start.1 = (bf16[8,128,128]{2,1,0:T(8,128)(2,1)}, bf16[8,128,128]{2,1,0:T(8,128)(2,1)}, u32[]{:S(2)}, u32[]{:S(2)}) collective-permute-start(bf16[8,128,128]{2,1,0:T(8,128)(2,1)} %all-to-all-done.1), channel_id=1, source_target_pairs={{0,16},{4,20},{8,24},{12,28},{16,0},{20,4},{24,8},{28,12},{32,48},... | collective-permute-start | bytes 786440 | tf_op jit(solution)/shard_map/ppermute | solution.py:135
  40.2 24.7 %collective-permute-start = (bf16[8,128,128]{2,1,0:T(8,128)(2,1)}, bf16[8,128,128]{2,1,0:T(8,128)(2,1)}, u32[]{:S(2)}, u32[]{:S(2)}) collective-permute-start(bf16[8,128,128]{2,1,0:T(8,128)(2,1)} %all-to-all-done.1), channel_id=1, source_target_pairs={{0,8},{4,12},{8,0},{12,4},{16,24},{20,28},{24,16},{28,20},{32,40},... | collective-permute-start | bytes 786440 | tf_op jit(solution)/shard_map/ppermute | solution.py:135
  47.8 30.7 %collective-permute-start.4 = (f32[]{:T(128)}, f32[]{:T(128)}, u32[]{:S(2)}, u32[]{:S(2)}) collective-permute-start(f32[]{:T(128)} %reduce_max.9), channel_id=1, source_target_pairs={{0,1},{1,0},{2,3},{3,2},{4,5},{5,4},{6,7},{7,6},{8,9},{9,8},{10,11... | collective-permute-start | bytes 20 | tf_op jit(solution)/shard_map/ppermute | solution.py:135
  69.9 15.7 %collective-permute-start.3 = (bf16[32,128,128]{2,1,0:T(8,128)(2,1)}, bf16[32,128,128]{2,1,0:T(8,128)(2,1)}, u32[]{:S(2)}, u32[]{:S(2)}) collective-permute-start(bf16[32,128,128]{2,1,0:T(8,128)(2,1)} %constant_dynamic-update-slice_fusion), channel_id=1, source_target_pairs={{0,4},{4,0},{8,12},{12,8},{16,20},{20,16},{24,28},{28,24},{32,36},... | collective-permute-start | bytes 3145736 | tf_op jit(solution)/shard_map/ppermute | solution.py:135
  72.9 4.8 %copy-start.5 = (pred[128]{0:T(512)(128)(4,1)S(1)}, pred[128]{0:T(512)(128)(4,1)}, u32[]{:S(2)}) copy-start(pred[128]{0:T(512)(128)(4,1)} %ne.41) | copy-start | bytes 388
  72.9 4.8 %copy-start.6 = (s32[128]{0:T(128)S(1)}, s32[128]{0:T(128)}, u32[]{:S(2)}) copy-start(s32[128]{0:T(128)} %div.12) | copy-start | bytes 1540
  72.9 4.8 %copy-start.7 = (s32[128]{0:T(128)S(1)}, s32[128]{0:T(128)}, u32[]{:S(2)}) copy-start(s32[128]{0:T(128)} %rem.19) | copy-start | bytes 1540
  72.9 4.9 %copy-start.4 = (f32[128]{0:T(128)S(1)}, f32[128]{0:T(128)}, u32[]{:S(2)}) copy-start(f32[128]{0:T(128)} %broadcast_in_dim.289) | copy-start | bytes 1540
  79.8 5.2 %collective-permute-start.5 = (f32[]{:T(128)}, f32[]{:T(128)}, u32[]{:S(2)}, u32[]{:S(2)}) collective-permute-start(f32[]{:T(128)} %max.25), channel_id=1, source_target_pairs={{0,2},{1,3},{2,0},{3,1},{4,6},{5,7},{6,4},{7,5},{8,10},{9,11},{10,... | collective-permute-start | bytes 20 | tf_op jit(solution)/shard_map/ppermute | solution.py:135
  92.8 6.3 %collective-permute-start.6 = (bf16[136,512]{1,0:T(8,128)(2,1)}, bf16[136,512]{1,0:T(8,128)(2,1)S(1)}, u32[]{:S(2)}, u32[]{:S(2)}) collective-permute-start(bf16[136,512]{1,0:T(8,128)(2,1)} %get-tuple-element.93), channel_id=1, source_target_pairs={{0,1},{1,0},{2,3},{3,2},{4,5},{5,4},{6,7},{7,6},{8,9},{9,8},{10,11... | collective-permute-start | bytes 417800 | tf_op jit(solution)/shard_map/ppermute | solution.py:135
  94.3 9.5 %collective-permute-start.7 = (bf16[136,512]{1,0:T(8,128)(2,1)}, bf16[136,512]{1,0:T(8,128)(2,1)S(1)}, u32[]{:S(2)}, u32[]{:S(2)}) collective-permute-start(bf16[136,512]{1,0:T(8,128)(2,1)} %get-tuple-element.94), channel_id=1, source_target_pairs={{0,2},{1,3},{2,0},{3,1},{4,6},{5,7},{6,4},{7,5},{8,10},{9,11},{10,... | collective-permute-start | bytes 417800 | tf_op jit(solution)/shard_map/ppermute | solution.py:135
  96.9 9.1 %collective-permute-start.8 = (bf16[136,512]{1,0:T(8,128)(2,1)}, bf16[136,512]{1,0:T(8,128)(2,1)S(1)}, u32[]{:S(2)}, u32[]{:S(2)}) collective-permute-start(bf16[136,512]{1,0:T(8,128)(2,1)} %get-tuple-element.95), channel_id=1, source_target_pairs={{0,3},{1,2},{2,1},{3,0},{4,7},{5,6},{6,5},{7,4},{8,11},{9,10},{10,... | collective-permute-start | bytes 417800 | tf_op jit(solution)/shard_map/ppermute | solution.py:135

commit v6 on v4

--- a/solution.py
+++ b/solution.py
@@ -8,6 +8,7 @@
 PS = 512
 S = 128
 TAPS = 7
+PLANE = 8
 HALF = TAPS // 2
 KS = 5
 PAD = KS // 2
@@ -77,22 +78,23 @@
         copy.start()
     for copy in copies:
         copy.wait()
-    out_ref[0] = warp_tiles(
+    warped = warp_tiles(
         [tile], base, offs_ref, wts_ref, taps_ref, [held[0]], [held[1]], [held[2]]
-    )[0]
-
-
-def repeat(owner, routes, offs, wts, taps, exposures, warp_rows, warp_cols, npatch):
+    )
+    out_ref[...] = jnp.broadcast_to(warped[0][None], out_ref.shape)
+
+
+def repeat(owner, routes, offs, wts, taps, exposures, warp_rows, warp_cols, npatch, copies):
     anywhere = pl.BlockSpec(memory_space=pl.ANY)
     return pl.pallas_call(
         lambda *refs: repeat_kernel(exposures.shape[0], *refs),
         name="repeat",
-        out_shape=jax.ShapeDtypeStruct((1, S, S), BF16),
+        out_shape=jax.ShapeDtypeStruct((copies, S, S), BF16),
         grid_spec=pltpu.PrefetchScalarGridSpec(
             num_scalar_prefetch=5,
             grid=(1,),
             in_specs=[anywhere] * 3,
-            out_specs=pl.BlockSpec((1, S, S), lambda i, *_: (0, 0, 0)),
+            out_specs=pl.BlockSpec((copies, S, S), lambda i, *_: (0, 0, 0)),
             scratch_shapes=[
                 pltpu.VMEM((3, S, S), BF16),
                 pltpu.SMEM((npatch,), jnp.int32),
@@ -173,11 +175,11 @@
     )(owner, routes, offs, wts, taps, exposures, warp_rows, warp_cols)
 
 
-def spread(index, masks):
-    total = 0
-    for bit, mask in enumerate(masks):
-        total = total | (((index >> bit) & 1) * mask)
-    return total
+def gathered_source(index, owner, rows):
+    step = index // rows
+    return (index % rows) * PLANE + (
+        (owner % PLANE) ^ (((step & 1) << 1) | ((step & 2) << 1) | ((step & 4) >> 2))
+    )
 
 
 def swap(x, axis, mask):
@@ -185,7 +187,7 @@
     return lax.ppermute(x, axis, [(i, i ^ mask) for i in range(size)])
 
 
-def place_kernel(per_step, nband, masks, owner_ref, table_ref, first_ref, *refs):
+def place_kernel(per_step, nband, gathered, owner_ref, table_ref, first_ref, *refs):
     second_refs, (cover_ref, coadd_ref, *strip_refs), (acc, full) = (
         refs[: -nband - 4], refs[-nband - 4 : -2], refs[-2:]
     )
@@ -205,8 +207,8 @@
             source = step * src.shape[0] + k
             if slot > 1:
                 source = source + (slot - 1) * src.shape[0] * steps
-            if slot and masks:
-                source = owner_ref[0] ^ spread(source, masks)
+            if slot and gathered:
+                source = gathered_source(source, owner_ref[0], table_ref.shape[1] // PLANE)
             code = table_ref[min(slot, 1), source]
 
             @pl.when(code > 0)
@@ -248,7 +250,7 @@
             ref[...] = rows[edge // 2 - PAD : edge // 2 - PAD + height].astype(BF16)
 
 
-def place(owner, table, first, seconds, cover, nband, masks):
+def place(owner, table, first, seconds, cover, nband, gathered):
     per_step = 16
     steps = first.shape[0] // per_step
     strip = PS // nband + 8
@@ -256,7 +258,7 @@
         pl.BlockSpec((x.shape[0] // steps, S, S), lambda i, *_: (i, 0, 0)) for x in (first, *seconds)
     ]
     return pl.pallas_call(
-        lambda *refs: place_kernel(per_step, nband, masks, *refs),
+        lambda *refs: place_kernel(per_step, nband, gathered, *refs),
         name="place",
         out_shape=(
             jax.ShapeDtypeStruct((PS, PS), BF16),
@@ -346,22 +348,24 @@
 
 
 def toeplitz(det_weight, nband, band):
-    channels = det_weight.shape[0]
-    taps = det_weight.reshape(channels, nband, KS, KS).transpose(0, 3, 1, 2)
-    order = jnp.arange(nband) ^ band
-    taps = sum(
-        jnp.where((order == b)[None, None, :, None], taps[:, :, b : b + 1], 0) for b in range(nband)
-    )
-    row_out = jnp.arange(8)[:, None]
-    out = []
-    for lo, hi in ((0, 8), (8, 12)):
-        row_in = jnp.arange(lo, hi)[None, :]
-        total = jnp.zeros((channels, 8, KS, nband, hi - lo), det_weight.dtype)
-        for r in range(KS):
-            on = (row_in - row_out == r)[None, :, None, None, :]
-            total = jnp.where(on, taps[:, None, :, :, r, None], total)
-        out.append(total.reshape(channels * 8, KS * nband * (hi - lo)))
-    return jnp.concatenate(out, axis=1)
+    channels, inputs = det_weight.shape
+    combos = KS * nband
+    column = jnp.arange(combos * 12, dtype=jnp.int32)
+    tail = column >= combos * 8
+    combo = jnp.where(tail, (column - combos * 8) >> 2, column >> 3)
+    row_in = jnp.where(tail, 8 + ((column - combos * 8) & 3), column & 7)
+    shift, slot = combo // nband, combo % nband
+    source = (slot ^ band) * (KS * KS) + shift
+    rows = jnp.arange(KS, dtype=jnp.int32)[:, None] * KS + source[None, :]
+    pick = (jnp.arange(inputs, dtype=jnp.int32)[:, None, None] == rows[None]).astype(BF16)
+    taps = lax.dot_general(
+        det_weight, pick, (((1,), (0,)), ((), ())), preferred_element_type=F32
+    )
+    offset = row_in[None, :] - jnp.arange(8, dtype=jnp.int32)[:, None]
+    total = jnp.zeros((channels, 8, combos * 12), F32)
+    for r in range(KS):
+        total = jnp.where((offset == r)[None], taps[:, None, r], total)
+    return total.astype(BF16).reshape(channels * 8, combos * 12)
 
 
 def slot_select(targets, capacity):
@@ -380,17 +384,17 @@
     offs_rows = offsets.transpose(0, 2, 1).reshape(2, -1)
     taps = psf_taps[:, 0].transpose(1, 2, 0).reshape(2 * TAPS, tiles).astype(F32)
     inputs = (owner[None], routes_row, offs_rows, weights, taps, exposures, warp_rows, warp_cols)
-    near = repeat(*inputs, npatch)
-    bits = npatch.bit_length() - 1
-    masks = [1 << bit for bit in [*range(3, bits), 1, 2, 0] if bit < bits]
-    near = [near] + [swap(near, "patch", mask) for mask in range(8, npatch, 8)]
+    extra = repeat(*inputs, npatch, npatch // PLANE)
+    lines = [list(range(i, npatch, PLANE)) for i in range(PLANE)]
+    near = lax.all_to_all(
+        extra, "patch", split_axis=0, concat_axis=0, axis_index_groups=lines, tiled=True
+    )
     buf0, buf1 = front(*inputs, npatch)
     buf0, near, routes_row, offs_rows, weights, det_weight, det_bias = lax.optimization_barrier(
         (buf0, near, routes_row, offs_rows, weights, det_weight, det_bias)
     )
-    near = jnp.concatenate(near, axis=0)
-    near = jnp.concatenate([near] + [swap(near, "patch", m) for m in (2, 4, 6)], axis=0)
-    far = swap(near, "patch", 1)
+    near = [near] + [swap(near, "patch", m) for m in (2, 4, 6)]
+    far = [swap(x, "patch", 1) for x in near]
     first = lax.all_to_all(buf0, "patch", split_axis=0, concat_axis=0, tiled=True)
     dest_all = routes_row.reshape(npatch, tiles)
     same = (dest_all[:, :, None] == dest_all[:, None, :]) & (
@@ -407,8 +411,8 @@
     ).reshape(-1)
     slot_corner = jnp.maximum(table.reshape(-1) - 1, 0)
     pixels = jnp.arange(PS, dtype=jnp.int32)
-    down = pixels[None, :] - (slot_corner // PS)[:, None]
-    right = pixels[None, :] - (slot_corner % PS)[:, None]
+    down = pixels[None, :] - (slot_corner >> (PS.bit_length() - 1))[:, None]
+    right = pixels[None, :] - (slot_corner & (PS - 1))[:, None]
     row_cover = jnp.where((down >= 0) & (down < S), slot_weights[:, None], 0.0)
     col_cover = ((right >= 0) & (right < S)).astype(F32)
     cover = jnp.einsum("ky,kx->yx", row_cover, col_cover, precision=lax.Precision.HIGHEST)
@@ -422,11 +426,11 @@
     where = jnp.stack([owner, band])
 
     def one_repeat():
-        return place(where, table, first, (near, far), cover, nband, masks)
+        return place(where, table, first, (*near, *far), cover, nband, True)
 
     def any_repeats():
         rest = lax.all_to_all(buf1, "patch", split_axis=0, concat_axis=0, tiled=True)
-        return place(where, table, first, (rest,), cover, nband, None)
+        return place(where, table, first, (rest,), cover, nband, False)
 
     coadd, *strips = lax.cond(repeats <= 1.0, one_repeat, any_repeats)
     strips = strips[:1] + [swap(x, "band", i) for i, x in enumerate(strips) if i]

time: 121 us -> 110 us (0.909); the launches traced: 119 us -> 109 us
  waiting for transfers between devices: 18 us -> 42.8 us
  local copies, waits for them, and re-layouts: 23.4 us -> 2.77 us
  starting transfers between devices: 40.4 us -> 31.9 us
  other arithmetic: 9.99 us -> 3.53 us
    ppermute x16 -> x12, starting transfers between devices: 29.8 us -> 15.9 us  [swap(): return lax.ppermute(x, axis, [(i, i ^ mask) for i in range(size)])]
    all_to_all x1, waiting for transfers between devices: 0.01 us -> 11.1 us  [body(): lax.all_to_all(buf0, 'patch', split_axis=0, concat_axis=0, tiled=True)]
    ppermute x16 -> x12, waiting for transfers between devices: 18 us -> 28.8 us  [swap(): return lax.ppermute(x, axis, [(i, i ^ mask) for i in range(size)])]
    all_to_all x0 -> x1, starting transfers between devices: none -> 8.58 us  [body(): lax.all_to_all(extra, 'patch', split_axis=0, concat_axis=0, axis_index_gr...]
    unnamed x47 -> x10, local copies, waits for them, and re-layouts: 8.38 us -> 0.02 us
    select_n x4 -> x0, local copies, waits for them, and re-layouts: 6.82 us -> none  [toeplitz(): total = jnp.where(on, taps[:, None, :, :, r, None], total)]
    select_n x3 -> x1, other arithmetic: 4.09 us -> 0.01 us  [toeplitz(): row_in = jnp.where(tail, 8 + (column - combos * 8 & 3), column & 7)]
    all_to_all x1, starting transfers between devices: 10.6 us -> 7.49 us  [body(): lax.all_to_all(buf0, 'patch', split_axis=0, concat_axis=0, tiled=True)]
  transfers between devices with their start and end apart: 17 -> 14, of which waited for: 5 -> 7; matrix products, arithmetic and copies ran while one was open for 27% -> 5% of each run, Pallas kernels for 6% -> 7%
where the time goes in v6:
time: 110 us; the launch traced here: 109 us
  waiting for transfers between devices  42.8 us (39%)
  starting transfers between devices  31.9 us (29%)
  Pallas kernels  24.6 us (22%)
  other arithmetic  3.53 us (3%)
  local copies, waits for them, and re-layouts  2.77 us (3%)
  between operations  2.75 us (2%)
    ppermute x12, waiting for transfers between devices, swap(): return lax.ppermute(x, axis, [(i, i ^ mask) for i in range(size)])  28.8 us
    ppermute x12, starting transfers between devices, swap(): return lax.ppermute(x, axis, [(i, i ^ mask) for i in range(size)])  15.9 us
    all_to_all x1, waiting for transfers between devices, body(): lax.all_to_all(buf0, 'patch', split_axis=0, concat_axis=0, tiled=True)  11.1 us
    all_to_all x1, starting transfers between devices, body(): lax.all_to_all(extra, 'patch', split_axis=0, concat_axis=0, axis_index_gr...  8.58 us
    pallas_call x1, Pallas kernels, front(): pl.pallas_call(lambda *refs: front_kernel(per_step, *refs), name='front',...  7.59 us
    all_to_all x1, starting transfers between devices, body(): lax.all_to_all(buf0, 'patch', split_axis=0, concat_axis=0, tiled=True)  7.49 us
    pallas_call x1, Pallas kernels, detect(): pl.pallas_call(lambda *refs: detect_kernel(nband, *refs), name='detect',...  6.46 us
    pallas_call x1, Pallas kernels, place(): pl.pallas_call(lambda *refs: place_kernel(per_step, nband, gathered, *ref...  6.18 us
  transfers between devices with their start and end apart: 14, of which 7 were waited for; matrix products, arithmetic and copies ran while one was open for 5% of the time, Pallas kernels for 7%

profile of v6, /device:TPU:32, one launch (start us, length us, event | category | flops | bytes accessed | tf_op | source)
XLA Modules:
  0.0 109.3 jit_solution(6765868601727811832)
XLA Ops:
  0.6 0.0 copy-start
  0.7 0.7 convert_bitcast_fusion
  1.3 0.6 reshape.288.refs_4_
  1.9 4.3 %repeat.1 = bf16[8,128,128]{2,1,0:T(8,128)(2,1)} custom-call(s32[1]{0:T(128)} %bitcast.2.refs_0_, s32[1,2048]{1,0:T(1,128)} %bitcast.33, s32[2,2048]{1,0:T(2,128)} %bitcast.30, f32[1,2048]{1,0:T(1,128)} %refs_3_.3, f32[14,32]{1,0:T(8,128)} %reshape.288.refs_4_, bf16[32,1,128,128]{3,2,1,0:T(8,128)(2,1)} %refs_5_.3, bf16[32,1,128,128]{3,2,1,0:T(8,128)(2,1)} %refs_6_.3, ...), custom_call_target="tpu_custom_call" | custom-call | tf_op jit(solution)/shard_map/repeat/pallas_call | solution.py:89
  6.3 8.6 %all-to-all-start.1 = ((bf16[8,128,128]{2,1,0:T(8,128)(2,1)}), bf16[8,128,128]{2,1,0:T(8,128)(2,1)}, u32[]{:S(2)}, u32[]{:S(2)}) async-start(bf16[8,128,128]{2,1,0:T(8,128)(2,1)} %repeat.1), calls=%async_computation.1 | async-start | bytes 524288 | tf_op jit(solution)/shard_map/all_to_all | solution.py:389
  14.9 7.6 %front.1 = (bf16[64,128,128]{2,1,0:T(8,128)(2,1)}, bf16[64,128,128]{2,1,0:T(8,128)(2,1)}) custom-call(s32[1]{0:T(128)} %bitcast.2.refs_0_, s32[1,2048]{1,0:T(1,128)} %bitcast.34, s32[2,2048]{1,0:T(2,128)} %bitcast.31, f32[1,2048]{1,0:T(1,128)} %refs_3_.3, f32[14,32]{1,0:T(8,128)} %reshape.288.refs_4_, bf16[32,1,128,128]{3,2,1,0:T(8,128)(2,1)} %refs_5_.3, ...), custom_call_target="tpu_custom_call" | custom-call | bytes 25165824 | tf_op jit(solution)/shard_map/front/pallas_call | solution.py:153
  22.5 2.9 %all-to-all-done.1 = bf16[8,128,128]{2,1,0:T(8,128)(2,1)} async-done(((bf16[8,128,128]{2,1,0:T(8,128)(2,1)}), bf16[8,128,128]{2,1,0:T(8,128)(2,1)}, u32[]{:S(2)}, u32[]{:S(2)}) %all-to-all-start.1) | async-done | bytes 262176 | tf_op jit(solution)/shard_map/all_to_all | solution.py:389
  25.4 7.5 %all-to-all-start.2 = ((bf16[64,128,128]{2,1,0:T(8,128)(2,1)}), bf16[64,128,128]{2,1,0:T(8,128)(2,1)S(1)}, u32[]{:S(2)}, u32[]{:S(2)}) async-start(bf16[64,128,128]{2,1,0:T(8,128)(2,1)} %get-tuple-element.99), calls=%async_computation.2 | async-start | bytes 4194304 | tf_op jit(solution)/shard_map/all_to_all | solution.py:398
  32.9 0.1 pad_add_fusion
  33.0 0.1 broadcast_add_fusion.1
  33.1 0.2 collective-permute-start.3
  33.4 2.7 %collective-permute-start.2 = (bf16[8,128,128]{2,1,0:T(8,128)(2,1)}, bf16[8,128,128]{2,1,0:T(8,128)(2,1)}, u32[]{:S(2)}, u32[]{:S(2)}) collective-permute-start(bf16[8,128,128]{2,1,0:T(8,128)(2,1)} %all-to-all-done.1), channel_id=1, source_target_pairs={{0,24},{4,28},{8,16},{12,20},{16,8},{20,12},{24,0},{28,4},{32,56},... | collective-permute-start | bytes 786440 | tf_op jit(solution)/shard_map/ppermute | solution.py:187
  36.1 0.9 collective-permute-start.1
  36.9 0.6 collective-permute-start
  37.5 0.5 broadcast.350
  38.0 0.0 copy-done.2
  38.0 0.7 reduce.10
  38.7 0.1 reshape.287
  38.7 0.1 copy.19
  38.8 0.2 reduce_window_sum.11
  39.0 0.1 copy.16
  39.1 0.1 copy.15
  39.2 0.2 and_reduce_fusion
  39.5 0.6 reduce_max.9
  40.1 1.6 %collective-permute-start.7 = (f32[]{:T(128)}, f32[]{:T(128)}, u32[]{:S(2)}, u32[]{:S(2)}) collective-permute-start(f32[]{:T(128)} %reduce_max.9), channel_id=1, source_target_pairs={{0,1},{1,0},{2,3},{3,2},{4,5},{5,4},{6,7},{7,6},{8,9},{9,8},{10,11... | collective-permute-start | bytes 20 | tf_op jit(solution)/shard_map/ppermute | solution.py:187
  41.7 0.0 copy-done.1
  41.7 0.1 add.103
  41.8 0.1 copy.17
  41.9 0.2 fusion
  42.1 0.5 broadcast.351
  42.7 0.6 reduce.11
  43.2 0.1 broadcast_in_dim.156
  43.3 0.1 copy.18
  43.4 0.2 fusion.2.refs_4_
  43.6 19.6 %collective-permute-done.2 = bf16[8,128,128]{2,1,0:T(8,128)(2,1)} collective-permute-done((bf16[8,128,128]{2,1,0:T(8,128)(2,1)}, bf16[8,128,128]{2,1,0:T(8,128)(2,1)}, u32[]{:S(2)}, u32[]{:S(2)}) %collective-permute-start.2) | collective-permute-done | bytes 262176 | tf_op jit(solution)/shard_map/ppermute | solution.py:187
  63.2 0.0 collective-permute-start.6
  63.2 0.0 collective-permute-done.1
  63.2 0.5 collective-permute-start.5
  63.7 0.0 collective-permute-done
  63.7 0.1 collective-permute-start.4
  63.9 0.1 shift_right_arithmetic.36
  63.9 0.1 and.100
  64.0 0.1 broadcast_in_dim.159
  64.1 0.1 broadcast_in_dim.180
  64.2 0.1 broadcast_in_dim.181
  64.3 0.7 fusion.5
  65.0 0.0 collective-permute-done.7
  66.3 4.6 %collective-permute-start.8 = (f32[]{:T(128)}, f32[]{:T(128)}, u32[]{:S(2)}, u32[]{:S(2)}) collective-permute-start(f32[]{:T(128)} %max.22), channel_id=1, source_target_pairs={{0,2},{1,3},{2,0},{3,1},{4,6},{5,7},{6,4},{7,5},{8,10},{9,11},{10,... | collective-permute-start | bytes 20 | tf_op jit(solution)/shard_map/ppermute | solution.py:187
  70.9 0.7 collective-permute-done.8
  72.2 0.0 collective-permute-done.3
  72.2 0.0 collective-permute-done.6
  72.2 0.0 collective-permute-done.5
  72.2 0.0 collective-permute-done.4
  72.2 11.1 %all-to-all-done.2 = bf16[64,128,128]{2,1,0:T(8,128)(2,1)S(1)} async-done(((bf16[64,128,128]{2,1,0:T(8,128)(2,1)}), bf16[64,128,128]{2,1,0:T(8,128)(2,1)S(1)}, u32[]{:S(2)}, u32[]{:S(2)}) %all-to-all-start.2) | async-done | bytes 2097184 | tf_op jit(solution)/shard_map/all_to_all | solution.py:398
  83.3 6.2 %conditional.1 = (bf16[136,512]{1,0:T(8,128)(2,1)}, bf16[136,512]{1,0:T(8,128)(2,1)}, bf16[136,512]{1,0:T(8,128)(2,1)}, bf16[136,512]{1,0:T(8,128)(2,1)}, bf16[1,1,512,512]{3,2,1,0:T(8,128)(2,1)}) conditional(s32[]{:T(128)} %convert_element_type.35, (bf16[64,128,128]{2,1,0:T(8,128)(2,1)}, s32[2]{0:T(128)S(1)}, s32[2,64]{1,0:T(2,128)S(1)}, ...), branch_computations={%region_6.7_spmd, %region_7.8_spmd} | conditional | bytes 4194344 | solution.py:435
  83.3 6.2 %place.3 = (bf16[512,512]{1,0:T(8,128)(2,1)}, bf16[136,512]{1,0:T(8,128)(2,1)}, bf16[136,512]{1,0:T(8,128)(2,1)}, bf16[136,512]{1,0:T(8,128)(2,1)}, bf16[136,512]{1,0:T(8,128)(2,1)}) custom-call(s32[2]{0:T(128)S(1)} %get-tuple-element.56.refs_0_, s32[2,64]{1,0:T(2,128)S(1)} %get-tuple-element.57.refs_1_, ...), custom_call_target="tpu_custom_call" | custom-call | tf_op jit(solution)/shard_map/cond/branch_1_fun/place/pallas_call | solution.py:260
  89.5 1.7 %collective-permute-start.9 = (bf16[136,512]{1,0:T(8,128)(2,1)}, bf16[136,512]{1,0:T(8,128)(2,1)S(1)}, u32[]{:S(2)}, u32[]{:S(2)}) collective-permute-start(bf16[136,512]{1,0:T(8,128)(2,1)} %get-tuple-element.121), channel_id=1, source_target_pairs={{0,1},{1,0},{2,3},{3,2},{4,5},{5,4},{6,7},{7,6},{8,9},{9,8},{10,11... | collective-permute-start | bytes 417800 | tf_op jit(solution)/shard_map/ppermute | solution.py:187
  91.2 2.8 %collective-permute-start.10 = (bf16[136,512]{1,0:T(8,128)(2,1)}, bf16[136,512]{1,0:T(8,128)(2,1)S(1)}, u32[]{:S(2)}, u32[]{:S(2)}) collective-permute-start(bf16[136,512]{1,0:T(8,128)(2,1)} %get-tuple-element.122), channel_id=1, source_target_pairs={{0,2},{1,3},{2,0},{3,1},{4,6},{5,7},{6,4},{7,5},{8,10},{9,11},{10,... | collective-permute-start | bytes 417800 | tf_op jit(solution)/shard_map/ppermute | solution.py:187
  94.0 0.2 collective-permute-start.11
  94.3 0.1 copy.21.refs_5_
  94.4 1.4 %collective-permute-done.9.refs_1_ = bf16[136,512]{1,0:T(8,128)(2,1)S(1)} collective-permute-done((bf16[136,512]{1,0:T(8,128)(2,1)}, bf16[136,512]{1,0:T(8,128)(2,1)S(1)}, u32[]{:S(2)}, u32[]{:S(2)}) %collective-permute-start.9) | collective-permute-done | bytes 139296 | tf_op jit(solution)/shard_map/ppermute | solution.py:187
  95.8 4.9 %collective-permute-done.10.refs_2_ = bf16[136,512]{1,0:T(8,128)(2,1)S(1)} collective-permute-done((bf16[136,512]{1,0:T(8,128)(2,1)}, bf16[136,512]{1,0:T(8,128)(2,1)S(1)}, u32[]{:S(2)}, u32[]{:S(2)}) %collective-permute-start.10) | collective-permute-done | bytes 139296 | tf_op jit(solution)/shard_map/ppermute | solution.py:187
  100.7 2.1 %collective-permute-done.11.refs_3_ = bf16[136,512]{1,0:T(8,128)(2,1)S(1)} collective-permute-done((bf16[136,512]{1,0:T(8,128)(2,1)}, bf16[136,512]{1,0:T(8,128)(2,1)S(1)}, u32[]{:S(2)}, u32[]{:S(2)}) %collective-permute-start.11) | collective-permute-done | bytes 139296 | tf_op jit(solution)/shard_map/ppermute | solution.py:187
  102.9 6.5 %detect.1 = bf16[64,128,512]{2,1,0:T(8,128)(2,1)} custom-call(bf16[136,512]{1,0:T(8,128)(2,1)} %get-tuple-element.120.refs_0_, bf16[136,512]{1,0:T(8,128)(2,1)S(1)} %collective-permute-done.9.refs_1_, bf16[136,512]{1,0:T(8,128)(2,1)S(1)} %collective-permute-done.10.refs_2_, bf16[136,512]{1,0:T(8,128)(2,1)S(1)} %collective-permute-done.11.refs_3_, ...), custom_call_target="tpu_custom_call" | custom-call | tf_op jit(solution)/shard_map/detect/pallas_call | solution.py:326
  (21 shorter events, 0.2 us)
Async XLA Ops:
  0.6 41.2 %copy-start = (bf16[64,100]{1,0:T(8,128)(2,1)S(1)}, bf16[64,100]{1,0:T(8,128)(2,1)}, u32[]{:S(2)}) copy-start(bf16[64,100]{1,0:T(8,128)(2,1)} %param.18) | copy-start | bytes 38404
  6.3 19.1 %all-to-all-start.1 = ((bf16[8,128,128]{2,1,0:T(8,128)(2,1)}), bf16[8,128,128]{2,1,0:T(8,128)(2,1)}, u32[]{:S(2)}, u32[]{:S(2)}) async-start(bf16[8,128,128]{2,1,0:T(8,128)(2,1)} %repeat.1), calls=%async_computation.1 | async-start | bytes 524288 | tf_op jit(solution)/shard_map/all_to_all | solution.py:389
  25.4 12.6 %copy-start.2 = (s32[1,2048,1]{1,2,0:T(1,128)S(1)}, s32[1,2048,1]{1,2,0:T(1,128)}, u32[]{:S(2)}) copy-start(s32[1,2048,1]{1,2,0:T(1,128)} %param.15) | copy-start | bytes 24580
  25.4 16.3 %copy-start.1 = (s32[1,2048,2]{1,2,0:T(2,128)S(1)}, s32[1,2048,2]{1,2,0:T(2,128)}, u32[]{:S(2)}) copy-start(s32[1,2048,2]{1,2,0:T(2,128)} %param.16) | copy-start | bytes 49156
  25.4 17.3 %copy-start.3 = (f32[1,2048]{1,0:T(1,128)S(1)}, f32[1,2048]{1,0:T(1,128)}, u32[]{:S(2)}) copy-start(f32[1,2048]{1,0:T(1,128)} %refs_3_.3) | copy-start | bytes 24580
  25.4 38.7 %copy-start.4 = (f32[64]{0:T(128)S(1)}, f32[64]{0:T(128)}, u32[]{:S(2)}) copy-start(f32[64]{0:T(128)} %param.19) | copy-start | bytes 772
  25.4 57.9 %all-to-all-start.2 = ((bf16[64,128,128]{2,1,0:T(8,128)(2,1)}), bf16[64,128,128]{2,1,0:T(8,128)(2,1)S(1)}, u32[]{:S(2)}, u32[]{:S(2)}) async-start(bf16[64,128,128]{2,1,0:T(8,128)(2,1)} %get-tuple-element.99), calls=%async_computation.2 | async-start | bytes 4194304 | tf_op jit(solution)/shard_map/all_to_all | solution.py:398
  33.1 39.1 %collective-permute-start.3 = (bf16[8,128,128]{2,1,0:T(8,128)(2,1)}, bf16[8,128,128]{2,1,0:T(8,128)(2,1)}, u32[]{:S(2)}, u32[]{:S(2)}) collective-permute-start(bf16[8,128,128]{2,1,0:T(8,128)(2,1)} %all-to-all-done.1), channel_id=1, source_target_pairs={{0,4},{4,0},{8,12},{12,8},{16,20},{20,16},{24,28},{28,24},{32,36},... | collective-permute-start | bytes 786440 | tf_op jit(solution)/shard_map/ppermute | solution.py:187
  33.4 29.9 %collective-permute-start.2 = (bf16[8,128,128]{2,1,0:T(8,128)(2,1)}, bf16[8,128,128]{2,1,0:T(8,128)(2,1)}, u32[]{:S(2)}, u32[]{:S(2)}) collective-permute-start(bf16[8,128,128]{2,1,0:T(8,128)(2,1)} %all-to-all-done.1), channel_id=1, source_target_pairs={{0,24},{4,28},{8,16},{12,20},{16,8},{20,12},{24,0},{28,4},{32,56},... | collective-permute-start | bytes 786440 | tf_op jit(solution)/shard_map/ppermute | solution.py:187
  36.1 27.2 %collective-permute-start.1 = (bf16[8,128,128]{2,1,0:T(8,128)(2,1)}, bf16[8,128,128]{2,1,0:T(8,128)(2,1)}, u32[]{:S(2)}, u32[]{:S(2)}) collective-permute-start(bf16[8,128,128]{2,1,0:T(8,128)(2,1)} %all-to-all-done.1), channel_id=1, source_target_pairs={{0,16},{4,20},{8,24},{12,28},{16,0},{20,4},{24,8},{28,12},{32,48},... | collective-permute-start | bytes 786440 | tf_op jit(solution)/shard_map/ppermute | solution.py:187
  36.9 26.8 %collective-permute-start = (bf16[8,128,128]{2,1,0:T(8,128)(2,1)}, bf16[8,128,128]{2,1,0:T(8,128)(2,1)}, u32[]{:S(2)}, u32[]{:S(2)}) collective-permute-start(bf16[8,128,128]{2,1,0:T(8,128)(2,1)} %all-to-all-done.1), channel_id=1, source_target_pairs={{0,8},{4,12},{8,0},{12,4},{16,24},{20,28},{24,16},{28,20},{32,40},... | collective-permute-start | bytes 786440 | tf_op jit(solution)/shard_map/ppermute | solution.py:187
  40.1 25.0 %collective-permute-start.7 = (f32[]{:T(128)}, f32[]{:T(128)}, u32[]{:S(2)}, u32[]{:S(2)}) collective-permute-start(f32[]{:T(128)} %reduce_max.9), channel_id=1, source_target_pairs={{0,1},{1,0},{2,3},{3,2},{4,5},{5,4},{6,7},{7,6},{8,9},{9,8},{10,11... | collective-permute-start | bytes 20 | tf_op jit(solution)/shard_map/ppermute | solution.py:187
  63.2 9.0 %collective-permute-start.6 = (bf16[8,128,128]{2,1,0:T(8,128)(2,1)}, bf16[8,128,128]{2,1,0:T(8,128)(2,1)}, u32[]{:S(2)}, u32[]{:S(2)}) collective-permute-start(bf16[8,128,128]{2,1,0:T(8,128)(2,1)} %collective-permute-done.2), channel_id=1, source_target_pairs={{0,4},{4,0},{8,12},{12,8},{16,20},{20,16},{24,28},{28,24},{32,36},... | collective-permute-start | bytes 786440 | tf_op jit(solution)/shard_map/ppermute | solution.py:187
  63.2 9.0 %collective-permute-start.5 = (bf16[8,128,128]{2,1,0:T(8,128)(2,1)}, bf16[8,128,128]{2,1,0:T(8,128)(2,1)}, u32[]{:S(2)}, u32[]{:S(2)}) collective-permute-start(bf16[8,128,128]{2,1,0:T(8,128)(2,1)} %collective-permute-done.1), channel_id=1, source_target_pairs={{0,4},{4,0},{8,12},{12,8},{16,20},{20,16},{24,28},{28,24},{32,36},... | collective-permute-start | bytes 786440 | tf_op jit(solution)/shard_map/ppermute | solution.py:187
  63.7 8.5 %collective-permute-start.4 = (bf16[8,128,128]{2,1,0:T(8,128)(2,1)}, bf16[8,128,128]{2,1,0:T(8,128)(2,1)}, u32[]{:S(2)}, u32[]{:S(2)}) collective-permute-start(bf16[8,128,128]{2,1,0:T(8,128)(2,1)} %collective-permute-done), channel_id=1, source_target_pairs={{0,4},{4,0},{8,12},{12,8},{16,20},{20,16},{24,28},{28,24},{32,36},... | collective-permute-start | bytes 786440 | tf_op jit(solution)/shard_map/ppermute | solution.py:187
  66.3 5.2 %collective-permute-start.8 = (f32[]{:T(128)}, f32[]{:T(128)}, u32[]{:S(2)}, u32[]{:S(2)}) collective-permute-start(f32[]{:T(128)} %max.22), channel_id=1, source_target_pairs={{0,2},{1,3},{2,0},{3,1},{4,6},{5,7},{6,4},{7,5},{8,10},{9,11},{10,... | collective-permute-start | bytes 20 | tf_op jit(solution)/shard_map/ppermute | solution.py:187
  89.5 6.3 %collective-permute-start.9 = (bf16[136,512]{1,0:T(8,128)(2,1)}, bf16[136,512]{1,0:T(8,128)(2,1)S(1)}, u32[]{:S(2)}, u32[]{:S(2)}) collective-permute-start(bf16[136,512]{1,0:T(8,128)(2,1)} %get-tuple-element.121), channel_id=1, source_target_pairs={{0,1},{1,0},{2,3},{3,2},{4,5},{5,4},{6,7},{7,6},{8,9},{9,8},{10,11... | collective-permute-start | bytes 417800 | tf_op jit(solution)/shard_map/ppermute | solution.py:187
  91.2 9.5 %collective-permute-start.10 = (bf16[136,512]{1,0:T(8,128)(2,1)}, bf16[136,512]{1,0:T(8,128)(2,1)S(1)}, u32[]{:S(2)}, u32[]{:S(2)}) collective-permute-start(bf16[136,512]{1,0:T(8,128)(2,1)} %get-tuple-element.122), channel_id=1, source_target_pairs={{0,2},{1,3},{2,0},{3,1},{4,6},{5,7},{6,4},{7,5},{8,10},{9,11},{10,... | collective-permute-start | bytes 417800 | tf_op jit(solution)/shard_map/ppermute | solution.py:187
  94.0 8.8 %collective-permute-start.11 = (bf16[136,512]{1,0:T(8,128)(2,1)}, bf16[136,512]{1,0:T(8,128)(2,1)S(1)}, u32[]{:S(2)}, u32[]{:S(2)}) collective-permute-start(bf16[136,512]{1,0:T(8,128)(2,1)} %get-tuple-element.123), channel_id=1, source_target_pairs={{0,3},{1,2},{2,1},{3,0},{4,7},{5,6},{6,5},{7,4},{8,11},{9,10},{10,... | collective-permute-start | bytes 417800 | tf_op jit(solution)/shard_map/ppermute | solution.py:187

commit v7 on v6

v7 whole, which is shorter than its diff:
```python
import jax
import jax.numpy as jnp
from jax import lax
from jax.experimental import pallas as pl
from jax.experimental.pallas import tpu as pltpu
from jax.sharding import PartitionSpec as P

PS = 512
S = 128
TAPS = 7
PLANE = 8
HALF = TAPS // 2
KS = 5
PAD = KS // 2
LANES = 128
F32 = jnp.float32
BF16 = jnp.bfloat16


def dot_nt(a, b):
    return lax.dot_general(a, b, (((1,), (1,)), ((), ())), preferred_element_type=F32)


def dot_nn(a, b):
    return lax.dot_general(a, b, (((1,), (0,)), ((), ())), preferred_element_type=F32)


def warp_tiles(here, base, offs_ref, wts_ref, taps_ref, tiles, rows, cols):
    diag = lax.broadcasted_iota(jnp.int32, (S, S), 1) - lax.broadcasted_iota(jnp.int32, (S, S), 0)

    def band(axis, tile):
        matrix = jnp.zeros((S, S), F32)
        for tap in range(TAPS):
            matrix = jnp.where(diag == tap - HALF, taps_ref[tap, axis, tile], matrix)
        return matrix.astype(BF16)

    each = range(len(here))
    psf_rows = [band(0, t) for t in here]
    psf_cols = [band(1, t) for t in here]
    half_done = [dot_nt(tiles[k], psf_cols[k]).astype(BF16) for k in each]
    matched = [dot_nn(psf_rows[k], half_done[k]).astype(BF16) for k in each]
    across = [dot_nt(matched[k], cols[k]).astype(BF16) for k in each]
    product = [dot_nn(rows[k], across[k]) for k in each]
    out = []
    for k in each:
        place = base + here[k]
        warped = wts_ref[0, place] * product[k]
        warped = pltpu.roll(warped, offs_ref[1, place] & (LANES - 1), 1)
        warped = pltpu.roll(warped, offs_ref[0, place] & 7, 0)
        out.append(warped.astype(BF16))
    return out


def repeat_kernel(
    tiles, owner_ref, routes_ref, offs_ref, wts_ref, taps_ref,
    exp_ref, rows_ref, cols_ref, out_ref, held, count, found, sems,
):
    base = owner_ref[0] * tiles
    found[0] = 0

    @pl.loop(0, count.shape[0], unroll=8)
    def _(i):
        count[i] = 0

    @pl.loop(0, tiles, unroll=4)
    def _(i):
        dest = routes_ref[0, base + i]
        rank = count[dest]
        count[dest] = rank + 1
        found[0] = jnp.where(rank > 0, i, found[0])

    tile = found[0]
    copies = [
        pltpu.make_async_copy(src.at[tile, 0], held.at[i], sems.at[i])
        for i, src in enumerate((exp_ref, rows_ref, cols_ref))
    ]
    for copy in copies:
        copy.start()
    for copy in copies:
        copy.wait()
    warped = warp_tiles(
        [tile], base, offs_ref, wts_ref, taps_ref, [held[0]], [held[1]], [held[2]]
    )
    out_ref[...] = jnp.broadcast_to(warped[0][None], out_ref.shape)


def repeat(owner, routes, offs, wts, taps, exposures, warp_rows, warp_cols, npatch, copies):
    anywhere = pl.BlockSpec(memory_space=pl.ANY)
    return pl.pallas_call(
        lambda *refs: repeat_kernel(exposures.shape[0], *refs),
        name="repeat",
        out_shape=jax.ShapeDtypeStruct((copies, S, S), BF16),
        grid_spec=pltpu.PrefetchScalarGridSpec(
            num_scalar_prefetch=5,
            grid=(1,),
            in_specs=[anywhere] * 3,
            out_specs=pl.BlockSpec((copies, S, S), lambda i, *_: (0, 0, 0)),
            scratch_shapes=[
                pltpu.VMEM((3, S, S), BF16),
                pltpu.SMEM((npatch,), jnp.int32),
                pltpu.SMEM((1,), jnp.int32),
                pltpu.SemaphoreType.DMA((3,)),
            ],
        ),
    )(owner, routes, offs, wts, taps, exposures, warp_rows, warp_cols)


def front_kernel(
    chunk, owner_ref, routes_ref, offs_ref, wts_ref, taps_ref,
    exp_ref, rows_ref, cols_ref, buf0_ref, buf1_ref, held, stage, count, load_sems, sems,
):
    tiles = stage.shape[0]
    base = owner_ref[0] * tiles
    loads = [
        [
            pltpu.make_async_copy(
                src.at[pl.ds(start, chunk), 0], held.at[i, pl.ds(start, chunk)], load_sems.at[i, n]
            )
            for i, src in enumerate((exp_ref, rows_ref, cols_ref))
        ]
        for n, start in enumerate(range(0, tiles, chunk))
    ]
    for copies in loads:
        for copy in copies:
            copy.start()

    @pl.loop(0, count.shape[0], unroll=8)
    def _(i):
        count[i] = 0

    for n, copies in enumerate(loads):
        for copy in copies:
            copy.wait()
        here = [n * chunk + k for k in range(chunk)]
        inputs = [[held[i, tile] for tile in here] for i in range(3)]
        warped = warp_tiles(here, base, offs_ref, wts_ref, taps_ref, *inputs)
        for tile, value in zip(here, warped):
            stage[tile] = value
        for tile in here:
            dest = routes_ref[0, base + tile]
            rank = count[dest]
            count[dest] = rank + 1

            @pl.when(rank == 0)
            def _():
                pltpu.make_async_copy(stage.at[tile], buf0_ref.at[dest], sems.at[tile]).start()

            @pl.when(rank > 0)
            def _():
                pltpu.make_async_copy(stage.at[tile], buf1_ref.at[dest], sems.at[tile]).start()

    @pl.loop(0, tiles, unroll=8)
    def _(i):
        pltpu.make_async_copy(stage.at[i], buf0_ref.at[0], sems.at[i]).wait()


def front(owner, routes, offs, wts, taps, exposures, warp_rows, warp_cols, npatch):
    tiles = exposures.shape[0]
    chunk = 16
    anywhere = pl.BlockSpec(memory_space=pl.ANY)
    scalars = pl.BlockSpec(memory_space=pltpu.SMEM)
    return pl.pallas_call(
        lambda *refs: front_kernel(chunk, *refs),
        name="front",
        out_shape=(
            jax.ShapeDtypeStruct((npatch, S, S), BF16),
            jax.ShapeDtypeStruct((npatch, S, S), BF16),
        ),
        cost_estimate=pl.CostEstimate(flops=0, bytes_accessed=24 << 20, transcendentals=0),
        in_specs=[scalars] * 5 + [anywhere] * 3,
        out_specs=(anywhere, anywhere),
        scratch_shapes=[
            pltpu.VMEM((3, tiles, S, S), BF16),
            pltpu.VMEM((tiles, S, S), BF16),
            pltpu.SMEM((npatch,), jnp.int32),
            pltpu.SemaphoreType.DMA((3, tiles // chunk)),
            pltpu.SemaphoreType.DMA((tiles,)),
        ],
    )(owner, routes, offs, wts, taps, exposures, warp_rows, warp_cols)


def gathered_source(index, owner, rows):
    step = index // rows
    return (index % rows) * PLANE + (
        (owner % PLANE) ^ (((step & 1) << 1) | ((step & 2) << 1) | ((step & 4) >> 2))
    )


def swap(x, axis, mask):
    size = lax.axis_size(axis)
    return lax.ppermute(x, axis, [(i, i ^ mask) for i in range(size)])


def place_kernel(nband, gathered, owner_ref, table_ref, first_ref, *refs):
    second_refs, (cover_ref, coadd_ref, *strip_refs), (held, acc, full, sems) = (
        refs[: -nband - 6], refs[-nband - 6 : -4], refs[-4:]
    )
    slots = first_ref.shape[0]
    strip_rows = PS // nband
    chunk = slots // 4
    pieces = [(first_ref.at[pl.ds(i, chunk)], i, chunk) for i in range(0, slots, chunk)]
    at = slots
    for ref in second_refs:
        pieces.append((ref, at, ref.shape[0]))
        at += ref.shape[0]
    copies = [
        pltpu.make_async_copy(src, held.at[pl.ds(start, size)], sems.at[i])
        for i, (src, start, size) in enumerate(pieces)
    ]
    for copy in copies:
        copy.start()
    acc[...] = jnp.zeros_like(acc)
    lane = lax.broadcasted_iota(jnp.int32, (8, LANES), 1)
    sub = lax.broadcasted_iota(jnp.int32, (8, LANES), 0)

    def add_tile(index, slot, source):
        code = table_ref[slot, source]

        @pl.when(code > 0)
        def _():
            corner = code - 1
            top = corner // PS
            left = corner & (PS - 1)
            base = pl.multiple_of((top // 8) * 8, 8)
            shift = top & 7
            part = left // LANES
            on = lane >= (left & (LANES - 1))
            tile = held[index].astype(F32)
            for g in range(S // 8):
                rows = tile[8 * g : 8 * g + 8]
                if g == 0:
                    low = jnp.where(sub < shift, rows, 0.0)
                    rows = rows - low
                    at = pl.ds(base + S, 8)
                    acc[part, at, :] += jnp.where(on, low, 0.0)
                    acc[part + 1, at, :] += jnp.where(on, 0.0, low)
                at = pl.ds(base + 8 * g, 8)
                acc[part, at, :] += jnp.where(on, rows, 0.0)
                acc[part + 1, at, :] += jnp.where(on, 0.0, rows)

    for copy, (_, start, size) in zip(copies, pieces):
        copy.wait()

        @pl.loop(0, size, unroll=min(size, 8))
        def _(i):
            if start < slots:
                add_tile(start + i, 0, start + i)
            else:
                source = start - slots + i
                if gathered:
                    source = gathered_source(source, owner_ref[0], slots // PLANE)
                add_tile(start + i, 1, source)

    edge = full.shape[0] - PS
    full[0 : edge // 2, :] = jnp.zeros((edge // 2, PS), F32)
    full[PS + edge // 2 :, :] = jnp.zeros((edge // 2, PS), F32)
    for part in range(PS // LANES):
        at = slice(part * LANES, part * LANES + LANES)
        value = (acc[part, 0:PS, :] * cover_ref[:, at]).astype(BF16)
        coadd_ref[:, at] = value
        full[edge // 2 : edge // 2 + PS, at] = value.astype(F32)
    height = strip_refs[0].shape[0]
    for i, ref in enumerate(strip_refs):
        start = pl.multiple_of((owner_ref[1] ^ i) * strip_rows, 8)
        rows = full[pl.ds(start, height + 8), :]
        ref[...] = rows[edge // 2 - PAD : edge // 2 - PAD + height].astype(BF16)


def place(owner, table, first, seconds, cover, nband, gathered):
    strip = PS // nband + 8
    anywhere = pl.BlockSpec(memory_space=pl.ANY)
    whole = pl.BlockSpec(memory_space=pltpu.VMEM)
    scalars = pl.BlockSpec(memory_space=pltpu.SMEM)
    tiles = first.shape[0] + sum(x.shape[0] for x in seconds)
    return pl.pallas_call(
        lambda *refs: place_kernel(nband, gathered, *refs),
        name="place",
        out_shape=(
            jax.ShapeDtypeStruct((PS, PS), BF16),
            *[jax.ShapeDtypeStruct((strip, PS), BF16)] * nband,
        ),
        in_specs=[scalars, scalars, anywhere, *[anywhere] * len(seconds), whole],
        out_specs=(whole,) * (nband + 1),
        scratch_shapes=[
            pltpu.VMEM((tiles, S, S), BF16),
            pltpu.VMEM((PS // LANES + 1, PS + 8, LANES), F32),
            pltpu.VMEM((PS + 16, PS), F32),
            pltpu.SemaphoreType.DMA((4 + len(seconds),)),
        ],
        compiler_params=pltpu.CompilerParams(vmem_limit_bytes=24 << 20),
    )(owner, table, first, *seconds, cover)


def detect_kernel(nband, *refs):
    strip_refs, (weight_ref, bias_ref, out_ref, main, edge, stage, sems) = (
        refs[:nband], refs[nband:]
    )
    groups = main.shape[0]
    slots, channels, rows, _ = stage.shape
    column = lax.broadcasted_iota(jnp.int32, (8, PS), 1)

    def prepare(g):
        pieces = []
        for s in range(KS):
            for b in range(nband):
                x = strip_refs[b][8 * g : 8 * g + 8, :].astype(F32)
                d = s - PAD
                if d:
                    x = pltpu.roll(x, (-d) % PS, 1)
                    x = jnp.where((column + d >= 0) & (column + d < PS), x, 0.0)
                pieces.append(x)
        if g < groups - 1:
            main[g] = jnp.concatenate(pieces, axis=0).astype(BF16)
        if g:
            edge[g] = jnp.concatenate([x[0:4] for x in pieces], axis=0).astype(BF16)

    def copy(chunk):
        slot = chunk % slots
        return pltpu.make_async_copy(
            stage.at[slot], out_ref.at[:, pl.ds(chunk * rows, rows), :], sems.at[slot]
        )

    prepare(0)
    per_chunk = rows // 8
    chunks = (groups - 1) // per_chunk
    for chunk in range(chunks):
        for i in range(per_chunk):
            prepare(chunk * per_chunk + i + 1)
        if chunk >= slots:
            copy(chunk - slots).wait()
        for i in range(per_chunk):
            g = chunk * per_chunk + i
            rhs = jnp.concatenate([main[g], edge[g + 1]], axis=0)
            res = dot_nn(weight_ref[...], rhs) + bias_ref[...]
            stage[chunk % slots, :, 8 * i : 8 * i + 8, :] = res.reshape(channels, 8, PS).astype(BF16)
        copy(chunk).start()
    for chunk in range(max(0, chunks - slots), chunks):
        copy(chunk).wait()


def detect(strips, weight, bias, channels, strip_rows):
    nband = len(strips)
    groups = strips[0].shape[0] // 8
    depth = nband * KS
    rows, slots = 16, 8
    whole = pl.BlockSpec(memory_space=pltpu.VMEM)
    return pl.pallas_call(
        lambda *refs: detect_kernel(nband, *refs),
        name="detect",
        out_shape=jax.ShapeDtypeStruct((channels, strip_rows, PS), BF16),
        in_specs=[whole] * (nband + 2),
        out_specs=pl.BlockSpec(memory_space=pl.ANY),
        scratch_shapes=[
            pltpu.VMEM((groups, depth * 8, PS), BF16),
            pltpu.VMEM((groups, depth * 4, PS), BF16),
            pltpu.VMEM((slots, channels, rows, PS), BF16),
            pltpu.SemaphoreType.DMA((slots,)),
        ],
        compiler_params=pltpu.CompilerParams(vmem_limit_bytes=24 << 20),
    )(*strips, weight, bias)


def toeplitz(det_weight, nband, band):
    channels, inputs = det_weight.shape
    combos = KS * nband
    column = jnp.arange(combos * 12, dtype=jnp.int32)
    tail = column >= combos * 8
    combo = jnp.where(tail, (column - combos * 8) >> 2, column >> 3)
    row_in = jnp.where(tail, 8 + ((column - combos * 8) & 3), column & 7)
    shift, slot = combo // nband, combo % nband
    source = (slot ^ band) * (KS * KS) + shift
    rows = jnp.arange(KS, dtype=jnp.int32)[:, None] * KS + source[None, :]
    pick = (jnp.arange(inputs, dtype=jnp.int32)[:, None, None] == rows[None]).astype(BF16)
    taps = lax.dot_general(
        det_weight, pick, (((1,), (0,)), ((), ())), preferred_element_type=F32
    )
    offset = row_in[None, :] - jnp.arange(8, dtype=jnp.int32)[:, None]
    total = jnp.zeros((channels, 8, combos * 12), F32)
    for r in range(KS):
        total = jnp.where((offset == r)[None], taps[:, None, r], total)
    return total.astype(BF16).reshape(channels * 8, combos * 12)


def slot_select(targets, capacity):
    counts = jnp.cumsum(targets.astype(jnp.int32), axis=1) - 1
    slot_ids = jnp.arange(capacity, dtype=jnp.int32)
    return targets[None] & (counts[None] == slot_ids[:, None, None])


def body(exposures, psf_taps, warp_rows, warp_cols, routes, offsets, weights, det_weight, det_bias):
    npatch = lax.axis_size("patch")
    nband = lax.axis_size("band")
    tiles = exposures.shape[0]
    capacity = 2
    owner = lax.axis_index("patch").astype(jnp.int32)
    routes_row = routes.transpose(0, 2, 1).reshape(1, -1)
    offs_rows = offsets.transpose(0, 2, 1).reshape(2, -1)
    taps = psf_taps[:, 0].transpose(2, 1, 0).astype(F32)
    inputs = (owner[None], routes_row, offs_rows, weights, taps, exposures, warp_rows, warp_cols)
    extra = repeat(*inputs, npatch, npatch // PLANE)
    lines = [list(range(i, npatch, PLANE)) for i in range(PLANE)]
    near = lax.all_to_all(
        extra, "patch", split_axis=0, concat_axis=0, axis_index_groups=lines, tiled=True
    )
    buf0, buf1 = front(*inputs, npatch)
    buf0, near, routes_row, offs_rows, weights, det_weight, det_bias = lax.optimization_barrier(
        (buf0, near, routes_row, offs_rows, weights, det_weight, det_bias)
    )
    near = [near] + [swap(near, "patch", m) for m in (2, 4, 6)]
    far = [swap(x, "patch", 1) for x in near]
    first = lax.all_to_all(buf0, "patch", split_axis=0, concat_axis=0, tiled=True)
    dest_all = routes_row.reshape(npatch, tiles)
    same = (dest_all[:, :, None] == dest_all[:, None, :]) & (
        jnp.arange(tiles)[None, :, None] > jnp.arange(tiles)[None, None, :]
    )
    repeats = jnp.max(jnp.sum(jnp.any(same, axis=2).astype(F32), axis=1))
    for bit in range(nband.bit_length() - 1):
        repeats = jnp.maximum(repeats, swap(repeats, "band", 1 << bit))
    landed = slot_select(dest_all == owner, capacity)
    corner = (offs_rows[0] * PS + offs_rows[1] + 1).reshape(npatch, tiles)
    table = jnp.sum(jnp.where(landed, corner[None], 0), axis=-1)
    slot_weights = jnp.sum(
        jnp.where(landed, weights.reshape(npatch, tiles)[None], 0.0), axis=-1
    ).reshape(-1)
    slot_corner = jnp.maximum(table.reshape(-1) - 1, 0)
    pixels = jnp.arange(PS, dtype=jnp.int32)
    down = pixels[None, :] - (slot_corner >> (PS.bit_length() - 1))[:, None]
    right = pixels[None, :] - (slot_corner & (PS - 1))[:, None]
    row_cover = jnp.where((down >= 0) & (down < S), slot_weights[:, None], 0.0)
    col_cover = ((right >= 0) & (right < S)).astype(F32)
    cover = jnp.einsum("ky,kx->yx", row_cover, col_cover, precision=lax.Precision.HIGHEST)
    cover = 1.0 / jnp.maximum(cover, 1.0)
    channels = det_weight.shape[0]
    strip_rows = PS // nband
    bias = jnp.broadcast_to(det_bias[:, None, None], (channels, 8, 1)).reshape(channels * 8, 1)
    band = lax.axis_index("band").astype(jnp.int32)
    first, near, far, table, cover, kernel, bias, repeats = lax.optimization_barrier(
        (first, near, far, table, cover, toeplitz(det_weight, nband, band), bias, repeats)
    )
    where = jnp.stack([owner, band])

    def one_repeat():
        return place(where, table, first, (*near, *far), cover, nband, True)

    def any_repeats():
        rest = lax.all_to_all(buf1, "patch", split_axis=0, concat_axis=0, tiled=True)
        return place(where, table, first, (rest,), cover, nband, False)

    coadd, *strips = lax.cond(repeats <= 1.0, one_repeat, any_repeats)
    strips = strips[:1] + [swap(x, "band", i) for i, x in enumerate(strips) if i]
    detection = detect(strips, kernel, bias, channels, strip_rows)
    return (coadd[None, None], detection[None])


def solution(mesh):
    placed = (
        P("patch", "band", None, None),
        P("patch", "band", None, None),
        P("patch", "band", None, None),
        P("patch", "band", None, None),
        P("band", None, None),
        P("band", None, None),
        P("band", None),
        P(),
        P(),
    )
    return jax.shard_map(
        body,
        mesh=mesh,
        in_specs=placed,
        out_specs=(P("patch", "band", None, None), P("patch", None, "band", None)),
        check_vma=False,
    )
```

time: 110 us -> 108 us (0.982); the launches traced: 109 us -> 106 us
  Pallas kernels: 24.6 us -> 20.6 us
    pallas_call x2, Pallas kernels: 13.8 us -> 12 us  [the longest x1 7.53 us: front(): pl.pallas_call(lambda *refs: front_kernel(chunk, *refs), name='front', ou...]
    pallas_call x1, Pallas kernels: 6.46 us -> 4.9 us  [detect(): pl.pallas_call(lambda *refs: detect_kernel(nband, *refs), name='detect',...]
  transfers between devices with their start and end apart: 14 -> 14, of which waited for: 7 -> 7; matrix products, arithmetic and copies ran while one was open for 5% -> 6% of each run, Pallas kernels for 7% -> 7%
where the time goes in v7:
time: 108 us; the launch traced here: 106 us
  waiting for transfers between devices  42.9 us (40%)
  starting transfers between devices  31.9 us (30%)
  Pallas kernels  20.6 us (19%)
  other arithmetic  4.25 us (4%)
  between operations  3.05 us (3%)
  local copies, waits for them, and re-layouts  2.26 us (2%)
    ppermute x12, waiting for transfers between devices, swap(): return lax.ppermute(x, axis, [(i, i ^ mask) for i in range(size)])  28.8 us
    ppermute x12, starting transfers between devices, swap(): return lax.ppermute(x, axis, [(i, i ^ mask) for i in range(size)])  15.9 us
    all_to_all x1, waiting for transfers between devices, body(): lax.all_to_all(buf0, 'patch', split_axis=0, concat_axis=0, tiled=True)  11.1 us
    all_to_all x1, starting transfers between devices, body(): lax.all_to_all(extra, 'patch', split_axis=0, concat_axis=0, axis_index_gr...  8.58 us
    pallas_call x1, Pallas kernels, front(): pl.pallas_call(lambda *refs: front_kernel(chunk, *refs), name='front', ou...  7.53 us
    all_to_all x1, starting transfers between devices, body(): lax.all_to_all(buf0, 'patch', split_axis=0, concat_axis=0, tiled=True)  7.43 us
    pallas_call x1, Pallas kernels, detect(): pl.pallas_call(lambda *refs: detect_kernel(nband, *refs), name='detect',...  4.9 us
    pallas_call x1, Pallas kernels, place(): pl.pallas_call(lambda *refs: place_kernel(nband, gathered, *refs), name='...  4.48 us
  transfers between devices with their start and end apart: 14, of which 7 were waited for; matrix products, arithmetic and copies ran while one was open for 6% of the time, Pallas kernels for 7%

profile of v7, /device:TPU:32, one launch (start us, length us, event | category | flops | bytes accessed | tf_op | source)
XLA Modules:
  0.0 106.0 jit_solution(3293351145287994188)
XLA Ops:
  0.6 0.0 copy-start
  0.7 1.3 %convert_bitcast_fusion.refs_4_ = f32[7,2,32]{2,1,0:T(2,128)} fusion(bf16[32,1,2,7]{0,2,3,1:T(2,128)(2,1)} %param.12), kind=kLoop, calls=%fused_computation.44 | loop fusion | flops 448 | bytes 2688 | tf_op jit(solution)/shard_map/convert_element_type | solution.py:398
  1.9 3.7 %repeat.1 = bf16[8,128,128]{2,1,0:T(8,128)(2,1)} custom-call(s32[1]{0:T(128)} %bitcast.2.refs_0_, s32[1,2048]{1,0:T(1,128)} %bitcast.33, s32[2,2048]{1,0:T(2,128)} %bitcast.30, f32[1,2048]{1,0:T(1,128)} %refs_3_.3, f32[7,2,32]{2,1,0:T(2,128)} %convert_bitcast_fusion.refs_4_, bf16[32,1,128,128]{3,2,1,0:T(8,128)(2,1)} %refs_5_.3, ...), custom_call_target="tpu_custom_call" | custom-call | tf_op jit(solution)/shard_map/repeat/pallas_call | solution.py:89
  5.7 8.6 %all-to-all-start.1 = ((bf16[8,128,128]{2,1,0:T(8,128)(2,1)}), bf16[8,128,128]{2,1,0:T(8,128)(2,1)}, u32[]{:S(2)}, u32[]{:S(2)}) async-start(bf16[8,128,128]{2,1,0:T(8,128)(2,1)} %repeat.1), calls=%async_computation.1 | async-start | bytes 524288 | tf_op jit(solution)/shard_map/all_to_all | solution.py:402
  14.3 7.5 %front.1 = (bf16[64,128,128]{2,1,0:T(8,128)(2,1)}, bf16[64,128,128]{2,1,0:T(8,128)(2,1)}) custom-call(s32[1]{0:T(128)} %bitcast.2.refs_0_, s32[1,2048]{1,0:T(1,128)} %bitcast.34, s32[2,2048]{1,0:T(2,128)} %bitcast.31, f32[1,2048]{1,0:T(1,128)} %refs_3_.3, f32[7,2,32]{2,1,0:T(2,128)} %convert_bitcast_fusion.refs_4_, bf16[32,1,128,128]{3,2,1,0:T(8,128)(2,1)} %refs_5_.3, ...), custom_call_target="tpu_custom_call" | custom-call | bytes 25165824 | tf_op jit(solution)/shard_map/front/pallas_call | solution.py:162
  21.8 3.0 %all-to-all-done.1 = bf16[8,128,128]{2,1,0:T(8,128)(2,1)} async-done(((bf16[8,128,128]{2,1,0:T(8,128)(2,1)}), bf16[8,128,128]{2,1,0:T(8,128)(2,1)}, u32[]{:S(2)}, u32[]{:S(2)}) %all-to-all-start.1) | async-done | bytes 262176 | tf_op jit(solution)/shard_map/all_to_all | solution.py:402
  24.8 7.4 %all-to-all-start.2 = ((bf16[64,128,128]{2,1,0:T(8,128)(2,1)}), bf16[64,128,128]{2,1,0:T(8,128)(2,1)S(1)}, u32[]{:S(2)}, u32[]{:S(2)}) async-start(bf16[64,128,128]{2,1,0:T(8,128)(2,1)} %get-tuple-element.99), calls=%async_computation.2 | async-start | bytes 4194304 | tf_op jit(solution)/shard_map/all_to_all | solution.py:411
  32.2 0.1 pad_add_fusion
  32.4 0.1 broadcast_add_fusion.1
  32.5 0.2 collective-permute-start.3
  32.7 2.7 %collective-permute-start.2 = (bf16[8,128,128]{2,1,0:T(8,128)(2,1)}, bf16[8,128,128]{2,1,0:T(8,128)(2,1)}, u32[]{:S(2)}, u32[]{:S(2)}) collective-permute-start(bf16[8,128,128]{2,1,0:T(8,128)(2,1)} %all-to-all-done.1), channel_id=1, source_target_pairs={{0,24},{4,28},{8,16},{12,20},{16,8},{20,12},{24,0},{28,4},{32,56},... | collective-permute-start | bytes 786440 | tf_op jit(solution)/shard_map/ppermute | solution.py:191
  35.4 0.9 collective-permute-start.1
  36.2 0.6 collective-permute-start
  36.8 0.5 broadcast.355
  37.3 0.0 copy-done.2
  37.3 0.7 reduce.10
  38.0 0.1 reshape.284
  38.1 0.1 copy.16
  38.2 0.2 reduce_window_sum.11
  38.4 0.1 copy.13
  38.4 0.1 copy.12
  38.5 0.2 and_reduce_fusion
  38.8 0.6 reduce_max.9
  39.4 1.6 %collective-permute-start.7 = (f32[]{:T(128)}, f32[]{:T(128)}, u32[]{:S(2)}, u32[]{:S(2)}) collective-permute-start(f32[]{:T(128)} %reduce_max.9), channel_id=1, source_target_pairs={{0,1},{1,0},{2,3},{3,2},{4,5},{5,4},{6,7},{7,6},{8,9},{9,8},{10,11... | collective-permute-start | bytes 20 | tf_op jit(solution)/shard_map/ppermute | solution.py:191
  41.0 0.0 copy-done.1
  41.0 0.1 add.103
  41.1 0.1 copy.14
  41.2 0.2 fusion.1
  41.5 0.6 broadcast.356
  42.1 0.0 copy-done.3
  42.1 0.7 reduce.11
  42.8 0.1 broadcast_in_dim.156
  42.9 0.1 copy.15
  42.9 0.2 fusion.3.refs_4_
  43.1 19.4 %collective-permute-done.2 = bf16[8,128,128]{2,1,0:T(8,128)(2,1)} collective-permute-done((bf16[8,128,128]{2,1,0:T(8,128)(2,1)}, bf16[8,128,128]{2,1,0:T(8,128)(2,1)}, u32[]{:S(2)}, u32[]{:S(2)}) %collective-permute-start.2) | collective-permute-done | bytes 262176 | tf_op jit(solution)/shard_map/ppermute | solution.py:191
  62.6 0.0 collective-permute-start.6
  62.6 0.0 collective-permute-done.1
  62.6 0.5 collective-permute-start.5
  63.1 0.0 collective-permute-done
  63.1 0.1 collective-permute-start.4
  63.2 0.1 shift_right_arithmetic.36
  63.3 0.1 and.100
  63.4 0.1 broadcast_in_dim.159
  63.4 0.1 broadcast_in_dim.180
  63.5 0.1 broadcast_in_dim.181
  63.6 0.8 fusion
  64.4 0.0 collective-permute-done.7
  65.7 4.6 %collective-permute-start.8 = (f32[]{:T(128)}, f32[]{:T(128)}, u32[]{:S(2)}, u32[]{:S(2)}) collective-permute-start(f32[]{:T(128)} %max.26), channel_id=1, source_target_pairs={{0,2},{1,3},{2,0},{3,1},{4,6},{5,7},{6,4},{7,5},{8,10},{9,11},{10,... | collective-permute-start | bytes 20 | tf_op jit(solution)/shard_map/ppermute | solution.py:191
  70.3 0.5 collective-permute-done.8
  71.5 0.0 collective-permute-done.3
  71.5 0.0 collective-permute-done.6
  71.5 0.0 collective-permute-done.5
  71.5 0.0 collective-permute-done.4
  71.5 11.1 %all-to-all-done.2 = bf16[64,128,128]{2,1,0:T(8,128)(2,1)S(1)} async-done(((bf16[64,128,128]{2,1,0:T(8,128)(2,1)}), bf16[64,128,128]{2,1,0:T(8,128)(2,1)S(1)}, u32[]{:S(2)}, u32[]{:S(2)}) %all-to-all-start.2) | async-done | bytes 2097184 | tf_op jit(solution)/shard_map/all_to_all | solution.py:411
  82.6 4.5 %conditional.1 = (bf16[136,512]{1,0:T(8,128)(2,1)}, bf16[136,512]{1,0:T(8,128)(2,1)}, bf16[136,512]{1,0:T(8,128)(2,1)}, bf16[136,512]{1,0:T(8,128)(2,1)}, bf16[1,1,512,512]{3,2,1,0:T(8,128)(2,1)}) conditional(s32[]{:T(128)} %convert_element_type.32, (bf16[64,128,128]{2,1,0:T(8,128)(2,1)}, s32[2]{0:T(128)S(1)}, s32[2,64]{1,0:T(2,128)S(1)}, ...), branch_computations={%region_6.7_spmd, %region_7.8_spmd} | conditional | bytes 4194344 | solution.py:449
  82.6 4.5 %place.3 = (bf16[512,512]{1,0:T(8,128)(2,1)}, bf16[136,512]{1,0:T(8,128)(2,1)}, bf16[136,512]{1,0:T(8,128)(2,1)}, bf16[136,512]{1,0:T(8,128)(2,1)}, bf16[136,512]{1,0:T(8,128)(2,1)}) custom-call(s32[2]{0:T(128)S(1)} %get-tuple-element.56.refs_0_, s32[2,64]{1,0:T(2,128)S(1)} %get-tuple-element.57.refs_1_, ...), custom_call_target="tpu_custom_call" | custom-call | tf_op jit(solution)/shard_map/cond/branch_1_fun/place/pallas_call | solution.py:275
  87.1 1.8 %collective-permute-start.9 = (bf16[136,512]{1,0:T(8,128)(2,1)}, bf16[136,512]{1,0:T(8,128)(2,1)S(1)}, u32[]{:S(2)}, u32[]{:S(2)}) collective-permute-start(bf16[136,512]{1,0:T(8,128)(2,1)} %get-tuple-element.121), channel_id=1, source_target_pairs={{0,1},{1,0},{2,3},{3,2},{4,5},{5,4},{6,7},{7,6},{8,9},{9,8},{10,11... | collective-permute-start | bytes 417800 | tf_op jit(solution)/shard_map/ppermute | solution.py:191
  88.9 3.0 %collective-permute-start.10 = (bf16[136,512]{1,0:T(8,128)(2,1)}, bf16[136,512]{1,0:T(8,128)(2,1)S(1)}, u32[]{:S(2)}, u32[]{:S(2)}) collective-permute-start(bf16[136,512]{1,0:T(8,128)(2,1)} %get-tuple-element.122), channel_id=1, source_target_pairs={{0,2},{1,3},{2,0},{3,1},{4,6},{5,7},{6,4},{7,5},{8,10},{9,11},{10,... | collective-permute-start | bytes 417800 | tf_op jit(solution)/shard_map/ppermute | solution.py:191
  91.9 0.0 collective-permute-start.11
  91.9 0.1 copy.18.refs_5_
  92.1 1.4 %collective-permute-done.9.refs_1_ = bf16[136,512]{1,0:T(8,128)(2,1)S(1)} collective-permute-done((bf16[136,512]{1,0:T(8,128)(2,1)}, bf16[136,512]{1,0:T(8,128)(2,1)S(1)}, u32[]{:S(2)}, u32[]{:S(2)}) %collective-permute-start.9) | collective-permute-done | bytes 139296 | tf_op jit(solution)/shard_map/ppermute | solution.py:191
  93.4 5.3 %collective-permute-done.10.refs_2_ = bf16[136,512]{1,0:T(8,128)(2,1)S(1)} collective-permute-done((bf16[136,512]{1,0:T(8,128)(2,1)}, bf16[136,512]{1,0:T(8,128)(2,1)S(1)}, u32[]{:S(2)}, u32[]{:S(2)}) %collective-permute-start.10) | collective-permute-done | bytes 139296 | tf_op jit(solution)/shard_map/ppermute | solution.py:191
  98.7 2.2 %collective-permute-done.11.refs_3_ = bf16[136,512]{1,0:T(8,128)(2,1)S(1)} collective-permute-done((bf16[136,512]{1,0:T(8,128)(2,1)}, bf16[136,512]{1,0:T(8,128)(2,1)S(1)}, u32[]{:S(2)}, u32[]{:S(2)}) %collective-permute-start.11) | collective-permute-done | bytes 139296 | tf_op jit(solution)/shard_map/ppermute | solution.py:191
  101.0 4.9 %detect.1 = bf16[64,128,512]{2,1,0:T(8,128)(2,1)} custom-call(bf16[136,512]{1,0:T(8,128)(2,1)} %get-tuple-element.120.refs_0_, bf16[136,512]{1,0:T(8,128)(2,1)S(1)} %collective-permute-done.9.refs_1_, bf16[136,512]{1,0:T(8,128)(2,1)S(1)} %collective-permute-done.10.refs_2_, bf16[136,512]{1,0:T(8,128)(2,1)S(1)} %collective-permute-done.11.refs_3_, ...), custom_call_target="tpu_custom_call" | custom-call | tf_op jit(solution)/shard_map/detect/pallas_call | solution.py:347
  (19 shorter events, 0.2 us)
Async XLA Ops:
  0.6 40.6 %copy-start = (bf16[64,100]{1,0:T(8,128)(2,1)S(1)}, bf16[64,100]{1,0:T(8,128)(2,1)}, u32[]{:S(2)}) copy-start(bf16[64,100]{1,0:T(8,128)(2,1)} %param.18) | copy-start | bytes 38404
  5.7 19.1 %all-to-all-start.1 = ((bf16[8,128,128]{2,1,0:T(8,128)(2,1)}), bf16[8,128,128]{2,1,0:T(8,128)(2,1)}, u32[]{:S(2)}, u32[]{:S(2)}) async-start(bf16[8,128,128]{2,1,0:T(8,128)(2,1)} %repeat.1), calls=%async_computation.1 | async-start | bytes 524288 | tf_op jit(solution)/shard_map/all_to_all | solution.py:402
  24.8 12.5 %copy-start.2 = (s32[1,2048,1]{1,2,0:T(1,128)S(1)}, s32[1,2048,1]{1,2,0:T(1,128)}, u32[]{:S(2)}) copy-start(s32[1,2048,1]{1,2,0:T(1,128)} %param.15) | copy-start | bytes 24580
  24.8 16.2 %copy-start.1 = (s32[1,2048,2]{1,2,0:T(2,128)S(1)}, s32[1,2048,2]{1,2,0:T(2,128)}, u32[]{:S(2)}) copy-start(s32[1,2048,2]{1,2,0:T(2,128)} %param.16) | copy-start | bytes 49156
  24.8 17.3 %copy-start.3 = (f32[1,2048]{1,0:T(1,128)S(1)}, f32[1,2048]{1,0:T(1,128)}, u32[]{:S(2)}) copy-start(f32[1,2048]{1,0:T(1,128)} %refs_3_.3) | copy-start | bytes 24580
  24.8 38.6 %copy-start.4 = (f32[64]{0:T(128)S(1)}, f32[64]{0:T(128)}, u32[]{:S(2)}) copy-start(f32[64]{0:T(128)} %param.19) | copy-start | bytes 772
  24.8 57.8 %all-to-all-start.2 = ((bf16[64,128,128]{2,1,0:T(8,128)(2,1)}), bf16[64,128,128]{2,1,0:T(8,128)(2,1)S(1)}, u32[]{:S(2)}, u32[]{:S(2)}) async-start(bf16[64,128,128]{2,1,0:T(8,128)(2,1)} %get-tuple-element.99), calls=%async_computation.2 | async-start | bytes 4194304 | tf_op jit(solution)/shard_map/all_to_all | solution.py:411
  32.5 39.0 %collective-permute-start.3 = (bf16[8,128,128]{2,1,0:T(8,128)(2,1)}, bf16[8,128,128]{2,1,0:T(8,128)(2,1)}, u32[]{:S(2)}, u32[]{:S(2)}) collective-permute-start(bf16[8,128,128]{2,1,0:T(8,128)(2,1)} %all-to-all-done.1), channel_id=1, source_target_pairs={{0,4},{4,0},{8,12},{12,8},{16,20},{20,16},{24,28},{28,24},{32,36},... | collective-permute-start | bytes 786440 | tf_op jit(solution)/shard_map/ppermute | solution.py:191
  32.7 29.9 %collective-permute-start.2 = (bf16[8,128,128]{2,1,0:T(8,128)(2,1)}, bf16[8,128,128]{2,1,0:T(8,128)(2,1)}, u32[]{:S(2)}, u32[]{:S(2)}) collective-permute-start(bf16[8,128,128]{2,1,0:T(8,128)(2,1)} %all-to-all-done.1), channel_id=1, source_target_pairs={{0,24},{4,28},{8,16},{12,20},{16,8},{20,12},{24,0},{28,4},{32,56},... | collective-permute-start | bytes 786440 | tf_op jit(solution)/shard_map/ppermute | solution.py:191
  35.4 27.2 %collective-permute-start.1 = (bf16[8,128,128]{2,1,0:T(8,128)(2,1)}, bf16[8,128,128]{2,1,0:T(8,128)(2,1)}, u32[]{:S(2)}, u32[]{:S(2)}) collective-permute-start(bf16[8,128,128]{2,1,0:T(8,128)(2,1)} %all-to-all-done.1), channel_id=1, source_target_pairs={{0,16},{4,20},{8,24},{12,28},{16,0},{20,4},{24,8},{28,12},{32,48},... | collective-permute-start | bytes 786440 | tf_op jit(solution)/shard_map/ppermute | solution.py:191
  36.2 26.8 %collective-permute-start = (bf16[8,128,128]{2,1,0:T(8,128)(2,1)}, bf16[8,128,128]{2,1,0:T(8,128)(2,1)}, u32[]{:S(2)}, u32[]{:S(2)}) collective-permute-start(bf16[8,128,128]{2,1,0:T(8,128)(2,1)} %all-to-all-done.1), channel_id=1, source_target_pairs={{0,8},{4,12},{8,0},{12,4},{16,24},{20,28},{24,16},{28,20},{32,40},... | collective-permute-start | bytes 786440 | tf_op jit(solution)/shard_map/ppermute | solution.py:191
  39.4 25.0 %collective-permute-start.7 = (f32[]{:T(128)}, f32[]{:T(128)}, u32[]{:S(2)}, u32[]{:S(2)}) collective-permute-start(f32[]{:T(128)} %reduce_max.9), channel_id=1, source_target_pairs={{0,1},{1,0},{2,3},{3,2},{4,5},{5,4},{6,7},{7,6},{8,9},{9,8},{10,11... | collective-permute-start | bytes 20 | tf_op jit(solution)/shard_map/ppermute | solution.py:191
  62.6 8.9 %collective-permute-start.6 = (bf16[8,128,128]{2,1,0:T(8,128)(2,1)}, bf16[8,128,128]{2,1,0:T(8,128)(2,1)}, u32[]{:S(2)}, u32[]{:S(2)}) collective-permute-start(bf16[8,128,128]{2,1,0:T(8,128)(2,1)} %collective-permute-done.2), channel_id=1, source_target_pairs={{0,4},{4,0},{8,12},{12,8},{16,20},{20,16},{24,28},{28,24},{32,36},... | collective-permute-start | bytes 786440 | tf_op jit(solution)/shard_map/ppermute | solution.py:191
  62.6 8.9 %collective-permute-start.5 = (bf16[8,128,128]{2,1,0:T(8,128)(2,1)}, bf16[8,128,128]{2,1,0:T(8,128)(2,1)}, u32[]{:S(2)}, u32[]{:S(2)}) collective-permute-start(bf16[8,128,128]{2,1,0:T(8,128)(2,1)} %collective-permute-done.1), channel_id=1, source_target_pairs={{0,4},{4,0},{8,12},{12,8},{16,20},{20,16},{24,28},{28,24},{32,36},... | collective-permute-start | bytes 786440 | tf_op jit(solution)/shard_map/ppermute | solution.py:191
  63.1 8.4 %collective-permute-start.4 = (bf16[8,128,128]{2,1,0:T(8,128)(2,1)}, bf16[8,128,128]{2,1,0:T(8,128)(2,1)}, u32[]{:S(2)}, u32[]{:S(2)}) collective-permute-start(bf16[8,128,128]{2,1,0:T(8,128)(2,1)} %collective-permute-done), channel_id=1, source_target_pairs={{0,4},{4,0},{8,12},{12,8},{16,20},{20,16},{24,28},{28,24},{32,36},... | collective-permute-start | bytes 786440 | tf_op jit(solution)/shard_map/ppermute | solution.py:191
  65.7 5.1 %collective-permute-start.8 = (f32[]{:T(128)}, f32[]{:T(128)}, u32[]{:S(2)}, u32[]{:S(2)}) collective-permute-start(f32[]{:T(128)} %max.26), channel_id=1, source_target_pairs={{0,2},{1,3},{2,0},{3,1},{4,6},{5,7},{6,4},{7,5},{8,10},{9,11},{10,... | collective-permute-start | bytes 20 | tf_op jit(solution)/shard_map/ppermute | solution.py:191
  87.1 6.3 %collective-permute-start.9 = (bf16[136,512]{1,0:T(8,128)(2,1)}, bf16[136,512]{1,0:T(8,128)(2,1)S(1)}, u32[]{:S(2)}, u32[]{:S(2)}) collective-permute-start(bf16[136,512]{1,0:T(8,128)(2,1)} %get-tuple-element.121), channel_id=1, source_target_pairs={{0,1},{1,0},{2,3},{3,2},{4,5},{5,4},{6,7},{7,6},{8,9},{9,8},{10,11... | collective-permute-start | bytes 417800 | tf_op jit(solution)/shard_map/ppermute | solution.py:191
  88.9 9.8 %collective-permute-start.10 = (bf16[136,512]{1,0:T(8,128)(2,1)}, bf16[136,512]{1,0:T(8,128)(2,1)S(1)}, u32[]{:S(2)}, u32[]{:S(2)}) collective-permute-start(bf16[136,512]{1,0:T(8,128)(2,1)} %get-tuple-element.122), channel_id=1, source_target_pairs={{0,2},{1,3},{2,0},{3,1},{4,6},{5,7},{6,4},{7,5},{8,10},{9,11},{10,... | collective-permute-start | bytes 417800 | tf_op jit(solution)/shard_map/ppermute | solution.py:191
  91.9 9.0 %collective-permute-start.11 = (bf16[136,512]{1,0:T(8,128)(2,1)}, bf16[136,512]{1,0:T(8,128)(2,1)S(1)}, u32[]{:S(2)}, u32[]{:S(2)}) collective-permute-start(bf16[136,512]{1,0:T(8,128)(2,1)} %get-tuple-element.123), channel_id=1, source_target_pairs={{0,3},{1,2},{2,1},{3,0},{4,7},{5,6},{6,5},{7,4},{8,11},{9,10},{10,... | collective-permute-start | bytes 417800 | tf_op jit(solution)/shard_map/ppermute | solution.py:191

commit v8 on v7

--- a/solution.py
+++ b/solution.py
@@ -51,10 +51,14 @@
     return out
 
 
-def repeat_kernel(
-    tiles, owner_ref, routes_ref, offs_ref, wts_ref, taps_ref,
-    exp_ref, rows_ref, cols_ref, out_ref, held, count, found, sems,
+def front_kernel(
+    part, parts, owner_ref, routes_ref, offs_ref, wts_ref, taps_ref,
+    exp_ref, rows_ref, cols_ref, *refs,
 ):
+    *outs, held, stage, count, ranks, found, load_sems, sems = refs[2 * part :]
+    buf0_ref, buf1_ref = outs[:2]
+    tiles = ranks.shape[0]
+    size = stage.shape[0]
     base = owner_ref[0] * tiles
     found[0] = 0
 
@@ -67,116 +71,77 @@
         dest = routes_ref[0, base + i]
         rank = count[dest]
         count[dest] = rank + 1
+        ranks[i] = rank
         found[0] = jnp.where(rank > 0, i, found[0])
 
-    tile = found[0]
-    copies = [
-        pltpu.make_async_copy(src.at[tile, 0], held.at[i], sems.at[i])
-        for i, src in enumerate((exp_ref, rows_ref, cols_ref))
-    ]
-    for copy in copies:
-        copy.start()
-    for copy in copies:
-        copy.wait()
-    warped = warp_tiles(
-        [tile], base, offs_ref, wts_ref, taps_ref, [held[0]], [held[1]], [held[2]]
-    )
-    out_ref[...] = jnp.broadcast_to(warped[0][None], out_ref.shape)
-
-
-def repeat(owner, routes, offs, wts, taps, exposures, warp_rows, warp_cols, npatch, copies):
-    anywhere = pl.BlockSpec(memory_space=pl.ANY)
-    return pl.pallas_call(
-        lambda *refs: repeat_kernel(exposures.shape[0], *refs),
-        name="repeat",
-        out_shape=jax.ShapeDtypeStruct((copies, S, S), BF16),
-        grid_spec=pltpu.PrefetchScalarGridSpec(
-            num_scalar_prefetch=5,
-            grid=(1,),
-            in_specs=[anywhere] * 3,
-            out_specs=pl.BlockSpec((copies, S, S), lambda i, *_: (0, 0, 0)),
-            scratch_shapes=[
-                pltpu.VMEM((3, S, S), BF16),
-                pltpu.SMEM((npatch,), jnp.int32),
-                pltpu.SMEM((1,), jnp.int32),
-                pltpu.SemaphoreType.DMA((3,)),
-            ],
-        ),
-    )(owner, routes, offs, wts, taps, exposures, warp_rows, warp_cols)
-
-
-def front_kernel(
-    chunk, owner_ref, routes_ref, offs_ref, wts_ref, taps_ref,
-    exp_ref, rows_ref, cols_ref, buf0_ref, buf1_ref, held, stage, count, load_sems, sems,
-):
-    tiles = stage.shape[0]
-    base = owner_ref[0] * tiles
+    chosen = found[0]
+    here = []
+    for n in range(part * size, part * size + size):
+        here.append(jnp.where(chosen >= n, n - 1, n) if n else chosen)
     loads = [
         [
-            pltpu.make_async_copy(
-                src.at[pl.ds(start, chunk), 0], held.at[i, pl.ds(start, chunk)], load_sems.at[i, n]
-            )
+            pltpu.make_async_copy(src.at[tile, 0], held.at[i, n], load_sems.at[i, n])
             for i, src in enumerate((exp_ref, rows_ref, cols_ref))
         ]
-        for n, start in enumerate(range(0, tiles, chunk))
+        for n, tile in enumerate(here)
     ]
     for copies in loads:
         for copy in copies:
             copy.start()
-
-    @pl.loop(0, count.shape[0], unroll=8)
-    def _(i):
-        count[i] = 0
-
-    for n, copies in enumerate(loads):
+    for copies in loads:
         for copy in copies:
             copy.wait()
-        here = [n * chunk + k for k in range(chunk)]
-        inputs = [[held[i, tile] for tile in here] for i in range(3)]
-        warped = warp_tiles(here, base, offs_ref, wts_ref, taps_ref, *inputs)
-        for tile, value in zip(here, warped):
-            stage[tile] = value
-        for tile in here:
-            dest = routes_ref[0, base + tile]
-            rank = count[dest]
-            count[dest] = rank + 1
-
-            @pl.when(rank == 0)
-            def _():
-                pltpu.make_async_copy(stage.at[tile], buf0_ref.at[dest], sems.at[tile]).start()
-
-            @pl.when(rank > 0)
-            def _():
-                pltpu.make_async_copy(stage.at[tile], buf1_ref.at[dest], sems.at[tile]).start()
-
-    @pl.loop(0, tiles, unroll=8)
-    def _(i):
-        pltpu.make_async_copy(stage.at[i], buf0_ref.at[0], sems.at[i]).wait()
-
-
-def front(owner, routes, offs, wts, taps, exposures, warp_rows, warp_cols, npatch):
-    tiles = exposures.shape[0]
-    chunk = 16
+    inputs = [[held[i, n] for n in range(size)] for i in range(3)]
+    warped = warp_tiles(here, base, offs_ref, wts_ref, taps_ref, *inputs)
+    if part == 0:
+        outs[2][...] = jnp.broadcast_to(warped[0][None], outs[2].shape)
+    for n, value in enumerate(warped):
+        stage[n] = value
+    for n, tile in enumerate(here):
+        dest = routes_ref[0, base + tile]
+        rank = ranks[tile]
+
+        @pl.when(rank == 0)
+        def _():
+            pltpu.make_async_copy(stage.at[n], buf0_ref.at[dest], sems.at[n]).start()
+
+        @pl.when(rank > 0)
+        def _():
+            pltpu.make_async_copy(stage.at[n], buf1_ref.at[dest], sems.at[n]).start()
+
+    for n in range(size):
+        pltpu.make_async_copy(stage.at[n], buf0_ref.at[0], sems.at[n]).wait()
+
+
+def front(part, inputs, buffers, npatch, copies):
+    parts = 2
+    tiles = inputs[5].shape[0]
+    size = tiles // parts
     anywhere = pl.BlockSpec(memory_space=pl.ANY)
+    outside = pl.BlockSpec(memory_space=pltpu.HBM)
+    whole = pl.BlockSpec(memory_space=pltpu.VMEM)
     scalars = pl.BlockSpec(memory_space=pltpu.SMEM)
+    slots = jax.ShapeDtypeStruct((npatch, S, S), BF16)
+    extra = jax.ShapeDtypeStruct((copies, S, S), BF16)
     return pl.pallas_call(
-        lambda *refs: front_kernel(chunk, *refs),
-        name="front",
-        out_shape=(
-            jax.ShapeDtypeStruct((npatch, S, S), BF16),
-            jax.ShapeDtypeStruct((npatch, S, S), BF16),
-        ),
-        cost_estimate=pl.CostEstimate(flops=0, bytes_accessed=24 << 20, transcendentals=0),
-        in_specs=[scalars] * 5 + [anywhere] * 3,
-        out_specs=(anywhere, anywhere),
+        lambda *refs: front_kernel(part, parts, *refs),
+        name="front" + "ab"[part],
+        out_shape=(slots, slots) if part else (slots, slots, extra),
+        cost_estimate=pl.CostEstimate(flops=0, bytes_accessed=16 << 20, transcendentals=0),
+        in_specs=[scalars] * 5 + [anywhere] * 3 + [outside] * len(buffers),
+        out_specs=(outside, outside) if part else (outside, outside, whole),
+        input_output_aliases={8: 0, 9: 1} if part else {},
         scratch_shapes=[
-            pltpu.VMEM((3, tiles, S, S), BF16),
-            pltpu.VMEM((tiles, S, S), BF16),
+            pltpu.VMEM((3, size, S, S), BF16),
+            pltpu.VMEM((size, S, S), BF16),
             pltpu.SMEM((npatch,), jnp.int32),
-            pltpu.SemaphoreType.DMA((3, tiles // chunk)),
-            pltpu.SemaphoreType.DMA((tiles,)),
+            pltpu.SMEM((tiles,), jnp.int32),
+            pltpu.SMEM((1,), jnp.int32),
+            pltpu.SemaphoreType.DMA((3, size)),
+            pltpu.SemaphoreType.DMA((size,)),
         ],
-    )(owner, routes, offs, wts, taps, exposures, warp_rows, warp_cols)
+        compiler_params=pltpu.CompilerParams(vmem_limit_bytes=63 << 20),
+    )(*inputs, *buffers)
 
 
 def gathered_source(index, owner, rows):
@@ -397,12 +362,12 @@
     offs_rows = offsets.transpose(0, 2, 1).reshape(2, -1)
     taps = psf_taps[:, 0].transpose(2, 1, 0).astype(F32)
     inputs = (owner[None], routes_row, offs_rows, weights, taps, exposures, warp_rows, warp_cols)
-    extra = repeat(*inputs, npatch, npatch // PLANE)
+    buf0, buf1, extra = front(0, inputs, (), npatch, npatch // PLANE)
     lines = [list(range(i, npatch, PLANE)) for i in range(PLANE)]
     near = lax.all_to_all(
         extra, "patch", split_axis=0, concat_axis=0, axis_index_groups=lines, tiled=True
     )
-    buf0, buf1 = front(*inputs, npatch)
+    buf0, buf1 = front(1, inputs, (buf0, buf1), npatch, npatch // PLANE)
     buf0, near, routes_row, offs_rows, weights, det_weight, det_bias = lax.optimization_barrier(
         (buf0, near, routes_row, offs_rows, weights, det_weight, det_bias)
     )

time: 108 us -> 109 us (level)
  Pallas kernels: 20.6 us -> 22.4 us
  waiting for transfers between devices: 42.9 us -> 44.2 us
    pallas_call x2, Pallas kernels: 11.3 us -> 13 us  [front(): pl.pallas_call(lambda *refs: front_kernel(part, parts, *refs), name='fron...]
    all_to_all x1, waiting for transfers between devices: 2.99 us -> 4.39 us  [body(): lax.all_to_all(extra, 'patch', split_axis=0, concat_axis=0, axis_index_gr...]
  transfers between devices with their start and end apart: 14 -> 14, of which waited for: 7 -> 7; matrix products, arithmetic and copies ran while one was open for 6% -> 6% of each run, Pallas kernels for 7% -> 6%
where the time goes in v8:
time: 109 us; the launch traced here: 108 us
  waiting for transfers between devices  44.2 us (41%)
  starting transfers between devices  31.1 us (29%)
  Pallas kernels  22.4 us (21%)
  other arithmetic  4.19 us (4%)
  between operations  2.88 us (3%)
  local copies, waits for them, and re-layouts  2.25 us (2%)
    ppermute x12, waiting for transfers between devices, swap(): return lax.ppermute(x, axis, [(i, i ^ mask) for i in range(size)])  28.7 us
    ppermute x12, starting transfers between devices, swap(): return lax.ppermute(x, axis, [(i, i ^ mask) for i in range(size)])  16.1 us
    pallas_call x2, Pallas kernels, front(): pl.pallas_call(lambda *refs: front_kernel(part, parts, *refs), name='fron...  13 us
    all_to_all x1, waiting for transfers between devices, body(): lax.all_to_all(buf0, 'patch', split_axis=0, concat_axis=0, tiled=True)  11.1 us
    all_to_all x1, starting transfers between devices, body(): lax.all_to_all(extra, 'patch', split_axis=0, concat_axis=0, axis_index_gr...  8.58 us
    all_to_all x1, starting transfers between devices, body(): lax.all_to_all(buf0, 'patch', split_axis=0, concat_axis=0, tiled=True)  6.46 us
    pallas_call x1, Pallas kernels, detect(): pl.pallas_call(lambda *refs: detect_kernel(nband, *refs), name='detect',...  4.9 us
    pallas_call x1, Pallas kernels, place(): pl.pallas_call(lambda *refs: place_kernel(nband, gathered, *refs), name='...  4.49 us
  transfers between devices with their start and end apart: 14, of which 7 were waited for; matrix products, arithmetic and copies ran while one was open for 6% of the time, Pallas kernels for 6%

profile of v8, /device:TPU:32, one launch (start us, length us, event | category | flops | bytes accessed | tf_op | source)
XLA Modules:
  0.0 108.0 jit_solution(585492946216172045)
XLA Ops:
  0.6 0.0 copy-start
  0.7 1.3 %convert_bitcast_fusion.refs_4_ = f32[7,2,32]{2,1,0:T(2,128)} fusion(bf16[32,1,2,7]{0,2,3,1:T(2,128)(2,1)} %param.12), kind=kLoop, calls=%fused_computation.44 | loop fusion | flops 448 | bytes 2688 | tf_op jit(solution)/shard_map/convert_element_type | solution.py:363
  1.9 6.8 %fronta.1 = (bf16[64,128,128]{2,1,0:T(8,128)(2,1)}, bf16[64,128,128]{2,1,0:T(8,128)(2,1)}, bf16[8,128,128]{2,1,0:T(8,128)(2,1)}) custom-call(s32[1]{0:T(128)} %bitcast.2.refs_0_, s32[1,2048]{1,0:T(1,128)} %bitcast.33, s32[2,2048]{1,0:T(2,128)} %bitcast.30, f32[1,2048]{1,0:T(1,128)} %refs_3_.3, f32[7,2,32]{2,1,0:T(2,128)} %convert_bitcast_fusion.refs_4_, ...), custom_call_target="tpu_custom_call" | custom-call | bytes 16777216 | tf_op jit(solution)/shard_map/fronta/pallas_call | solution.py:126
  8.8 8.6 %all-to-all-start.1 = ((bf16[8,128,128]{2,1,0:T(8,128)(2,1)}), bf16[8,128,128]{2,1,0:T(8,128)(2,1)}, u32[]{:S(2)}, u32[]{:S(2)}) async-start(bf16[8,128,128]{2,1,0:T(8,128)(2,1)} %get-tuple-element.104), calls=%async_computation.1 | async-start | bytes 524288 | tf_op jit(solution)/shard_map/all_to_all | solution.py:367
  17.4 6.1 %frontb.1 = (bf16[64,128,128]{2,1,0:T(8,128)(2,1)}, bf16[64,128,128]{2,1,0:T(8,128)(2,1)}) custom-call(s32[1]{0:T(128)} %bitcast.2.refs_0_, s32[1,2048]{1,0:T(1,128)} %bitcast.34, s32[2,2048]{1,0:T(2,128)} %bitcast.31, f32[1,2048]{1,0:T(1,128)} %refs_3_.3, f32[7,2,32]{2,1,0:T(2,128)} %convert_bitcast_fusion.refs_4_, ...), custom_call_target="tpu_custom_call", output_to_operand_aliasing={{0}: (8, {}), {1}: (9, {})} | custom-call | bytes 16777216 | tf_op jit(solution)/shard_map/frontb/pallas_call | solution.py:126
  23.5 4.4 %all-to-all-done.1 = bf16[8,128,128]{2,1,0:T(8,128)(2,1)} async-done(((bf16[8,128,128]{2,1,0:T(8,128)(2,1)}), bf16[8,128,128]{2,1,0:T(8,128)(2,1)}, u32[]{:S(2)}, u32[]{:S(2)}) %all-to-all-start.1) | async-done | bytes 262176 | tf_op jit(solution)/shard_map/all_to_all | solution.py:367
  27.9 6.5 %all-to-all-start.2 = ((bf16[64,128,128]{2,1,0:T(8,128)(2,1)}), bf16[64,128,128]{2,1,0:T(8,128)(2,1)S(1)}, u32[]{:S(2)}, u32[]{:S(2)}) async-start(bf16[64,128,128]{2,1,0:T(8,128)(2,1)} %get-tuple-element.105), calls=%async_computation.2 | async-start | bytes 4194304 | tf_op jit(solution)/shard_map/all_to_all | solution.py:376
  34.4 0.1 pad_add_fusion
  34.5 0.1 broadcast_add_fusion.1
  34.6 0.2 collective-permute-start.3
  34.8 2.7 %collective-permute-start.2 = (bf16[8,128,128]{2,1,0:T(8,128)(2,1)}, bf16[8,128,128]{2,1,0:T(8,128)(2,1)}, u32[]{:S(2)}, u32[]{:S(2)}) collective-permute-start(bf16[8,128,128]{2,1,0:T(8,128)(2,1)} %all-to-all-done.1), channel_id=1, source_target_pairs={{0,24},{4,28},{8,16},{12,20},{16,8},{20,12},{24,0},{28,4},{32,56},... | collective-permute-start | bytes 786440 | tf_op jit(solution)/shard_map/ppermute | solution.py:156
  37.5 0.9 collective-permute-start.1
  38.4 0.6 collective-permute-start
  38.9 0.5 broadcast.355
  39.4 0.0 copy-done.2
  39.4 0.7 reduce.10
  40.1 0.1 reshape.284
  40.2 0.1 copy.18
  40.3 0.2 reduce_window_sum.11
  40.5 0.1 copy.15
  40.6 0.1 copy.14
  40.6 0.2 and_reduce_fusion
  40.9 0.6 reduce_max.9
  41.5 1.6 %collective-permute-start.7 = (f32[]{:T(128)}, f32[]{:T(128)}, u32[]{:S(2)}, u32[]{:S(2)}) collective-permute-start(f32[]{:T(128)} %reduce_max.9), channel_id=1, source_target_pairs={{0,1},{1,0},{2,3},{3,2},{4,5},{5,4},{6,7},{7,6},{8,9},{9,8},{10,11... | collective-permute-start | bytes 20 | tf_op jit(solution)/shard_map/ppermute | solution.py:156
  43.1 0.0 copy-done.1
  43.1 0.1 add.103
  43.2 0.1 copy.16
  43.3 0.0 copy-done
  43.3 0.2 fusion.1
  43.6 0.6 broadcast.356
  44.2 0.7 reduce.11
  44.8 0.1 broadcast_in_dim.156
  44.9 0.1 copy.17
  45.0 0.2 fusion.3.refs_4_
  45.2 19.5 %collective-permute-done.2 = bf16[8,128,128]{2,1,0:T(8,128)(2,1)} collective-permute-done((bf16[8,128,128]{2,1,0:T(8,128)(2,1)}, bf16[8,128,128]{2,1,0:T(8,128)(2,1)}, u32[]{:S(2)}, u32[]{:S(2)}) %collective-permute-start.2) | collective-permute-done | bytes 262176 | tf_op jit(solution)/shard_map/ppermute | solution.py:156
  64.7 0.0 collective-permute-start.6
  64.7 0.0 collective-permute-done.1
  64.7 0.5 collective-permute-start.5
  65.2 0.0 collective-permute-done
  65.2 0.1 collective-permute-start.4
  65.3 0.1 shift_right_arithmetic.36
  65.4 0.1 and.100
  65.5 0.1 broadcast_in_dim.159
  65.6 0.1 broadcast_in_dim.180
  65.6 0.1 broadcast_in_dim.181
  65.7 0.8 fusion
  66.5 0.0 collective-permute-done.7
  67.8 4.8 %collective-permute-start.8 = (f32[]{:T(128)}, f32[]{:T(128)}, u32[]{:S(2)}, u32[]{:S(2)}) collective-permute-start(f32[]{:T(128)} %max.26), channel_id=1, source_target_pairs={{0,2},{1,3},{2,0},{3,1},{4,6},{5,7},{6,4},{7,5},{8,10},{9,11},{10,... | collective-permute-start | bytes 20 | tf_op jit(solution)/shard_map/ppermute | solution.py:156
  72.5 0.5 collective-permute-done.8
  73.6 0.0 collective-permute-done.3
  73.6 0.0 collective-permute-done.6
  73.7 0.0 collective-permute-done.5
  73.7 0.0 collective-permute-done.4
  73.7 11.1 %all-to-all-done.2 = bf16[64,128,128]{2,1,0:T(8,128)(2,1)S(1)} async-done(((bf16[64,128,128]{2,1,0:T(8,128)(2,1)}), bf16[64,128,128]{2,1,0:T(8,128)(2,1)S(1)}, u32[]{:S(2)}, u32[]{:S(2)}) %all-to-all-start.2) | async-done | bytes 2097184 | tf_op jit(solution)/shard_map/all_to_all | solution.py:376
  84.8 4.5 %conditional.1 = (bf16[136,512]{1,0:T(8,128)(2,1)}, bf16[136,512]{1,0:T(8,128)(2,1)}, bf16[136,512]{1,0:T(8,128)(2,1)}, bf16[136,512]{1,0:T(8,128)(2,1)}, bf16[1,1,512,512]{3,2,1,0:T(8,128)(2,1)}) conditional(s32[]{:T(128)} %convert_element_type.32, (bf16[64,128,128]{2,1,0:T(8,128)(2,1)}, s32[2]{0:T(128)S(1)}, s32[2,64]{1,0:T(2,128)S(1)}, ...), branch_computations={%region_6.7_spmd, %region_7.8_spmd} | conditional | bytes 4194344 | solution.py:414
  84.8 4.5 %place.3 = (bf16[512,512]{1,0:T(8,128)(2,1)}, bf16[136,512]{1,0:T(8,128)(2,1)}, bf16[136,512]{1,0:T(8,128)(2,1)}, bf16[136,512]{1,0:T(8,128)(2,1)}, bf16[136,512]{1,0:T(8,128)(2,1)}) custom-call(s32[2]{0:T(128)S(1)} %get-tuple-element.56.refs_0_, s32[2,64]{1,0:T(2,128)S(1)} %get-tuple-element.57.refs_1_, ...), custom_call_target="tpu_custom_call" | custom-call | tf_op jit(solution)/shard_map/cond/branch_1_fun/place/pallas_call | solution.py:240
  89.3 1.8 %collective-permute-start.9 = (bf16[136,512]{1,0:T(8,128)(2,1)}, bf16[136,512]{1,0:T(8,128)(2,1)S(1)}, u32[]{:S(2)}, u32[]{:S(2)}) collective-permute-start(bf16[136,512]{1,0:T(8,128)(2,1)} %get-tuple-element.127), channel_id=1, source_target_pairs={{0,1},{1,0},{2,3},{3,2},{4,5},{5,4},{6,7},{7,6},{8,9},{9,8},{10,11... | collective-permute-start | bytes 417800 | tf_op jit(solution)/shard_map/ppermute | solution.py:156
  91.0 3.0 %collective-permute-start.10 = (bf16[136,512]{1,0:T(8,128)(2,1)}, bf16[136,512]{1,0:T(8,128)(2,1)S(1)}, u32[]{:S(2)}, u32[]{:S(2)}) collective-permute-start(bf16[136,512]{1,0:T(8,128)(2,1)} %get-tuple-element.128), channel_id=1, source_target_pairs={{0,2},{1,3},{2,0},{3,1},{4,6},{5,7},{6,4},{7,5},{8,10},{9,11},{10,... | collective-permute-start | bytes 417800 | tf_op jit(solution)/shard_map/ppermute | solution.py:156
  94.0 0.0 collective-permute-start.11
  94.1 0.1 copy.20.refs_5_
  94.2 1.4 %collective-permute-done.9.refs_1_ = bf16[136,512]{1,0:T(8,128)(2,1)S(1)} collective-permute-done((bf16[136,512]{1,0:T(8,128)(2,1)}, bf16[136,512]{1,0:T(8,128)(2,1)S(1)}, u32[]{:S(2)}, u32[]{:S(2)}) %collective-permute-start.9) | collective-permute-done | bytes 139296 | tf_op jit(solution)/shard_map/ppermute | solution.py:156
  95.6 5.1 %collective-permute-done.10.refs_2_ = bf16[136,512]{1,0:T(8,128)(2,1)S(1)} collective-permute-done((bf16[136,512]{1,0:T(8,128)(2,1)}, bf16[136,512]{1,0:T(8,128)(2,1)S(1)}, u32[]{:S(2)}, u32[]{:S(2)}) %collective-permute-start.10) | collective-permute-done | bytes 139296 | tf_op jit(solution)/shard_map/ppermute | solution.py:156
  100.7 2.2 %collective-permute-done.11.refs_3_ = bf16[136,512]{1,0:T(8,128)(2,1)S(1)} collective-permute-done((bf16[136,512]{1,0:T(8,128)(2,1)}, bf16[136,512]{1,0:T(8,128)(2,1)S(1)}, u32[]{:S(2)}, u32[]{:S(2)}) %collective-permute-start.11) | collective-permute-done | bytes 139296 | tf_op jit(solution)/shard_map/ppermute | solution.py:156
  102.9 4.9 %detect.1 = bf16[64,128,512]{2,1,0:T(8,128)(2,1)} custom-call(bf16[136,512]{1,0:T(8,128)(2,1)} %get-tuple-element.126.refs_0_, bf16[136,512]{1,0:T(8,128)(2,1)S(1)} %collective-permute-done.9.refs_1_, bf16[136,512]{1,0:T(8,128)(2,1)S(1)} %collective-permute-done.10.refs_2_, bf16[136,512]{1,0:T(8,128)(2,1)S(1)} %collective-permute-done.11.refs_3_, ...), custom_call_target="tpu_custom_call" | custom-call | tf_op jit(solution)/shard_map/detect/pallas_call | solution.py:312
  (19 shorter events, 0.2 us)
Async XLA Ops:
  0.6 42.7 %copy-start = (bf16[64,100]{1,0:T(8,128)(2,1)S(1)}, bf16[64,100]{1,0:T(8,128)(2,1)}, u32[]{:S(2)}) copy-start(bf16[64,100]{1,0:T(8,128)(2,1)} %param.18) | copy-start | bytes 38404
  8.8 19.1 %all-to-all-start.1 = ((bf16[8,128,128]{2,1,0:T(8,128)(2,1)}), bf16[8,128,128]{2,1,0:T(8,128)(2,1)}, u32[]{:S(2)}, u32[]{:S(2)}) async-start(bf16[8,128,128]{2,1,0:T(8,128)(2,1)} %get-tuple-element.104), calls=%async_computation.1 | async-start | bytes 524288 | tf_op jit(solution)/shard_map/all_to_all | solution.py:367
  27.9 11.6 %copy-start.2 = (s32[1,2048,1]{1,2,0:T(1,128)S(1)}, s32[1,2048,1]{1,2,0:T(1,128)}, u32[]{:S(2)}) copy-start(s32[1,2048,1]{1,2,0:T(1,128)} %param.15) | copy-start | bytes 24580
  27.9 15.2 %copy-start.1 = (s32[1,2048,2]{1,2,0:T(2,128)S(1)}, s32[1,2048,2]{1,2,0:T(2,128)}, u32[]{:S(2)}) copy-start(s32[1,2048,2]{1,2,0:T(2,128)} %param.16) | copy-start | bytes 49156
  27.9 16.3 %copy-start.3 = (f32[1,2048]{1,0:T(1,128)S(1)}, f32[1,2048]{1,0:T(1,128)}, u32[]{:S(2)}) copy-start(f32[1,2048]{1,0:T(1,128)} %refs_3_.3) | copy-start | bytes 24580
  27.9 37.7 %copy-start.4 = (f32[64]{0:T(128)S(1)}, f32[64]{0:T(128)}, u32[]{:S(2)}) copy-start(f32[64]{0:T(128)} %param.19) | copy-start | bytes 772
  27.9 56.9 %all-to-all-start.2 = ((bf16[64,128,128]{2,1,0:T(8,128)(2,1)}), bf16[64,128,128]{2,1,0:T(8,128)(2,1)S(1)}, u32[]{:S(2)}, u32[]{:S(2)}) async-start(bf16[64,128,128]{2,1,0:T(8,128)(2,1)} %get-tuple-element.105), calls=%async_computation.2 | async-start | bytes 4194304 | tf_op jit(solution)/shard_map/all_to_all | solution.py:376
  34.6 39.1 %collective-permute-start.3 = (bf16[8,128,128]{2,1,0:T(8,128)(2,1)}, bf16[8,128,128]{2,1,0:T(8,128)(2,1)}, u32[]{:S(2)}, u32[]{:S(2)}) collective-permute-start(bf16[8,128,128]{2,1,0:T(8,128)(2,1)} %all-to-all-done.1), channel_id=1, source_target_pairs={{0,4},{4,0},{8,12},{12,8},{16,20},{20,16},{24,28},{28,24},{32,36},... | collective-permute-start | bytes 786440 | tf_op jit(solution)/shard_map/ppermute | solution.py:156
  34.8 29.9 %collective-permute-start.2 = (bf16[8,128,128]{2,1,0:T(8,128)(2,1)}, bf16[8,128,128]{2,1,0:T(8,128)(2,1)}, u32[]{:S(2)}, u32[]{:S(2)}) collective-permute-start(bf16[8,128,128]{2,1,0:T(8,128)(2,1)} %all-to-all-done.1), channel_id=1, source_target_pairs={{0,24},{4,28},{8,16},{12,20},{16,8},{20,12},{24,0},{28,4},{32,56},... | collective-permute-start | bytes 786440 | tf_op jit(solution)/shard_map/ppermute | solution.py:156
  37.5 27.2 %collective-permute-start.1 = (bf16[8,128,128]{2,1,0:T(8,128)(2,1)}, bf16[8,128,128]{2,1,0:T(8,128)(2,1)}, u32[]{:S(2)}, u32[]{:S(2)}) collective-permute-start(bf16[8,128,128]{2,1,0:T(8,128)(2,1)} %all-to-all-done.1), channel_id=1, source_target_pairs={{0,16},{4,20},{8,24},{12,28},{16,0},{20,4},{24,8},{28,12},{32,48},... | collective-permute-start | bytes 786440 | tf_op jit(solution)/shard_map/ppermute | solution.py:156
  38.4 26.8 %collective-permute-start = (bf16[8,128,128]{2,1,0:T(8,128)(2,1)}, bf16[8,128,128]{2,1,0:T(8,128)(2,1)}, u32[]{:S(2)}, u32[]{:S(2)}) collective-permute-start(bf16[8,128,128]{2,1,0:T(8,128)(2,1)} %all-to-all-done.1), channel_id=1, source_target_pairs={{0,8},{4,12},{8,0},{12,4},{16,24},{20,28},{24,16},{28,20},{32,40},... | collective-permute-start | bytes 786440 | tf_op jit(solution)/shard_map/ppermute | solution.py:156
  41.5 25.0 %collective-permute-start.7 = (f32[]{:T(128)}, f32[]{:T(128)}, u32[]{:S(2)}, u32[]{:S(2)}) collective-permute-start(f32[]{:T(128)} %reduce_max.9), channel_id=1, source_target_pairs={{0,1},{1,0},{2,3},{3,2},{4,5},{5,4},{6,7},{7,6},{8,9},{9,8},{10,11... | collective-permute-start | bytes 20 | tf_op jit(solution)/shard_map/ppermute | solution.py:156
  64.7 9.0 %collective-permute-start.6 = (bf16[8,128,128]{2,1,0:T(8,128)(2,1)}, bf16[8,128,128]{2,1,0:T(8,128)(2,1)}, u32[]{:S(2)}, u32[]{:S(2)}) collective-permute-start(bf16[8,128,128]{2,1,0:T(8,128)(2,1)} %collective-permute-done.2), channel_id=1, source_target_pairs={{0,4},{4,0},{8,12},{12,8},{16,20},{20,16},{24,28},{28,24},{32,36},... | collective-permute-start | bytes 786440 | tf_op jit(solution)/shard_map/ppermute | solution.py:156
  64.7 9.0 %collective-permute-start.5 = (bf16[8,128,128]{2,1,0:T(8,128)(2,1)}, bf16[8,128,128]{2,1,0:T(8,128)(2,1)}, u32[]{:S(2)}, u32[]{:S(2)}) collective-permute-start(bf16[8,128,128]{2,1,0:T(8,128)(2,1)} %collective-permute-done.1), channel_id=1, source_target_pairs={{0,4},{4,0},{8,12},{12,8},{16,20},{20,16},{24,28},{28,24},{32,36},... | collective-permute-start | bytes 786440 | tf_op jit(solution)/shard_map/ppermute | solution.py:156
  65.2 8.5 %collective-permute-start.4 = (bf16[8,128,128]{2,1,0:T(8,128)(2,1)}, bf16[8,128,128]{2,1,0:T(8,128)(2,1)}, u32[]{:S(2)}, u32[]{:S(2)}) collective-permute-start(bf16[8,128,128]{2,1,0:T(8,128)(2,1)} %collective-permute-done), channel_id=1, source_target_pairs={{0,4},{4,0},{8,12},{12,8},{16,20},{20,16},{24,28},{28,24},{32,36},... | collective-permute-start | bytes 786440 | tf_op jit(solution)/shard_map/ppermute | solution.py:156
  67.8 5.3 %collective-permute-start.8 = (f32[]{:T(128)}, f32[]{:T(128)}, u32[]{:S(2)}, u32[]{:S(2)}) collective-permute-start(f32[]{:T(128)} %max.26), channel_id=1, source_target_pairs={{0,2},{1,3},{2,0},{3,1},{4,6},{5,7},{6,4},{7,5},{8,10},{9,11},{10,... | collective-permute-start | bytes 20 | tf_op jit(solution)/shard_map/ppermute | solution.py:156
  89.3 6.3 %collective-permute-start.9 = (bf16[136,512]{1,0:T(8,128)(2,1)}, bf16[136,512]{1,0:T(8,128)(2,1)S(1)}, u32[]{:S(2)}, u32[]{:S(2)}) collective-permute-start(bf16[136,512]{1,0:T(8,128)(2,1)} %get-tuple-element.127), channel_id=1, source_target_pairs={{0,1},{1,0},{2,3},{3,2},{4,5},{5,4},{6,7},{7,6},{8,9},{9,8},{10,11... | collective-permute-start | bytes 417800 | tf_op jit(solution)/shard_map/ppermute | solution.py:156
  91.0 9.7 %collective-permute-start.10 = (bf16[136,512]{1,0:T(8,128)(2,1)}, bf16[136,512]{1,0:T(8,128)(2,1)S(1)}, u32[]{:S(2)}, u32[]{:S(2)}) collective-permute-start(bf16[136,512]{1,0:T(8,128)(2,1)} %get-tuple-element.128), channel_id=1, source_target_pairs={{0,2},{1,3},{2,0},{3,1},{4,6},{5,7},{6,4},{7,5},{8,10},{9,11},{10,... | collective-permute-start | bytes 417800 | tf_op jit(solution)/shard_map/ppermute | solution.py:156
  94.0 8.9 %collective-permute-start.11 = (bf16[136,512]{1,0:T(8,128)(2,1)}, bf16[136,512]{1,0:T(8,128)(2,1)S(1)}, u32[]{:S(2)}, u32[]{:S(2)}) collective-permute-start(bf16[136,512]{1,0:T(8,128)(2,1)} %get-tuple-element.129), channel_id=1, source_target_pairs={{0,3},{1,2},{2,1},{3,0},{4,7},{5,6},{6,5},{7,4},{8,11},{9,10},{10,... | collective-permute-start | bytes 417800 | tf_op jit(solution)/shard_map/ppermute | solution.py:156

commit v9 on v7

--- a/solution.py
+++ b/solution.py
@@ -51,11 +51,37 @@
     return out
 
 
+def own_entries(owner_ref, sources, targets, sems, tiles):
+    per_row = LANES // tiles
+    start = pl.multiple_of((owner_ref[0] // per_row) * LANES, LANES)
+    copies = [
+        pltpu.make_async_copy(src.at[:, pl.ds(start, LANES)], dst, sems.at[i])
+        for i, (src, dst) in enumerate(zip(sources, targets))
+    ]
+    for copy in copies:
+        copy.start()
+    for copy in copies:
+        copy.wait()
+    return (owner_ref[0] % per_row) * tiles
+
+
+def own_scratch():
+    return [
+        pltpu.SMEM((1, LANES), jnp.int32),
+        pltpu.SMEM((2, LANES), jnp.int32),
+        pltpu.SMEM((1, LANES), F32),
+        pltpu.SemaphoreType.DMA((3,)),
+    ]
+
+
 def repeat_kernel(
-    tiles, owner_ref, routes_ref, offs_ref, wts_ref, taps_ref,
+    tiles, owner_ref, all_routes, all_offs, all_wts, taps_ref,
     exp_ref, rows_ref, cols_ref, out_ref, held, count, found, sems,
+    routes_ref, offs_ref, wts_ref, own_sems,
 ):
-    base = owner_ref[0] * tiles
+    base = own_entries(
+        owner_ref, (all_routes, all_offs, all_wts), (routes_ref, offs_ref, wts_ref), own_sems, tiles
+    )
     found[0] = 0
 
     @pl.loop(0, count.shape[0], unroll=8)
@@ -86,31 +112,29 @@
 
 def repeat(owner, routes, offs, wts, taps, exposures, warp_rows, warp_cols, npatch, copies):
     anywhere = pl.BlockSpec(memory_space=pl.ANY)
+    scalars = pl.BlockSpec(memory_space=pltpu.SMEM)
     return pl.pallas_call(
         lambda *refs: repeat_kernel(exposures.shape[0], *refs),
         name="repeat",
         out_shape=jax.ShapeDtypeStruct((copies, S, S), BF16),
-        grid_spec=pltpu.PrefetchScalarGridSpec(
-            num_scalar_prefetch=5,
-            grid=(1,),
-            in_specs=[anywhere] * 3,
-            out_specs=pl.BlockSpec((copies, S, S), lambda i, *_: (0, 0, 0)),
-            scratch_shapes=[
-                pltpu.VMEM((3, S, S), BF16),
-                pltpu.SMEM((npatch,), jnp.int32),
-                pltpu.SMEM((1,), jnp.int32),
-                pltpu.SemaphoreType.DMA((3,)),
-            ],
-        ),
+        in_specs=[scalars, anywhere, anywhere, anywhere, scalars] + [anywhere] * 3,
+        out_specs=pl.BlockSpec(memory_space=pltpu.VMEM),
+        scratch_shapes=[
+            pltpu.VMEM((3, S, S), BF16),
+            pltpu.SMEM((npatch,), jnp.int32),
+            pltpu.SMEM((1,), jnp.int32),
+            pltpu.SemaphoreType.DMA((3,)),
+            *own_scratch(),
+        ],
     )(owner, routes, offs, wts, taps, exposures, warp_rows, warp_cols)
 
 
 def front_kernel(
-    chunk, owner_ref, routes_ref, offs_ref, wts_ref, taps_ref,
+    chunk, owner_ref, all_routes, all_offs, all_wts, taps_ref,
     exp_ref, rows_ref, cols_ref, buf0_ref, buf1_ref, held, stage, count, load_sems, sems,
+    routes_ref, offs_ref, wts_ref, own_sems,
 ):
     tiles = stage.shape[0]
-    base = owner_ref[0] * tiles
     loads = [
         [
             pltpu.make_async_copy(
@@ -128,6 +152,9 @@
     def _(i):
         count[i] = 0
 
+    base = own_entries(
+        owner_ref, (all_routes, all_offs, all_wts), (routes_ref, offs_ref, wts_ref), own_sems, tiles
+    )
     for n, copies in enumerate(loads):
         for copy in copies:
             copy.wait()
@@ -167,7 +194,7 @@
             jax.ShapeDtypeStruct((npatch, S, S), BF16),
         ),
         cost_estimate=pl.CostEstimate(flops=0, bytes_accessed=24 << 20, transcendentals=0),
-        in_specs=[scalars] * 5 + [anywhere] * 3,
+        in_specs=[scalars, anywhere, anywhere, anywhere, scalars] + [anywhere] * 3,
         out_specs=(anywhere, anywhere),
         scratch_shapes=[
             pltpu.VMEM((3, tiles, S, S), BF16),
@@ -175,6 +202,7 @@
             pltpu.SMEM((npatch,), jnp.int32),
             pltpu.SemaphoreType.DMA((3, tiles // chunk)),
             pltpu.SemaphoreType.DMA((tiles,)),
+            *own_scratch(),
         ],
     )(owner, routes, offs, wts, taps, exposures, warp_rows, warp_cols)
 

time: 108 us -> 106 us (0.981); the launches traced: 106 us -> 106 us
  no operation moved by 1% of the time
where the time goes in v9:
time: 106 us
  waiting for transfers between devices  43.1 us (41%)
  starting transfers between devices  31.4 us (30%)
  Pallas kernels  20.5 us (19%)
  other arithmetic  4.25 us (4%)
  between operations  3.05 us (3%)
  local copies, waits for them, and re-layouts  2.26 us (2%)
    ppermute x12, waiting for transfers between devices, swap(): return lax.ppermute(x, axis, [(i, i ^ mask) for i in range(size)])  28.4 us
    ppermute x12, starting transfers between devices, swap(): return lax.ppermute(x, axis, [(i, i ^ mask) for i in range(size)])  15.9 us
    all_to_all x1, waiting for transfers between devices, body(): lax.all_to_all(buf0, 'patch', split_axis=0, concat_axis=0, tiled=True)  11.1 us
    all_to_all x1, starting transfers between devices, body(): lax.all_to_all(extra, 'patch', split_axis=0, concat_axis=0, axis_index_gr...  8.58 us
    pallas_call x1, Pallas kernels, front(): pl.pallas_call(lambda *refs: front_kernel(chunk, *refs), name='front', ou...  7.03 us
    all_to_all x1, starting transfers between devices, body(): lax.all_to_all(buf0, 'patch', split_axis=0, concat_axis=0, tiled=True)  6.92 us
    pallas_call x1, Pallas kernels, detect(): pl.pallas_call(lambda *refs: detect_kernel(nband, *refs), name='detect',...  4.9 us
    pallas_call x1, Pallas kernels, place(): pl.pallas_call(lambda *refs: place_kernel(nband, gathered, *refs), name='...  4.66 us
  transfers between devices with their start and end apart: 14, of which 7 were waited for; matrix products, arithmetic and copies ran while one was open for 6% of the time, Pallas kernels for 7%

profile of v9, /device:TPU:32, one launch (start us, length us, event | category | flops | bytes accessed | tf_op | source)
XLA Modules:
  0.0 105.5 jit_solution(9220166963777867487)
XLA Ops:
  0.6 0.0 copy-start
  0.7 1.3 %convert_bitcast_fusion.refs_4_ = f32[7,2,32]{2,1,0:T(2,128)} fusion(bf16[32,1,2,7]{0,2,3,1:T(2,128)(2,1)} %param.12), kind=kLoop, calls=%fused_computation.44 | loop fusion | flops 448 | bytes 2688 | tf_op jit(solution)/shard_map/convert_element_type | solution.py:426
  1.9 3.9 %repeat.1 = bf16[8,128,128]{2,1,0:T(8,128)(2,1)} custom-call(s32[1]{0:T(128)} %bitcast.2.refs_0_, s32[1,2048]{1,0:T(1,128)} %bitcast.33, s32[2,2048]{1,0:T(2,128)} %bitcast.30, f32[1,2048]{1,0:T(1,128)} %refs_3_.3, f32[7,2,32]{2,1,0:T(2,128)} %convert_bitcast_fusion.refs_4_, bf16[32,1,128,128]{3,2,1,0:T(8,128)(2,1)} %refs_5_.3, ...), custom_call_target="tpu_custom_call" | custom-call | tf_op jit(solution)/shard_map/repeat/pallas_call | solution.py:116
  5.9 8.6 %all-to-all-start.1 = ((bf16[8,128,128]{2,1,0:T(8,128)(2,1)}), bf16[8,128,128]{2,1,0:T(8,128)(2,1)}, u32[]{:S(2)}, u32[]{:S(2)}) async-start(bf16[8,128,128]{2,1,0:T(8,128)(2,1)} %repeat.1), calls=%async_computation.1 | async-start | bytes 524288 | tf_op jit(solution)/shard_map/all_to_all | solution.py:430
  14.5 7.0 %front.1 = (bf16[64,128,128]{2,1,0:T(8,128)(2,1)}, bf16[64,128,128]{2,1,0:T(8,128)(2,1)}) custom-call(s32[1]{0:T(128)} %bitcast.2.refs_0_, s32[1,2048]{1,0:T(1,128)} %bitcast.34, s32[2,2048]{1,0:T(2,128)} %bitcast.31, f32[1,2048]{1,0:T(1,128)} %refs_3_.3, f32[7,2,32]{2,1,0:T(2,128)} %convert_bitcast_fusion.refs_4_, bf16[32,1,128,128]{3,2,1,0:T(8,128)(2,1)} %refs_5_.3, ...), custom_call_target="tpu_custom_call" | custom-call | bytes 25165824 | tf_op jit(solution)/shard_map/front/pallas_call | solution.py:189
  21.5 3.5 %all-to-all-done.1 = bf16[8,128,128]{2,1,0:T(8,128)(2,1)} async-done(((bf16[8,128,128]{2,1,0:T(8,128)(2,1)}), bf16[8,128,128]{2,1,0:T(8,128)(2,1)}, u32[]{:S(2)}, u32[]{:S(2)}) %all-to-all-start.1) | async-done | bytes 262176 | tf_op jit(solution)/shard_map/all_to_all | solution.py:430
  25.0 6.9 %all-to-all-start.2 = ((bf16[64,128,128]{2,1,0:T(8,128)(2,1)}), bf16[64,128,128]{2,1,0:T(8,128)(2,1)S(1)}, u32[]{:S(2)}, u32[]{:S(2)}) async-start(bf16[64,128,128]{2,1,0:T(8,128)(2,1)} %get-tuple-element.99), calls=%async_computation.2 | async-start | bytes 4194304 | tf_op jit(solution)/shard_map/all_to_all | solution.py:439
  31.9 0.1 pad_add_fusion
  32.1 0.1 broadcast_add_fusion.1
  32.1 0.2 collective-permute-start.3
  32.4 2.7 %collective-permute-start.2 = (bf16[8,128,128]{2,1,0:T(8,128)(2,1)}, bf16[8,128,128]{2,1,0:T(8,128)(2,1)}, u32[]{:S(2)}, u32[]{:S(2)}) collective-permute-start(bf16[8,128,128]{2,1,0:T(8,128)(2,1)} %all-to-all-done.1), channel_id=1, source_target_pairs={{0,24},{4,28},{8,16},{12,20},{16,8},{20,12},{24,0},{28,4},{32,56},... | collective-permute-start | bytes 786440 | tf_op jit(solution)/shard_map/ppermute | solution.py:219
  35.1 0.9 collective-permute-start.1
  35.9 0.6 collective-permute-start
  36.5 0.5 broadcast.355
  37.0 0.0 copy-done.2
  37.0 0.7 reduce.10
  37.7 0.1 reshape.284
  37.7 0.1 copy.16
  37.8 0.2 reduce_window_sum.11
  38.0 0.1 copy.13
  38.1 0.1 copy.12
  38.2 0.2 and_reduce_fusion
  38.5 0.6 reduce_max.9
  39.1 1.6 %collective-permute-start.7 = (f32[]{:T(128)}, f32[]{:T(128)}, u32[]{:S(2)}, u32[]{:S(2)}) collective-permute-start(f32[]{:T(128)} %reduce_max.9), channel_id=1, source_target_pairs={{0,1},{1,0},{2,3},{3,2},{4,5},{5,4},{6,7},{7,6},{8,9},{9,8},{10,11... | collective-permute-start | bytes 20 | tf_op jit(solution)/shard_map/ppermute | solution.py:219
  40.7 0.0 copy-done.1
  40.7 0.1 add.103
  40.8 0.1 copy.14
  40.9 0.2 fusion.1
  41.2 0.6 broadcast.356
  41.8 0.7 reduce.11
  42.5 0.1 broadcast_in_dim.156
  42.5 0.1 copy.15
  42.6 0.2 fusion.3.refs_4_
  42.8 19.4 %collective-permute-done.2 = bf16[8,128,128]{2,1,0:T(8,128)(2,1)} collective-permute-done((bf16[8,128,128]{2,1,0:T(8,128)(2,1)}, bf16[8,128,128]{2,1,0:T(8,128)(2,1)}, u32[]{:S(2)}, u32[]{:S(2)}) %collective-permute-start.2) | collective-permute-done | bytes 262176 | tf_op jit(solution)/shard_map/ppermute | solution.py:219
  62.2 0.0 collective-permute-start.6
  62.2 0.0 collective-permute-done.1
  62.2 0.5 collective-permute-start.5
  62.8 0.0 collective-permute-done
  62.8 0.1 collective-permute-start.4
  62.9 0.1 shift_right_arithmetic.36
  63.0 0.1 and.100
  63.0 0.1 broadcast_in_dim.159
  63.1 0.0 copy-done.4
  63.1 0.1 broadcast_in_dim.180
  63.2 0.1 broadcast_in_dim.181
  63.3 0.8 fusion
  64.1 0.0 collective-permute-done.7
  65.4 4.6 %collective-permute-start.8 = (f32[]{:T(128)}, f32[]{:T(128)}, u32[]{:S(2)}, u32[]{:S(2)}) collective-permute-start(f32[]{:T(128)} %max.26), channel_id=1, source_target_pairs={{0,2},{1,3},{2,0},{3,1},{4,6},{5,7},{6,4},{7,5},{8,10},{9,11},{10,... | collective-permute-start | bytes 20 | tf_op jit(solution)/shard_map/ppermute | solution.py:219
  70.0 0.5 collective-permute-done.8
  71.2 0.0 collective-permute-done.3
  71.2 0.0 collective-permute-done.6
  71.2 0.0 collective-permute-done.5
  71.2 0.0 collective-permute-done.4
  71.2 11.1 %all-to-all-done.2 = bf16[64,128,128]{2,1,0:T(8,128)(2,1)S(1)} async-done(((bf16[64,128,128]{2,1,0:T(8,128)(2,1)}), bf16[64,128,128]{2,1,0:T(8,128)(2,1)S(1)}, u32[]{:S(2)}, u32[]{:S(2)}) %all-to-all-start.2) | async-done | bytes 2097184 | tf_op jit(solution)/shard_map/all_to_all | solution.py:439
  82.3 4.7 %conditional.1 = (bf16[136,512]{1,0:T(8,128)(2,1)}, bf16[136,512]{1,0:T(8,128)(2,1)}, bf16[136,512]{1,0:T(8,128)(2,1)}, bf16[136,512]{1,0:T(8,128)(2,1)}, bf16[1,1,512,512]{3,2,1,0:T(8,128)(2,1)}) conditional(s32[]{:T(128)} %convert_element_type.32, (bf16[64,128,128]{2,1,0:T(8,128)(2,1)}, s32[2]{0:T(128)S(1)}, s32[2,64]{1,0:T(2,128)S(1)}, ...), branch_computations={%region_6.7_spmd, %region_7.8_spmd} | conditional | bytes 4194344 | solution.py:477
  82.3 4.7 %place.3 = (bf16[512,512]{1,0:T(8,128)(2,1)}, bf16[136,512]{1,0:T(8,128)(2,1)}, bf16[136,512]{1,0:T(8,128)(2,1)}, bf16[136,512]{1,0:T(8,128)(2,1)}, bf16[136,512]{1,0:T(8,128)(2,1)}) custom-call(s32[2]{0:T(128)S(1)} %get-tuple-element.56.refs_0_, s32[2,64]{1,0:T(2,128)S(1)} %get-tuple-element.57.refs_1_, ...), custom_call_target="tpu_custom_call" | custom-call | tf_op jit(solution)/shard_map/cond/branch_1_fun/place/pallas_call | solution.py:303
  87.0 1.6 %collective-permute-start.9 = (bf16[136,512]{1,0:T(8,128)(2,1)}, bf16[136,512]{1,0:T(8,128)(2,1)S(1)}, u32[]{:S(2)}, u32[]{:S(2)}) collective-permute-start(bf16[136,512]{1,0:T(8,128)(2,1)} %get-tuple-element.121), channel_id=1, source_target_pairs={{0,1},{1,0},{2,3},{3,2},{4,5},{5,4},{6,7},{7,6},{8,9},{9,8},{10,11... | collective-permute-start | bytes 417800 | tf_op jit(solution)/shard_map/ppermute | solution.py:219
  88.6 2.9 %collective-permute-start.10 = (bf16[136,512]{1,0:T(8,128)(2,1)}, bf16[136,512]{1,0:T(8,128)(2,1)S(1)}, u32[]{:S(2)}, u32[]{:S(2)}) collective-permute-start(bf16[136,512]{1,0:T(8,128)(2,1)} %get-tuple-element.122), channel_id=1, source_target_pairs={{0,2},{1,3},{2,0},{3,1},{4,6},{5,7},{6,4},{7,5},{8,10},{9,11},{10,... | collective-permute-start | bytes 417800 | tf_op jit(solution)/shard_map/ppermute | solution.py:219
  91.5 0.3 collective-permute-start.11
  91.8 0.1 copy.18.refs_5_
  91.9 1.6 %collective-permute-done.9.refs_1_ = bf16[136,512]{1,0:T(8,128)(2,1)S(1)} collective-permute-done((bf16[136,512]{1,0:T(8,128)(2,1)}, bf16[136,512]{1,0:T(8,128)(2,1)S(1)}, u32[]{:S(2)}, u32[]{:S(2)}) %collective-permute-start.9) | collective-permute-done | bytes 139296 | tf_op jit(solution)/shard_map/ppermute | solution.py:219
  93.5 4.8 %collective-permute-done.10.refs_2_ = bf16[136,512]{1,0:T(8,128)(2,1)S(1)} collective-permute-done((bf16[136,512]{1,0:T(8,128)(2,1)}, bf16[136,512]{1,0:T(8,128)(2,1)S(1)}, u32[]{:S(2)}, u32[]{:S(2)}) %collective-permute-start.10) | collective-permute-done | bytes 139296 | tf_op jit(solution)/shard_map/ppermute | solution.py:219
  98.2 2.2 %collective-permute-done.11.refs_3_ = bf16[136,512]{1,0:T(8,128)(2,1)S(1)} collective-permute-done((bf16[136,512]{1,0:T(8,128)(2,1)}, bf16[136,512]{1,0:T(8,128)(2,1)S(1)}, u32[]{:S(2)}, u32[]{:S(2)}) %collective-permute-start.11) | collective-permute-done | bytes 139296 | tf_op jit(solution)/shard_map/ppermute | solution.py:219
  100.4 4.9 %detect.1 = bf16[64,128,512]{2,1,0:T(8,128)(2,1)} custom-call(bf16[136,512]{1,0:T(8,128)(2,1)} %get-tuple-element.120.refs_0_, bf16[136,512]{1,0:T(8,128)(2,1)S(1)} %collective-permute-done.9.refs_1_, bf16[136,512]{1,0:T(8,128)(2,1)S(1)} %collective-permute-done.10.refs_2_, bf16[136,512]{1,0:T(8,128)(2,1)S(1)} %collective-permute-done.11.refs_3_, ...), custom_call_target="tpu_custom_call" | custom-call | tf_op jit(solution)/shard_map/detect/pallas_call | solution.py:375
  (19 shorter events, 0.2 us)
Async XLA Ops:
  0.6 40.3 %copy-start = (bf16[64,100]{1,0:T(8,128)(2,1)S(1)}, bf16[64,100]{1,0:T(8,128)(2,1)}, u32[]{:S(2)}) copy-start(bf16[64,100]{1,0:T(8,128)(2,1)} %param.18) | copy-start | bytes 38404
  5.9 19.1 %all-to-all-start.1 = ((bf16[8,128,128]{2,1,0:T(8,128)(2,1)}), bf16[8,128,128]{2,1,0:T(8,128)(2,1)}, u32[]{:S(2)}, u32[]{:S(2)}) async-start(bf16[8,128,128]{2,1,0:T(8,128)(2,1)} %repeat.1), calls=%async_computation.1 | async-start | bytes 524288 | tf_op jit(solution)/shard_map/all_to_all | solution.py:430
  25.0 12.0 %copy-start.2 = (s32[1,2048,1]{1,2,0:T(1,128)S(1)}, s32[1,2048,1]{1,2,0:T(1,128)}, u32[]{:S(2)}) copy-start(s32[1,2048,1]{1,2,0:T(1,128)} %param.15) | copy-start | bytes 24580
  25.0 15.7 %copy-start.1 = (s32[1,2048,2]{1,2,0:T(2,128)S(1)}, s32[1,2048,2]{1,2,0:T(2,128)}, u32[]{:S(2)}) copy-start(s32[1,2048,2]{1,2,0:T(2,128)} %param.16) | copy-start | bytes 49156
  25.0 16.8 %copy-start.3 = (f32[1,2048]{1,0:T(1,128)S(1)}, f32[1,2048]{1,0:T(1,128)}, u32[]{:S(2)}) copy-start(f32[1,2048]{1,0:T(1,128)} %refs_3_.3) | copy-start | bytes 24580
  25.0 38.1 %copy-start.4 = (f32[64]{0:T(128)S(1)}, f32[64]{0:T(128)}, u32[]{:S(2)}) copy-start(f32[64]{0:T(128)} %param.19) | copy-start | bytes 772
  25.0 57.3 %all-to-all-start.2 = ((bf16[64,128,128]{2,1,0:T(8,128)(2,1)}), bf16[64,128,128]{2,1,0:T(8,128)(2,1)S(1)}, u32[]{:S(2)}, u32[]{:S(2)}) async-start(bf16[64,128,128]{2,1,0:T(8,128)(2,1)} %get-tuple-element.99), calls=%async_computation.2 | async-start | bytes 4194304 | tf_op jit(solution)/shard_map/all_to_all | solution.py:439
  32.1 39.0 %collective-permute-start.3 = (bf16[8,128,128]{2,1,0:T(8,128)(2,1)}, bf16[8,128,128]{2,1,0:T(8,128)(2,1)}, u32[]{:S(2)}, u32[]{:S(2)}) collective-permute-start(bf16[8,128,128]{2,1,0:T(8,128)(2,1)} %all-to-all-done.1), channel_id=1, source_target_pairs={{0,4},{4,0},{8,12},{12,8},{16,20},{20,16},{24,28},{28,24},{32,36},... | collective-permute-start | bytes 786440 | tf_op jit(solution)/shard_map/ppermute | solution.py:219
  32.4 29.9 %collective-permute-start.2 = (bf16[8,128,128]{2,1,0:T(8,128)(2,1)}, bf16[8,128,128]{2,1,0:T(8,128)(2,1)}, u32[]{:S(2)}, u32[]{:S(2)}) collective-permute-start(bf16[8,128,128]{2,1,0:T(8,128)(2,1)} %all-to-all-done.1), channel_id=1, source_target_pairs={{0,24},{4,28},{8,16},{12,20},{16,8},{20,12},{24,0},{28,4},{32,56},... | collective-permute-start | bytes 786440 | tf_op jit(solution)/shard_map/ppermute | solution.py:219
  35.1 27.2 %collective-permute-start.1 = (bf16[8,128,128]{2,1,0:T(8,128)(2,1)}, bf16[8,128,128]{2,1,0:T(8,128)(2,1)}, u32[]{:S(2)}, u32[]{:S(2)}) collective-permute-start(bf16[8,128,128]{2,1,0:T(8,128)(2,1)} %all-to-all-done.1), channel_id=1, source_target_pairs={{0,16},{4,20},{8,24},{12,28},{16,0},{20,4},{24,8},{28,12},{32,48},... | collective-permute-start | bytes 786440 | tf_op jit(solution)/shard_map/ppermute | solution.py:219
  35.9 26.8 %collective-permute-start = (bf16[8,128,128]{2,1,0:T(8,128)(2,1)}, bf16[8,128,128]{2,1,0:T(8,128)(2,1)}, u32[]{:S(2)}, u32[]{:S(2)}) collective-permute-start(bf16[8,128,128]{2,1,0:T(8,128)(2,1)} %all-to-all-done.1), channel_id=1, source_target_pairs={{0,8},{4,12},{8,0},{12,4},{16,24},{20,28},{24,16},{28,20},{32,40},... | collective-permute-start | bytes 786440 | tf_op jit(solution)/shard_map/ppermute | solution.py:219
  39.1 25.0 %collective-permute-start.7 = (f32[]{:T(128)}, f32[]{:T(128)}, u32[]{:S(2)}, u32[]{:S(2)}) collective-permute-start(f32[]{:T(128)} %reduce_max.9), channel_id=1, source_target_pairs={{0,1},{1,0},{2,3},{3,2},{4,5},{5,4},{6,7},{7,6},{8,9},{9,8},{10,11... | collective-permute-start | bytes 20 | tf_op jit(solution)/shard_map/ppermute | solution.py:219
  62.2 8.9 %collective-permute-start.6 = (bf16[8,128,128]{2,1,0:T(8,128)(2,1)}, bf16[8,128,128]{2,1,0:T(8,128)(2,1)}, u32[]{:S(2)}, u32[]{:S(2)}) collective-permute-start(bf16[8,128,128]{2,1,0:T(8,128)(2,1)} %collective-permute-done.2), channel_id=1, source_target_pairs={{0,4},{4,0},{8,12},{12,8},{16,20},{20,16},{24,28},{28,24},{32,36},... | collective-permute-start | bytes 786440 | tf_op jit(solution)/shard_map/ppermute | solution.py:219
  62.2 8.9 %collective-permute-start.5 = (bf16[8,128,128]{2,1,0:T(8,128)(2,1)}, bf16[8,128,128]{2,1,0:T(8,128)(2,1)}, u32[]{:S(2)}, u32[]{:S(2)}) collective-permute-start(bf16[8,128,128]{2,1,0:T(8,128)(2,1)} %collective-permute-done.1), channel_id=1, source_target_pairs={{0,4},{4,0},{8,12},{12,8},{16,20},{20,16},{24,28},{28,24},{32,36},... | collective-permute-start | bytes 786440 | tf_op jit(solution)/shard_map/ppermute | solution.py:219
  62.8 8.4 %collective-permute-start.4 = (bf16[8,128,128]{2,1,0:T(8,128)(2,1)}, bf16[8,128,128]{2,1,0:T(8,128)(2,1)}, u32[]{:S(2)}, u32[]{:S(2)}) collective-permute-start(bf16[8,128,128]{2,1,0:T(8,128)(2,1)} %collective-permute-done), channel_id=1, source_target_pairs={{0,4},{4,0},{8,12},{12,8},{16,20},{20,16},{24,28},{28,24},{32,36},... | collective-permute-start | bytes 786440 | tf_op jit(solution)/shard_map/ppermute | solution.py:219
  65.4 5.1 %collective-permute-start.8 = (f32[]{:T(128)}, f32[]{:T(128)}, u32[]{:S(2)}, u32[]{:S(2)}) collective-permute-start(f32[]{:T(128)} %max.26), channel_id=1, source_target_pairs={{0,2},{1,3},{2,0},{3,1},{4,6},{5,7},{6,4},{7,5},{8,10},{9,11},{10,... | collective-permute-start | bytes 20 | tf_op jit(solution)/shard_map/ppermute | solution.py:219
  87.0 6.5 %collective-permute-start.9 = (bf16[136,512]{1,0:T(8,128)(2,1)}, bf16[136,512]{1,0:T(8,128)(2,1)S(1)}, u32[]{:S(2)}, u32[]{:S(2)}) collective-permute-start(bf16[136,512]{1,0:T(8,128)(2,1)} %get-tuple-element.121), channel_id=1, source_target_pairs={{0,1},{1,0},{2,3},{3,2},{4,5},{5,4},{6,7},{7,6},{8,9},{9,8},{10,11... | collective-permute-start | bytes 417800 | tf_op jit(solution)/shard_map/ppermute | solution.py:219
  88.6 9.6 %collective-permute-start.10 = (bf16[136,512]{1,0:T(8,128)(2,1)}, bf16[136,512]{1,0:T(8,128)(2,1)S(1)}, u32[]{:S(2)}, u32[]{:S(2)}) collective-permute-start(bf16[136,512]{1,0:T(8,128)(2,1)} %get-tuple-element.122), channel_id=1, source_target_pairs={{0,2},{1,3},{2,0},{3,1},{4,6},{5,7},{6,4},{7,5},{8,10},{9,11},{10,... | collective-permute-start | bytes 417800 | tf_op jit(solution)/shard_map/ppermute | solution.py:219
  91.5 8.9 %collective-permute-start.11 = (bf16[136,512]{1,0:T(8,128)(2,1)}, bf16[136,512]{1,0:T(8,128)(2,1)S(1)}, u32[]{:S(2)}, u32[]{:S(2)}) collective-permute-start(bf16[136,512]{1,0:T(8,128)(2,1)} %get-tuple-element.123), channel_id=1, source_target_pairs={{0,3},{1,2},{2,1},{3,0},{4,7},{5,6},{6,5},{7,4},{8,11},{9,10},{10,... | collective-permute-start | bytes 417800 | tf_op jit(solution)/shard_map/ppermute | solution.py:219
